TPU v7x, 128 devices: a whole 4x4x4 slice. The times are simulated.
128 devices in a mesh: fsdp: 16 (over y_lo, z, core), chan: 8 (over y_hi, x).
Axes of the slice: x: 4, y: 4 (y_hi: 2, y_lo: 2; y = y_hi * 2 + y_lo), z: 4, core: 2. Of those that a mesh axis runs over, the one named last changes fastest.
Arguments:
- in_master: float32 [4096, 2, 4096], P(('fsdp', 'chan')), may hold values from -0.09375 to 0.09375
- in_moment: float32 [4096, 2, 4096], P(('fsdp', 'chan')), may hold values from -1.8 to 1.8
- in_velocity: float32 [4096, 2, 4096], P(('fsdp', 'chan')), may hold values from 0.05 to 1
- in_grad: bfloat16 [4096, 2, 4096], P(('fsdp', 'chan')), may hold values from -6 to 6
- out_master: float32 [4096, 4096], P(('fsdp', 'chan')), may hold values from -0.09375 to 0.09375
- out_moment: float32 [4096, 4096], P(('fsdp', 'chan')), may hold values from -1.8 to 1.8
- out_velocity: float32 [4096, 4096], P(('fsdp', 'chan')), may hold values from 0.001 to 1
- out_grad: bfloat16 [4096, 4096], P(('fsdp', 'chan')), may hold values from -6 to 6
- embed_table: bfloat16 [65536, 4096], P('fsdp', 'chan'), may hold values from -18 to 18
- tokens: int32 [4, 2048], P(None, 'fsdp'), may hold values from 0 to 65535, as said below
- conv_state: bfloat16 [2048, 3, 4096], P('fsdp', None, 'chan'), may hold values from -6 to 6
- ssm_state: float32 [2048, 16, 4096], P('fsdp', None, 'chan'), may hold values from -6 to 6
- conv_weight: float32 [4, 4096], P(None, 'chan'), may hold values from -3 to 3
- conv_bias: float32 [4096], P('chan'), may hold values from -3 to 3
- x_proj_w: bfloat16 [288, 4096], P(None, 'chan'), may hold values from -0.09375 to 0.09375
- dt_proj_w: bfloat16 [4096, 256], P('chan'), may hold values from -0.375 to 0.375
- dt_bias: float32 [4096], P('chan'), may hold values from -4.5 to -2
- a_log: float32 [16, 4096], P(None, 'chan'), may hold values from 0 to 2.77
- d_skip: float32 [4096], P('chan'), may hold values from 0.5 to 2
Outputs:
- in_master_new: float32 [4096, 2, 4096], P(('fsdp', 'chan'))
- out_master_new: float32 [4096, 4096], P(('fsdp', 'chan'))
- block_out: bfloat16 [4, 2048, 4096], P(None, 'fsdp', 'chan')
- conv_state_new: bfloat16 [2048, 3, 4096], P('fsdp', None, 'chan')
- ssm_state_new: float32 [2048, 16, 4096], P('fsdp', None, 'chan')
Inputs may be any that keep to these rules, and one draw needn't show every extreme that they name: Split the ids into 16 equal consecutive vocabulary blocks and the sequences into 16 equal consecutive replicas; of one replica's 4 x 128 tokens at most 64 lie in any one block, and some block holds exactly 64 of them.
All inputs are finite; a program needn't handle non-finite values.
Results may differ from a plain program's by a relative error of at most 0.012.
Values may be sent and summed in bfloat16 or wider, within the bound.
No kernel may reach another device: no remote copies, remote signals or barrier semaphores. Data moves between devices by JAX's collectives and lax.ppermute only.
A program may use at most 128 MiB of HBM per device.

v0:
```python
import math

import jax
import jax.numpy as jnp
from jax import lax
from jax.sharding import PartitionSpec as P

RANK = 256
NSTATE = 16


learn_rate = 0.01
beta_first = 0.8
beta_second = 0.95
adam_eps = 1e-08
weight_decay = 0.1
bias_first = 1.0 - math.pow(0.8, 10)
bias_second = 1.0 - math.pow(0.95, 10)
norm_eps = 1e-06


def sent_to_all(x, axis):
    length = lax.axis_size(axis)
    return lax.all_to_all(jnp.broadcast_to(x[None], (length, *x.shape)), axis, 0, 0, tiled=True)


def of_everyone(x, axis):
    return sent_to_all(x, axis).sum(axis=0)


def cut_along(x, dim, length):
    before, after = (x.shape[:dim], x.shape[dim + 1 :])
    return jnp.moveaxis(x.reshape(*before, length, -1, *after), dim, 0)


def sum_at_owner(x, axis, dim):
    blocks = cut_along(x, dim, lax.axis_size(axis))
    arrived = lax.all_to_all(blocks, axis, split_axis=0, concat_axis=0, tiled=True)
    return arrived.astype(jnp.float32).sum(axis=0)


def adam_update(master, moment, velocity, grad):
    gradient = grad.astype(jnp.float32)
    moment = beta_first * moment + (1.0 - beta_first) * gradient
    velocity = beta_second * velocity + (1.0 - beta_second) * gradient * gradient
    update = moment / bias_first / (jnp.sqrt(velocity / bias_second) + adam_eps)
    return master - learn_rate * (update + weight_decay * master)


def per_device(
    in_master,
    in_moment,
    in_velocity,
    in_grad,
    out_master,
    out_moment,
    out_velocity,
    out_grad,
    embed_table,
    tokens,
    conv_state,
    ssm_state,
    conv_weight,
    conv_bias,
    x_proj_w,
    dt_proj_w,
    dt_bias,
    a_log,
    d_skip,
):
    in_new = adam_update(in_master, in_moment, in_velocity, in_grad)
    out_new = adam_update(out_master, out_moment, out_velocity, out_grad)
    pieces = (
        in_new[:, 0, :].astype(jnp.bfloat16),
        in_new[:, 1, :].astype(jnp.bfloat16),
        out_new.astype(jnp.bfloat16),
    )
    replicas = lax.axis_size("fsdp")
    spread = (
        lax.all_to_all(pieces[0], "chan", split_axis=1, concat_axis=0, tiled=True),
        lax.all_to_all(pieces[1], "chan", split_axis=1, concat_axis=0, tiled=True),
        lax.all_to_all(pieces[2], "chan", split_axis=1, concat_axis=0, tiled=True),
    )
    relay_x, relay_z, relay_out = (
        lax.all_gather(spread[0], "fsdp", axis=0, tiled=True),
        lax.all_gather(spread[1], "fsdp", axis=0, tiled=True),
        lax.all_gather(spread[2], "fsdp", axis=0, tiled=True),
    )
    vocab_rows = embed_table.shape[0]
    feature_part = embed_table.shape[1]
    own_steps, own_rows = tokens.shape
    count = own_steps * own_rows
    capacity = 2 * count // replicas
    flat_tokens = tokens.reshape(count)
    owner = flat_tokens // vocab_rows
    holders = jnp.arange(replicas, dtype=jnp.int32)
    one_hot = (owner[:, None] == holders[None, :]).astype(jnp.int32)
    earlier = jnp.cumsum(one_hot, axis=0) - one_hot
    slot = jnp.sum(earlier * one_hot, axis=1)
    place = owner * capacity + slot
    requests = jnp.full((replicas * capacity,), -1, jnp.int32).at[place].set(flat_tokens)
    asked = lax.all_to_all(
        requests.reshape(replicas, capacity), "fsdp", split_axis=0, concat_axis=0, tiled=True
    )
    offset = asked - lax.axis_index("fsdp") * vocab_rows
    inside = jnp.logical_and(asked >= 0, jnp.logical_and(offset >= 0, offset < vocab_rows))
    looked = jnp.take(embed_table, jnp.clip(offset, 0, vocab_rows - 1).reshape(-1), axis=0)
    looked = looked.reshape(replicas, capacity, feature_part)
    looked = jnp.where(inside[:, :, None], looked, jnp.zeros((), jnp.bfloat16))
    replies = lax.all_to_all(looked, "fsdp", split_axis=0, concat_axis=0, tiled=True)
    found = jnp.take(replies.reshape(replicas * capacity, feature_part), place, axis=0)
    found = found.reshape(own_steps, own_rows, feature_part)
    inputs = lax.all_gather(found, "chan", axis=2, tiled=True)
    steps, rows, width = inputs.shape
    flat = inputs.reshape(steps * rows, width).astype(jnp.float32)
    normed = (flat * lax.rsqrt(jnp.mean(flat * flat, axis=1, keepdims=True) + norm_eps)).astype(
        jnp.bfloat16
    )
    x_in = (
        jnp.dot(normed, relay_x, preferred_element_type=jnp.float32)
        .astype(jnp.bfloat16)
        .reshape(steps, rows, -1)
    )
    z_in = (
        jnp.dot(normed, relay_z, preferred_element_type=jnp.float32)
        .astype(jnp.bfloat16)
        .reshape(steps, rows, -1)
    )
    decay = -jnp.exp(a_log)
    contract_last = (((1,), (1,)), ((), ()))
    window_state = conv_state
    state = ssm_state
    gates = []
    for step in range(steps):
        window = jnp.concatenate([window_state, x_in[step][:, None, :]], axis=1)
        mixed_conv = jnp.sum(window.astype(jnp.float32) * conv_weight[None], axis=1) + conv_bias
        act = jax.nn.silu(mixed_conv).astype(jnp.bfloat16)
        partial_value = lax.dot_general(
            act, x_proj_w, contract_last, preferred_element_type=jnp.float32
        )
        dbc = of_everyone(partial_value, "chan")
        dt_low = dbc[:, :RANK].astype(jnp.bfloat16)
        b_mat = dbc[:, RANK : RANK + NSTATE]
        c_mat = dbc[:, RANK + NSTATE :]
        delta = jax.nn.softplus(
            lax.dot_general(dt_low, dt_proj_w, contract_last, preferred_element_type=jnp.float32)
            + dt_bias
        )
        act_real = act.astype(jnp.float32)
        state = (
            jnp.exp(delta[:, None, :] * decay[None]) * state
            + (delta * act_real)[:, None, :] * b_mat[:, :, None]
        )
        y_out = jnp.sum(c_mat[:, :, None] * state, axis=1) + d_skip * act_real
        gated = (y_out * jax.nn.silu(z_in[step].astype(jnp.float32))).astype(jnp.bfloat16)
        gates.append(gated)
        window_state = window[:, 1:, :]
    stacked_gates = jnp.stack(gates)
    terms = lax.dot_general(
        stacked_gates, relay_out, (((2,), (1,)), ((), ())), preferred_element_type=jnp.float32
    )
    mixed_all = sum_at_owner(terms.astype(jnp.bfloat16), "chan", 2)
    block_out = (found.astype(jnp.float32) + mixed_all).astype(jnp.bfloat16)
    return (in_new, out_new, block_out, window_state, state)


def solution(mesh):
    placed = (
        P(("fsdp", "chan"), None, None),
        P(("fsdp", "chan"), None, None),
        P(("fsdp", "chan"), None, None),
        P(("fsdp", "chan"), None, None),
        P(("fsdp", "chan"), None),
        P(("fsdp", "chan"), None),
        P(("fsdp", "chan"), None),
        P(("fsdp", "chan"), None),
        P("fsdp", "chan"),
        P(None, "fsdp"),
        P("fsdp", None, "chan"),
        P("fsdp", None, "chan"),
        P(None, "chan"),
        P("chan"),
        P(None, "chan"),
        P("chan", None),
        P("chan"),
        P(None, "chan"),
        P("chan"),
    )
    return jax.shard_map(
        per_device,
        mesh=mesh,
        in_specs=placed,
        out_specs=(
            P(("fsdp", "chan"), None, None),
            P(("fsdp", "chan"), None),
            P(None, "fsdp", "chan"),
            P("fsdp", None, "chan"),
            P("fsdp", None, "chan"),
        ),
        check_vma=False,
    )
```

profile of v0, /device:TPU:6, one launch (start us, length us, event | category | flops | bytes accessed | tf_op | source)
XLA Modules:
  0.0 386.3 jit_solution(11892223950714199581)
XLA Ops:
  7.2 0.7 add_select_fusion
  7.9 0.7 add_select_fusion.1
  8.6 1.2 reduce-window.6
  9.8 0.2 slice_reduce_fusion.2
  10.1 0.7 compare_select_fusion.6
  10.8 2.6 scatter_custom_fusion
  13.4 0.7 all_to_all.62
  14.1 6.4 %all-to-all-start = ((s32[16,1,64]{2,1,0:T(1,128)}), s32[16,1,64]{2,1,0:T(1,128)S(1)}, u32[]{:S(2)}, u32[]{:S(2)}) async-start(s32[16,1,64]{2,1,0:T(1,128)} %all_to_all.62), calls=%async_computation | async-start | bytes 16384 | tf_op jit(solution)/shard_map/all_to_all | solution.py:102
  20.6 6.0 %all-to-all-done = s32[16,1,64]{2,1,0:T(1,128)S(1)} async-done(((s32[16,1,64]{2,1,0:T(1,128)}), s32[16,1,64]{2,1,0:T(1,128)S(1)}, u32[]{:S(2)}, u32[]{:S(2)}) %all-to-all-start) | async-done | bytes 4128 | tf_op jit(solution)/shard_map/all_to_all | solution.py:102
  26.7 6.7 %gather_fusion = bf16[1024,512]{1,0:T(8,128)(2,1)S(1)} fusion(bf16[4096,512]{1,0:T(8,128)(2,1)} %param.27, s32[1024]{0:T(1024)S(1)} %broadcast_clamp_fusion), kind=kCustom, calls=%fused_computation | custom fusion | bytes 2101248 | tf_op jit(solution)/shard_map/jit(_take)/gather | solution.py:107
  33.4 1.2 select_select_fusion
  34.6 3.8 all-to-all-start.1
  38.5 16.5 %all-to-all-done.1 = bf16[16,64,512]{2,1,0:T(8,128)(2,1)S(1)} async-done(((bf16[16,64,512]{2,1,0:T(8,128)(2,1)}), bf16[16,64,512]{2,1,0:T(8,128)(2,1)S(1)}, u32[]{:S(2)}, u32[]{:S(2)}) %all-to-all-start.1) | async-done | bytes 1048608 | tf_op jit(solution)/shard_map/all_to_all | solution.py:110
  55.0 2.0 gather_fusion.1
  57.0 0.9 broadcast_select_fusion
  58.0 5.5 %fusion.68 = (bf16[32,2,4096]{2,1,0:T(2,128)(2,1)S(1)}, f32[32,2,4096]{2,1,0:T(2,128)}) fusion(f32[32,2,4096]{2,1,0:T(2,128)S(1)} %copy-done.6, f32[32,2,4096]{2,1,0:T(2,128)} %param.21, bf16[32,2,4096]{2,1,0:T(2,128)(2,1)S(1)} %copy-done.7, f32[32,2,4096]{2,1,0:T(2,128)} %param.20), kind=kLoop, calls=%fused_computation.183 | loop fusion | flops 4456448 | bytes 5242880 | tf_op jit(solution)/shard_map/convert.6
  63.5 2.3 slice_reduce_fusion.1
  65.8 15.4 %all_to_all.90 = bf16[32,8,512]{2,0,1:T(8,128)(2,1)} all-to-all(bf16[32,8,512]{2,0,1:T(8,128)(2,1)S(1)} %bitcast.124), channel_id=1, replica_groups=mesh['fsdp'=16,'chan'=8] {'chan'}, dimensions={1} | all-to-all | bytes 524288 | tf_op jit(solution)/shard_map/all_to_all | solution.py:80
  81.3 12.1 %all_to_all.91 = bf16[32,8,512]{2,0,1:T(8,128)(2,1)} all-to-all(bf16[32,8,512]{2,0,1:T(8,128)(2,1)S(1)} %bitcast.125), channel_id=1, replica_groups=mesh['fsdp'=16,'chan'=8] {'chan'}, dimensions={1} | all-to-all | bytes 524288 | tf_op jit(solution)/shard_map/all_to_all | solution.py:81
  93.5 2.4 fusion.69
  95.9 13.8 %all_to_all.92 = bf16[32,8,512]{2,0,1:T(8,128)(2,1)} all-to-all(bf16[32,8,512]{2,0,1:T(8,128)(2,1)S(1)} %bitcast.126), channel_id=1, replica_groups=mesh['fsdp'=16,'chan'=8] {'chan'}, dimensions={1} | all-to-all | bytes 524288 | tf_op jit(solution)/shard_map/all_to_all | solution.py:82
  109.8 32.8 %all-gather.5.cloned.1.call-done = bf16[4,128,4096]{2,1,0:T(8,128)(2,1)} async-done(((bf16[4,128,512]{2,1,0:T(8,128)(2,1)}), bf16[4,128,4096]{2,1,0:T(8,128)(2,1)}) %all-gather.5.cloned.1.call-update) | async-done | bytes 4194320 | tf_op jit(solution)/shard_map/all_gather | solution.py:113
  142.5 3.2 multiply_reduce_fusion
  145.8 0.2 copy-done.2
  146.0 3.4 fusion
  149.4 31.2 %all-gather.7.cloned.1.call-done = bf16[4096,512]{1,0:T(8,128)(2,1)} async-done(((bf16[256,512]{1,0:T(8,128)(2,1)}), bf16[4096,512]{1,0:T(8,128)(2,1)}) %all-gather.7.cloned.1.call-update) | async-done | bytes 4194320 | tf_op jit(solution)/shard_map/all_gather | solution.py:85
  180.6 5.8 %convolution_convert_fusion.2 = bf16[512,512]{1,0:T(8,128)(2,1)S(1)} fusion(bf16[512,4096]{1,0:T(8,128)(2,1)} %fusion, bf16[4096,512]{1,0:T(8,128)(2,1)} %all-gather.7.cloned.1.call-done), kind=kOutput, calls=%fused_computation.21 | convolution fusion | flops 2147745792 | bytes 8912896 | tf_op jit(solution)/shard_map/dot_general | solution.py:120
  186.6 0.4 multiply_reduce_fusion.8
  187.1 0.3 multiply_convert_fusion.3
  187.4 0.2 fusion.78
  187.6 1.2 broadcast_in_dim.52
  188.8 7.1 %all-to-all-start.7 = ((f32[8,128,288]{1,2,0:T(8,128)}), f32[8,128,288]{1,2,0:T(8,128)S(1)}, u32[]{:S(2)}, u32[]{:S(2)}) async-start(f32[8,128,288]{1,2,0:T(8,128)} %broadcast_in_dim.52), calls=%async_computation.7 | async-start | bytes 2359296 | tf_op jit(solution)/shard_map/all_to_all | solution.py:24
  195.9 0.2 fusion.77
  196.1 19.1 %all-to-all-done.7 = f32[8,128,288]{1,2,0:T(8,128)S(1)} async-done(((f32[8,128,288]{1,2,0:T(8,128)}), f32[8,128,288]{1,2,0:T(8,128)S(1)}, u32[]{:S(2)}, u32[]{:S(2)}) %all-to-all-start.7) | async-done | bytes 1179680 | tf_op jit(solution)/shard_map/all_to_all | solution.py:24
  215.2 1.1 broadcast_in_dim.51
  216.3 5.2 %all-to-all-start.6 = ((f32[8,128,288]{1,2,0:T(8,128)}), f32[8,128,288]{1,2,0:T(8,128)}, u32[]{:S(2)}, u32[]{:S(2)}) async-start(f32[8,128,288]{1,2,0:T(8,128)} %broadcast_in_dim.51), calls=%async_computation.6 | async-start | bytes 2359296 | tf_op jit(solution)/shard_map/all_to_all | solution.py:24
  221.5 0.2 fusion.76
  221.7 18.6 %all-to-all-done.6 = f32[8,128,288]{1,2,0:T(8,128)} async-done(((f32[8,128,288]{1,2,0:T(8,128)}), f32[8,128,288]{1,2,0:T(8,128)}, u32[]{:S(2)}, u32[]{:S(2)}) %all-to-all-start.6) | async-done | bytes 1179680 | tf_op jit(solution)/shard_map/all_to_all | solution.py:24
  240.3 1.1 broadcast_in_dim.50
  241.4 4.9 %all-to-all-start.5 = ((f32[8,128,288]{1,2,0:T(8,128)}), f32[8,128,288]{1,2,0:T(8,128)}, u32[]{:S(2)}, u32[]{:S(2)}) async-start(f32[8,128,288]{1,2,0:T(8,128)} %broadcast_in_dim.50), calls=%async_computation.5 | async-start | bytes 2359296 | tf_op jit(solution)/shard_map/all_to_all | solution.py:24
  246.3 0.2 fusion.75
  246.6 16.5 %all-to-all-done.5 = f32[8,128,288]{1,2,0:T(8,128)} async-done(((f32[8,128,288]{1,2,0:T(8,128)}), f32[8,128,288]{1,2,0:T(8,128)}, u32[]{:S(2)}, u32[]{:S(2)}) %all-to-all-start.5) | async-done | bytes 1179680 | tf_op jit(solution)/shard_map/all_to_all | solution.py:24
  263.1 1.1 broadcast_in_dim.49
  264.2 7.0 %all-to-all-start.3 = ((f32[8,128,288]{1,2,0:T(8,128)}), f32[8,128,288]{1,2,0:T(8,128)}, u32[]{:S(2)}, u32[]{:S(2)}) async-start(f32[8,128,288]{1,2,0:T(8,128)} %broadcast_in_dim.49), calls=%async_computation.3 | async-start | bytes 2359296 | tf_op jit(solution)/shard_map/all_to_all | solution.py:24
  271.2 6.7 %convolution_convert_fusion.1 = bf16[512,512]{1,0:T(8,128)(2,1)} fusion(bf16[512,4096]{1,0:T(8,128)(2,1)} %fusion, bf16[4096,512]{1,0:T(8,128)(2,1)} %all-gather.9.cloned.1.call-done), kind=kOutput, calls=%fused_computation.20 | convolution fusion | flops 2147745792 | bytes 8912896 | tf_op jit(solution)/shard_map/dot_general | solution.py:125
  278.2 1.3 reduce_sum.150
  279.7 1.3 reduce_sum.147
  281.3 9.1 %all-to-all-done.3 = f32[8,128,288]{1,2,0:T(8,128)} async-done(((f32[8,128,288]{1,2,0:T(8,128)}), f32[8,128,288]{1,2,0:T(8,128)}, u32[]{:S(2)}, u32[]{:S(2)}) %all-to-all-start.3) | async-done | bytes 1179680 | tf_op jit(solution)/shard_map/all_to_all | solution.py:24
  290.4 1.4 reduce_sum.144
  291.9 0.7 copy.54
  292.6 0.4 convert_multiply_fusion.4
  293.0 0.4 convert_multiply_fusion.7
  293.3 0.4 convert_multiply_fusion.10
  293.7 0.4 convert_multiply_fusion.13
  294.1 0.8 copy-done.3
  294.8 8.7 %multiply_reduce_fusion.3 = (f32[128,512]{1,0:T(8,128)S(1)}, f32[128,512]{1,0:T(8,128)S(1)}, f32[128,512]{1,0:T(8,128)S(1)}, f32[128,512]{1,0:T(8,128)S(1)}, f32[128,16,512]{2,1,0:T(8,128)}) fusion(f32[128,16]{1,0:T(8,128)S(1)} %copy.56, f32[128,16]{1,0:T(8,128)S(1)} %copy.57, f32[128,512]{1,0:T(8,128)S(1)} %get-tuple-element.44, f32[128,16]{1,0:T(8,128)} %copy.54, ...), kind=kLoop, calls=%fused_computation.14 | loop fusion | flops 24903680 | bytes 11632640 | tf_op jit(solution)/shard_map/reduce_sum | solution.py:154
  303.6 0.4 fusion.56
  304.0 4.6 %convolution_convert_fusion = bf16[4,128,4096]{2,1,0:T(8,128)(2,1)S(1)} fusion(bf16[4096,512]{1,0:T(8,128)(2,1)} %all-gather.11.cloned.1.call-done, bf16[1,128,512]{2,1,0:T(8,128)(2,1)S(1)} %get-tuple-element.25, bf16[1,128,512]{2,1,0:T(8,128)(2,1)S(1)} %get-tuple-element.26, bf16[1,128,512]{2,1,0:T(8,128)(2,1)S(1)} %get-tuple-element.27, ...), kind=kOutput, calls=%fused_computation.7 | convolution fusion | flops 2150367232 | bytes 8912896 | tf_op jit(solution)/shard_map/dot_general | solution.py:159
  308.6 2.4 copy.74
  311.0 5.3 %all-to-all-start.9 = ((bf16[8,4,128,512]{3,2,1,0:T(8,128)(2,1)}), bf16[8,4,128,512]{3,2,1,0:T(8,128)(2,1)}, u32[]{:S(2)}, u32[]{:S(2)}) async-start(bf16[8,4,128,512]{3,2,1,0:T(8,128)(2,1)} %bitcast.115), calls=%async_computation.9 | async-start | bytes 8388608 | tf_op jit(solution)/shard_map/all_to_all | solution.py:38
  316.3 0.8 fusion.25
  317.1 58.8 %all-to-all-done.9 = bf16[8,4,128,512]{3,2,1,0:T(8,128)(2,1)} async-done(((bf16[8,4,128,512]{3,2,1,0:T(8,128)(2,1)}), bf16[8,4,128,512]{3,2,1,0:T(8,128)(2,1)}, u32[]{:S(2)}, u32[]{:S(2)}) %all-to-all-start.9) | async-done | bytes 4194336 | tf_op jit(solution)/shard_map/all_to_all | solution.py:38
  375.8 2.9 convert_reduce_fusion
  378.8 1.0 add_convert_fusion
  (78 shorter events, 1.7 us)
Async XLA Ops:
  7.2 180.2 %copy-start = (bf16[288,512]{1,0:T(8,128)(2,1)S(1)}, bf16[288,512]{1,0:T(8,128)(2,1)}, u32[]{:S(2)}) copy-start(bf16[288,512]{1,0:T(8,128)(2,1)} %param.33) | copy-start | bytes 884740
  14.1 12.4 %all-to-all-start = ((s32[16,1,64]{2,1,0:T(1,128)}), s32[16,1,64]{2,1,0:T(1,128)S(1)}, u32[]{:S(2)}, u32[]{:S(2)}) async-start(s32[16,1,64]{2,1,0:T(1,128)} %all_to_all.62), calls=%async_computation | async-start | bytes 16384 | tf_op jit(solution)/shard_map/all_to_all | solution.py:102
  33.4 5.1 %copy-start.12 = (s32[4,128]{1,0:T(4,128)S(1)}, s32[4,128]{1,0:T(4,128)}, u32[]{:S(2)}) copy-start(s32[4,128]{1,0:T(4,128)} %param.28) | copy-start | bytes 6148
  34.6 23.4 %copy-start.6 = (f32[32,2,4096]{2,1,0:T(2,128)S(1)}, f32[32,2,4096]{2,1,0:T(2,128)}, u32[]{:S(2)}) copy-start(f32[32,2,4096]{2,1,0:T(2,128)} %param.19) | copy-start | bytes 3145732
  34.6 23.4 %copy-start.7 = (bf16[32,2,4096]{2,1,0:T(2,128)(2,1)S(1)}, bf16[32,2,4096]{2,1,0:T(2,128)(2,1)}, u32[]{:S(2)}) copy-start(bf16[32,2,4096]{2,1,0:T(2,128)(2,1)} %param.22) | copy-start | bytes 1572868
  34.6 20.4 %all-to-all-start.1 = ((bf16[16,64,512]{2,1,0:T(8,128)(2,1)}), bf16[16,64,512]{2,1,0:T(8,128)(2,1)S(1)}, u32[]{:S(2)}, u32[]{:S(2)}) async-start(bf16[16,64,512]{2,1,0:T(8,128)(2,1)} %select_select_fusion), calls=%async_computation.1 | async-start | bytes 2097152 | tf_op jit(solution)/shard_map/all_to_all | solution.py:110
  38.4 104.1 %all-gather.5.cloned.1.call-start = ((), (), s32[]{:S(2)}) async-start(), calls=%async_computation.10 | async-start | bytes 4718592 | tf_op jit(solution)/shard_map/all_gather | solution.py:113
  38.5 25.0 %copy-start.15 = (pred[4,128]{1,0:T(4,128)(4,1)}, pred[4,128]{1,0:T(4,128)(4,1)S(1)}, u32[]{:S(2)}) copy-start(pred[4,128]{1,0:T(4,128)(4,1)S(1)} %compare_and_fusion.1) | copy-start | bytes 1540
  57.9 35.5 %copy-start.8 = (f32[32,4096]{1,0:T(8,128)S(1)}, f32[32,4096]{1,0:T(8,128)}, u32[]{:S(2)}) copy-start(f32[32,4096]{1,0:T(8,128)} %param.23) | copy-start | bytes 1572868
  57.9 35.5 %copy-start.10 = (bf16[32,4096]{1,0:T(8,128)(2,1)S(1)}, bf16[32,4096]{1,0:T(8,128)(2,1)}, u32[]{:S(2)}) copy-start(bf16[32,4096]{1,0:T(8,128)(2,1)} %param.26) | copy-start | bytes 786436
  57.9 122.7 %all-gather.7.cloned.1.call-start = ((), (), s32[]{:S(2)}) async-start(), calls=%async_computation.11 | async-start | bytes 4456448 | tf_op jit(solution)/shard_map/all_gather | solution.py:85
  81.2 190.0 %all-gather.9.cloned.1.call-start = ((), (), s32[]{:S(2)}) async-start(), calls=%async_computation.12 | async-start | bytes 4456448 | tf_op jit(solution)/shard_map/all_gather | solution.py:86
  93.4 210.6 %all-gather.11.cloned.1.call-start = ((), (), s32[]{:S(2)}) async-start(), calls=%async_computation.13 | async-start | bytes 4456448 | tf_op jit(solution)/shard_map/all_gather | solution.py:87
  142.5 3.4 copy-start.2
  149.4 37.1 %copy-start.5 = (bf16[128,3,512]{2,0,1:T(8,128)(2,1)S(1)}, bf16[128,3,512]{2,0,1:T(8,128)(2,1)}, u32[]{:S(2)}) copy-start(bf16[128,3,512]{2,0,1:T(8,128)(2,1)} %param.29) | copy-start | bytes 1179652
  149.4 37.2 %copy-start.14 = (f32[4,512]{1,0:T(4,128)S(1)}, f32[4,512]{1,0:T(4,128)}, u32[]{:S(2)}) copy-start(f32[4,512]{1,0:T(4,128)} %param.31) | copy-start | bytes 24580
  186.4 0.7 copy-start.17
  188.8 26.4 %all-to-all-start.7 = ((f32[8,128,288]{1,2,0:T(8,128)}), f32[8,128,288]{1,2,0:T(8,128)S(1)}, u32[]{:S(2)}, u32[]{:S(2)}) async-start(f32[8,128,288]{1,2,0:T(8,128)} %broadcast_in_dim.52), calls=%async_computation.7 | async-start | bytes 2359296 | tf_op jit(solution)/shard_map/all_to_all | solution.py:24
  195.9 50.4 %copy-start.13 = (f32[16,512]{1,0:T(8,128)S(1)}, f32[16,512]{1,0:T(8,128)}, u32[]{:S(2)}) copy-start(f32[16,512]{1,0:T(8,128)} %param.36) | copy-start | bytes 98308
  216.3 24.0 %all-to-all-start.6 = ((f32[8,128,288]{1,2,0:T(8,128)}), f32[8,128,288]{1,2,0:T(8,128)}, u32[]{:S(2)}, u32[]{:S(2)}) async-start(f32[8,128,288]{1,2,0:T(8,128)} %broadcast_in_dim.51), calls=%async_computation.6 | async-start | bytes 2359296 | tf_op jit(solution)/shard_map/all_to_all | solution.py:24
  241.4 21.7 %all-to-all-start.5 = ((f32[8,128,288]{1,2,0:T(8,128)}), f32[8,128,288]{1,2,0:T(8,128)}, u32[]{:S(2)}, u32[]{:S(2)}) async-start(f32[8,128,288]{1,2,0:T(8,128)} %broadcast_in_dim.50), calls=%async_computation.5 | async-start | bytes 2359296 | tf_op jit(solution)/shard_map/all_to_all | solution.py:24
  264.2 26.2 %all-to-all-start.3 = ((f32[8,128,288]{1,2,0:T(8,128)}), f32[8,128,288]{1,2,0:T(8,128)}, u32[]{:S(2)}, u32[]{:S(2)}) async-start(f32[8,128,288]{1,2,0:T(8,128)} %broadcast_in_dim.49), calls=%async_computation.3 | async-start | bytes 2359296 | tf_op jit(solution)/shard_map/all_to_all | solution.py:24
  277.9 14.7 %copy-start.4 = (bf16[512,256]{1,0:T(8,128)(2,1)S(1)}, bf16[512,256]{1,0:T(8,128)(2,1)}, u32[]{:S(2)}) copy-start(bf16[512,256]{1,0:T(8,128)(2,1)} %param.34) | copy-start | bytes 786436
  277.9 14.7 %copy-start.11 = (f32[512]{0:T(512)S(1)}, f32[512]{0:T(512)}, u32[]{:S(2)}) copy-start(f32[512]{0:T(512)} %param.35) | copy-start | bytes 6148
  292.6 2.2 copy-start.3
  294.8 8.7 %copy-start.9 = (bf16[512,512]{1,0:T(8,128)(2,1)S(1)}, bf16[512,512]{1,0:T(8,128)(2,1)}, u32[]{:S(2)}) copy-start(bf16[512,512]{1,0:T(8,128)(2,1)} %convolution_convert_fusion.1) | copy-start | bytes 1572868
  294.8 8.7 %copy-start.18 = (f32[512]{0:T(512)S(1)}, f32[512]{0:T(512)}, u32[]{:S(2)}) copy-start(f32[512]{0:T(512)} %param.37) | copy-start | bytes 6148
  311.0 64.8 %all-to-all-start.9 = ((bf16[8,4,128,512]{3,2,1,0:T(8,128)(2,1)}), bf16[8,4,128,512]{3,2,1,0:T(8,128)(2,1)}, u32[]{:S(2)}, u32[]{:S(2)}) async-start(bf16[8,4,128,512]{3,2,1,0:T(8,128)(2,1)} %bitcast.115), calls=%async_computation.9 | async-start | bytes 8388608 | tf_op jit(solution)/shard_map/all_to_all | solution.py:38
  316.3 62.5 %copy-start.16 = (pred[4,128]{1,0:T(4,128)(4,1)S(1)}, pred[4,128]{1,0:T(4,128)(4,1)}, u32[]{:S(2)}) copy-start(pred[4,128]{1,0:T(4,128)(4,1)} %copy-done.15) | copy-start | bytes 1540
  316.3 63.5 %copy-start.1 = (bf16[288,512]{1,0:T(8,128)(2,1)S(1)}, bf16[288,512]{1,0:T(8,128)(2,1)}, u32[]{:S(2)}) copy-start(bf16[288,512]{1,0:T(8,128)(2,1)} %param.33) | copy-start | bytes 884740
Sparse Core Ops, SparseCore 0:
  58.0 84.4 all-gather.4
  144.2 36.3 all-gather.6
  182.3 59.8 all-gather.8
  243.8 53.0 all-gather.10
where the time goes:
time: 387 us; the launch traced here: 386 us
  waiting for transfers between devices  209 us (54%)
  blocking collectives  41.3 us (11%)
  starting transfers between devices  39.8 us (10%)
  other arithmetic  39 us (10%)
  local copies, waits for them, and re-layouts  24.1 us (6%)
  matrix products  19.4 us (5%)
  between operations  14.2 us (4%)
    all_to_all x4, waiting for transfers between devices, sent_to_all(): lax.all_to_all(jnp.broadcast_to(x[None], (length, *x.shape)), axis, 0, 0,...  63.2 us
    all_to_all x1, waiting for transfers between devices, sum_at_owner(): lax.all_to_all(blocks, axis, split_axis=0, concat_axis=0, tiled=True)  58.8 us
    all_gather x1, waiting for transfers between devices, per_device(): inputs = lax.all_gather(found, 'chan', axis=2, tiled=True)  32.8 us
    all_gather x1, waiting for transfers between devices, per_device(): lax.all_gather(spread[0], 'fsdp', axis=0, tiled=True)  31.2 us
    all_to_all x4, starting transfers between devices, sent_to_all(): lax.all_to_all(jnp.broadcast_to(x[None], (length, *x.shape)), axis, 0, 0,...  24.2 us
    all_to_all x1, waiting for transfers between devices, per_device(): lax.all_to_all(looked, 'fsdp', split_axis=0, concat_axis=0, tiled=True)  16.5 us
    all_to_all x1, blocking collectives, per_device(): lax.all_to_all(pieces[0], 'chan', split_axis=1, concat_axis=0, tiled=True)  15.4 us
    all_to_all x1, blocking collectives, per_device(): lax.all_to_all(pieces[2], 'chan', split_axis=1, concat_axis=0, tiled=True)  13.8 us
  transfers between devices with their start and end apart: 11, of which 9 were waited for; matrix products, arithmetic and copies ran while one was open for 14% of the time, Pallas kernels for 0%

commit v1 on v0

v1 whole, which is shorter than its diff:
```python
import functools
import math

import jax
import jax.numpy as jnp
from jax import lax
from jax.experimental import pallas as pl
from jax.experimental.pallas import tpu as pltpu
from jax.sharding import PartitionSpec as P

RANK = 256
NSTATE = 16

learn_rate = 0.01
beta_first = 0.8
beta_second = 0.95
adam_eps = 1e-08
weight_decay = 0.1
bias_first = 1.0 - math.pow(0.8, 10)
bias_second = 1.0 - math.pow(0.95, 10)
norm_eps = 1e-06

BOTH = ("fsdp", "chan")
DEVICES = [
    (yl, z, co, yh, x)
    for yl in range(2)
    for z in range(4)
    for co in range(2)
    for yh in range(2)
    for x in range(4)
]


def place_of(yl, z, co, yh, x):
    return (yl * 8 + z * 2 + co) * 8 + yh * 4 + x


def in_route(k):
    return [
        (place_of(yl, z, co, yh, x), place_of(yh, z, co, yl, (x + k) % 4))
        for yl, z, co, yh, x in DEVICES
    ]


def out_route(j):
    return [
        (place_of(yl, z, co, yh, x), place_of(yl, x, co, (yh + j) % 2, z))
        for yl, z, co, yh, x in DEVICES
    ]


def from_x(a, k):
    return lax.ppermute(a, "chan", [(i, (i // 4) * 4 + (i % 4 - k) % 4) for i in range(8)])


def from_partner(a):
    return lax.ppermute(a, "chan", [(i, i ^ 4) for i in range(8)])


def adam_update(master, moment, velocity, grad):
    gradient = grad.astype(jnp.float32)
    moment = beta_first * moment + (1.0 - beta_first) * gradient
    velocity = beta_second * velocity + (1.0 - beta_second) * gradient * gradient
    update = moment / bias_first / (jnp.sqrt(velocity / bias_second) + adam_eps)
    return master - learn_rate * (update + weight_decay * master)


def in_product_kernel(s_ref, a0, a1, a2, a3, w0, w1, o_ref, acc):
    k = pl.program_id(0)
    for kk, a in enumerate((a0, a1, a2, a3)):

        @pl.when(k == kk)
        def _(kk=kk, a=a):
            total = None
            for h, w in enumerate((w0, w1)):
                lhs = jnp.concatenate(
                    [a[:, h * 128 : h * 128 + 128], a[:, 256 + h * 128 : 384 + h * 128]], axis=1
                )
                part = jnp.dot(lhs, w[...].reshape(256, 512), preferred_element_type=jnp.float32)
                total = part if total is None else total + part
            if kk == 0:
                acc[...] = total
            elif kk < 3:
                acc[...] += total
            else:
                o_ref[...] = (acc[...] + total).astype(o_ref.dtype)


def in_product(chunks, weights, column, x, dtype):
    tokens = chunks[0].shape[0]
    scalars = jnp.stack([column, x]).astype(jnp.int32)
    whole = pl.BlockSpec((tokens, 512), lambda k, s: (0, 0))
    return pl.pallas_call(
        in_product_kernel,
        out_shape=jax.ShapeDtypeStruct((tokens, 512), dtype),
        grid_spec=pltpu.PrefetchScalarGridSpec(
            num_scalar_prefetch=1,
            grid=(4,),
            in_specs=[whole] * 4
            + [
                pl.BlockSpec((2, 128, 512), lambda k, s: (lax.rem(s[1] + k, 4), 0, s[0])),
                pl.BlockSpec((2, 128, 512), lambda k, s: (4 + lax.rem(s[1] + k, 4), 0, s[0])),
            ],
            out_specs=whole,
            scratch_shapes=[pltpu.VMEM((tokens, 512), jnp.float32)],
        ),
        compiler_params=pltpu.CompilerParams(vmem_limit_bytes=24 * 2**20),
        cost_estimate=pl.CostEstimate(
            flops=2 * tokens * 2048 * 512, bytes_accessed=6 * 2**20, transcendentals=0
        ),
        name="in_product",
    )(scalars, *chunks, weights, weights)


def out_product_kernel(s_ref, a0, a1, a2, a3, w_ref, o_ref, acc):
    k = pl.program_id(0)
    rows = [
        w_ref[xs * 2 + co, yh * 32 : yh * 32 + 32, :]
        for co in range(2)
        for yh in range(2)
        for xs in range(4)
    ]
    rhs = jnp.concatenate(rows, axis=0)
    for kk, a in enumerate((a0, a1, a2, a3)):

        @pl.when(k == kk)
        def _(kk=kk, a=a):
            total = lax.dot_general(
                a[...], rhs, (((1,), (1,)), ((), ())), preferred_element_type=jnp.float32
            )
            if kk == 0:
                acc[...] = total
            elif kk < 3:
                acc[...] += total
            else:
                o_ref[...] = (acc[...] + total).astype(o_ref.dtype)


def out_product(chunks, weights, block, x, dtype):
    tokens = chunks[0].shape[0]
    scalars = jnp.stack([block, x]).astype(jnp.int32)
    whole = pl.BlockSpec((tokens, 512), lambda k, s: (0, 0))

    def where(k, s):
        source = lax.rem(s[1] + k, 4)
        return (s[0], 2 + source // 2, lax.rem(source, 2))

    return pl.pallas_call(
        out_product_kernel,
        out_shape=jax.ShapeDtypeStruct((tokens, 512), dtype),
        grid_spec=pltpu.PrefetchScalarGridSpec(
            num_scalar_prefetch=1,
            grid=(4,),
            in_specs=[whole] * 4 + [pl.BlockSpec((8, 64, 512), where)],
            out_specs=whole,
            scratch_shapes=[pltpu.VMEM((tokens, 512), jnp.float32)],
        ),
        compiler_params=pltpu.CompilerParams(vmem_limit_bytes=24 * 2**20),
        cost_estimate=pl.CostEstimate(
            flops=2 * tokens * 2048 * 512, bytes_accessed=6 * 2**20, transcendentals=0
        ),
        name="out_product",
    )(scalars, *chunks, weights)


def per_device(
    in_master,
    in_moment,
    in_velocity,
    in_grad,
    out_master,
    out_moment,
    out_velocity,
    out_grad,
    embed_table,
    tokens,
    conv_state,
    ssm_state,
    conv_weight,
    conv_bias,
    x_proj_w,
    dt_proj_w,
    dt_bias,
    a_log,
    d_skip,
):
    bf16 = jnp.bfloat16
    f32 = jnp.float32
    chan = lax.axis_index("chan")
    yh, x = chan // 4, chan % 4
    replicas = lax.axis_size("fsdp")
    vocab_rows, feature_part = embed_table.shape
    steps, rows = tokens.shape
    count = steps * rows
    capacity = 2 * count // replicas

    flat_tokens = tokens.reshape(count)
    owner = flat_tokens // vocab_rows
    order = jnp.arange(count, dtype=jnp.int32)
    before = jnp.logical_and(owner[:, None] == owner[None, :], order[:, None] < order[None, :])
    slot = jnp.sum(before.astype(jnp.int32), axis=0)
    place = owner * capacity + slot
    slots = jnp.arange(replicas * capacity, dtype=jnp.int32)
    hit = place[None, :] == slots[:, None]
    requests = jnp.sum(jnp.where(hit, flat_tokens[None, :] + 1, 0), axis=1) - 1
    asked = lax.all_to_all(
        requests.reshape(replicas, capacity), "fsdp", split_axis=0, concat_axis=0, tiled=True
    )

    in_new = adam_update(in_master, in_moment, in_velocity, in_grad)
    out_new = adam_update(out_master, out_moment, out_velocity, out_grad)
    own = in_new.shape[0]

    def route_in(matrix):
        blocks = in_new[:, matrix, :].astype(bf16).reshape(own, 2, 4, 512)
        got = []
        for k in range(4):
            piece = lax.dynamic_index_in_dim(blocks, (x + k) % 4, 2, keepdims=False)
            got.append(lax.ppermute(piece.reshape(own, 1024), BOTH, in_route(k)))
        stacked = jnp.stack(got)
        return jnp.concatenate(
            [lax.dynamic_index_in_dim(stacked, (x - source) % 4, 0, keepdims=False) for source in range(4)],
            axis=0,
        )

    def route_out():
        halves = out_new.astype(bf16).reshape(own, 2, 2048)
        got = []
        for j in range(2):
            piece = lax.dynamic_index_in_dim(halves, (yh + j) % 2, 1, keepdims=False)
            got.append(lax.ppermute(piece, BOTH, out_route(j)))
        first = jnp.where(yh == 0, got[0], got[1])
        second = jnp.where(yh == 0, got[1], got[0])
        both = jnp.concatenate([first, second], axis=0)
        return jnp.concatenate([both[:, :1024], both[:, 1024:]], axis=0)

    weights_x = lax.all_gather(route_in(0), "fsdp", axis=0, tiled=False)
    rest = jnp.concatenate([route_in(1), route_out()], axis=0)
    weights_zo = lax.all_gather(rest, "fsdp", axis=0, tiled=False)

    offset = jnp.clip(asked - lax.axis_index("fsdp") * vocab_rows, 0, vocab_rows - 1)
    looked = embed_table.at[offset.reshape(-1)].get(mode="promise_in_bounds")
    replies = lax.all_to_all(
        looked.reshape(replicas, capacity, feature_part), "fsdp", split_axis=0, concat_axis=0, tiled=True
    )
    found = replies.reshape(replicas * capacity, feature_part).at[place].get(mode="promise_in_bounds")

    chunks = [found] + [from_x(found, k) for k in (1, 2, 3)]
    found_real = found.astype(f32)
    squares = jnp.sum(found_real * found_real, axis=1).reshape(steps, rows)
    everyone = lax.all_to_all(
        jnp.broadcast_to(squares[None], (8, steps, rows)), "chan", 0, 0, tiled=True
    )
    scale = lax.rsqrt(everyone.sum(axis=0) / (8 * feature_part) + norm_eps)

    def project(weights):
        away = from_partner(in_product(chunks, weights, 1 - yh, x, bf16))
        here = in_product(chunks, weights, yh, x, f32)
        total = (here + away.astype(f32)).reshape(steps, rows, -1)
        return (total * scale[:, :, None]).astype(bf16)

    x_in = project(weights_x)

    window = jnp.concatenate([conv_state, jnp.moveaxis(x_in, 0, 1)], axis=1)
    acts = []
    for step in range(steps):
        mixed_conv = (
            jnp.sum(window[:, step : step + 4].astype(f32) * conv_weight[None], axis=1) + conv_bias
        )
        acts.append(jax.nn.silu(mixed_conv).astype(bf16))
    window_state = window[:, steps:, :]
    act = jnp.concatenate(acts, axis=0)
    contract_last = (((1,), (1,)), ((), ()))
    partial_value = lax.dot_general(act, x_proj_w, contract_last, preferred_element_type=f32).astype(bf16)
    arrived = lax.all_to_all(
        jnp.broadcast_to(partial_value[None], (8, *partial_value.shape)), "chan", 0, 0, tiled=True
    )
    dbc = arrived.astype(f32).sum(axis=0)

    z_in = project(weights_zo)

    dt_low = dbc[:, :RANK].astype(bf16)
    delta_all = jax.nn.softplus(
        lax.dot_general(dt_low, dt_proj_w, contract_last, preferred_element_type=f32) + dt_bias
    ).reshape(steps, rows, -1)
    b_all = dbc[:, RANK : RANK + NSTATE].reshape(steps, rows, NSTATE)
    c_all = dbc[:, RANK + NSTATE :].reshape(steps, rows, NSTATE)
    decay = -jnp.exp(a_log)
    state = ssm_state
    gates = []
    for step in range(steps):
        delta = delta_all[step]
        act_real = acts[step].astype(f32)
        state = (
            jnp.exp(delta[:, None, :] * decay[None]) * state
            + (delta * act_real)[:, None, :] * b_all[step][:, :, None]
        )
        y_out = jnp.sum(c_all[step][:, :, None] * state, axis=1) + d_skip * act_real
        gates.append((y_out * jax.nn.silu(z_in[step].astype(f32))).astype(bf16))
    gated = jnp.concatenate(gates, axis=0)

    gated_chunks = [gated] + [from_x(gated, k) for k in (1, 2, 3)]
    away = from_partner(out_product(gated_chunks, weights_zo, 1 - yh, x, bf16))
    here = out_product(gated_chunks, weights_zo, yh, x, f32)
    block_out = (found.astype(f32) + (here + away.astype(f32))).astype(bf16).reshape(steps, rows, -1)
    return (in_new, out_new, block_out, window_state, state)


def solution(mesh):
    split = P(("fsdp", "chan"), None, None)
    flat = P(("fsdp", "chan"), None)
    placed = (
        split,
        split,
        split,
        split,
        flat,
        flat,
        flat,
        flat,
        P("fsdp", "chan"),
        P(None, "fsdp"),
        P("fsdp", None, "chan"),
        P("fsdp", None, "chan"),
        P(None, "chan"),
        P("chan"),
        P(None, "chan"),
        P("chan", None),
        P("chan"),
        P(None, "chan"),
        P("chan"),
    )
    return jax.shard_map(
        per_device,
        mesh=mesh,
        in_specs=placed,
        out_specs=(
            split,
            flat,
            P(None, "fsdp", "chan"),
            P("fsdp", None, "chan"),
            P("fsdp", None, "chan"),
        ),
        check_vma=False,
    )
```

time: 387 us -> 280 us (0.72)
  waiting for transfers between devices: 209 us -> 127 us
  blocking collectives: 41.3 us -> 0 us
  starting transfers between devices: 39.8 us -> 66.5 us
  other arithmetic: 39 us -> 21.5 us
  matrix products: 19.4 us -> 2.4 us
  Pallas kernels: 0 us -> 16.5 us
  local copies, waits for them, and re-layouts: 24.1 us -> 30.4 us
    all_to_all x6 -> x3, waiting for transfers between devices: 138 us -> 49.9 us  [the longest x1 27.4 us: per_device(): lax.all_to_all(jnp.broadcast_to(partial_value[None], (8, *partial_value.s...]
    ppermute x0 -> x19, waiting for transfers between devices: none -> 71.3 us  [the longest x6 37.6 us: from_x(): lax.ppermute(a, 'chan', [(i, i // 4 * 4 + (i % 4 - k) % 4) for i in range...]
    all_gather x4 -> x2, waiting for transfers between devices: 64 us -> 0.02 us  [the longest x1 0.02 us: per_device(): weights_zo = lax.all_gather(rest, 'fsdp', axis=0, tiled=False)]
    all_to_all x3 -> x0, blocking collectives: 41.3 us -> none  [the longest x1 15.4 us: per_device(): lax.all_to_all(pieces[0], 'chan', split_axis=1, concat_axis=0, tiled=True)]
    ppermute x0 -> x19, starting transfers between devices: none -> 39.9 us  [the longest x2 18.4 us: route_out(): got.append(lax.ppermute(piece, BOTH, out_route(j)))]
    dot_general x7 -> x1, matrix products: 17.9 us -> 0.34 us  [per_device(): lax.dot_general(act, x_proj_w, contract_last, preferred_element_type=f32)]
    pallas_call x0 -> x6, Pallas kernels: none -> 16.5 us  [the longest x4 10.6 us: in_product(): pl.pallas_call(in_product_kernel, out_shape=jax.ShapeDtypeStruct((tokens,...]
    all_to_all x6 -> x3, starting transfers between devices: 33.2 us -> 20.6 us  [the longest x1 9.62 us: per_device(): lax.all_to_all(jnp.broadcast_to(squares[None], (8, steps, rows)), 'chan',...]
  transfers between devices with their start and end apart: 11 -> 25, of which waited for: 9 -> 14; matrix products, arithmetic and copies ran while one was open for 14% -> 6% of each run, Pallas kernels for 0% -> 5%
where the time goes in v1:
time: 280 us
  waiting for transfers between devices  127 us (45%)
  starting transfers between devices  66.5 us (24%)
  local copies, waits for them, and re-layouts  30.4 us (11%)
  other arithmetic  21.5 us (8%)
  Pallas kernels  16.5 us (6%)
  between operations  14.9 us (5%)
    ppermute x6, waiting for transfers between devices, from_x(): lax.ppermute(a, 'chan', [(i, i // 4 * 4 + (i % 4 - k) % 4) for i in range...  37.6 us
    all_to_all x1, waiting for transfers between devices, per_device(): lax.all_to_all(jnp.broadcast_to(partial_value[None], (8, *partial_value.s...  27.4 us
    all_to_all x1, waiting for transfers between devices, per_device(): lax.all_to_all(looked.reshape(replicas, capacity, feature_part), 'fsdp',...  22.5 us
    ppermute x3, waiting for transfers between devices, from_partner(): return lax.ppermute(a, 'chan', [(i, i ^ 4) for i in range(8)])  21.9 us
    ppermute x2, starting transfers between devices, route_out(): got.append(lax.ppermute(piece, BOTH, out_route(j)))  18.4 us
    pallas_call x4, Pallas kernels, in_product(): pl.pallas_call(in_product_kernel, out_shape=jax.ShapeDtypeStruct((tokens,...  10.6 us
    all_to_all x1, starting transfers between devices, per_device(): lax.all_to_all(jnp.broadcast_to(squares[None], (8, steps, rows)), 'chan',...  9.62 us
    ppermute x8, starting transfers between devices, route_in(): got.append(lax.ppermute(piece.reshape(own, 1024), BOTH, in_route(k)))  9.53 us
  transfers between devices with their start and end apart: 25, of which 14 were waited for; matrix products, arithmetic and copies ran while one was open for 6% of the time, Pallas kernels for 5%

profile of v1, /device:TPU:6, one launch (start us, length us, event | category | flops | bytes accessed | tf_op | source)
XLA Modules:
  0.0 279.5 jit_solution(13626915797853392984)
XLA Ops:
  7.3 5.7 %fusion.62 = (bf16[32,2,4096]{2,1,0:T(2,128)(2,1)S(1)}, f32[32,2,4096]{2,1,0:T(2,128)}) fusion(f32[32,2,4096]{2,1,0:T(2,128)} %param.19, f32[32,2,4096]{2,1,0:T(2,128)} %param.21, bf16[32,2,4096]{2,1,0:T(2,128)(2,1)} %param.22, f32[32,2,4096]{2,1,0:T(2,128)} %param.20), kind=kLoop, calls=%fused_computation.177 | loop fusion | flops 4456448 | bytes 5242880 | tf_op jit(solution)/shard_map/convert.6
  13.0 2.2 slice_reduce_fusion
  15.6 3.6 %dynamic-slice_reduce_fusion.3 = (bf16[32,2,512]{2,1,0:T(2,128)(2,1)S(1)}, bf16[32,2,512]{2,1,0:T(2,128)(2,1)S(1)}, bf16[32,2,512]{2,1,0:T(2,128)(2,1)S(1)}, bf1...) fusion(bf16[32,2,4,512]{3,2,1,0:T(4,128)(2,1)S(1)} %convert_ele, ...), kind=kLoop, calls=%fused_computation.133 | loop fusion | bytes 1048592 | tf_op jit(solution)/shard_map/jit(dynamic_index_in_dim)/dynamic_slice | solution.py:218
  19.2 0.7 collective-permute-start.3
  19.9 0.9 collective-permute-start.6
  20.8 1.1 collective-permute-start.5
  21.9 2.2 collective-permute-start.4
  24.2 1.8 collective-permute-done.6
  25.9 0.7 collective-permute-done.5
  26.6 0.4 collective-permute-done.4
  27.1 0.7 pad_maximum_fusion.3
  28.0 2.7 collective-permute-start.9
  30.7 0.9 collective-permute-start.10
  31.8 0.8 collective-permute-start.8
  32.7 1.2 fusion.60
  34.1 0.5 constant_dynamic-slice_fusion
  34.8 8.5 %collective-permute-start.12 = (bf16[32,2048]{1,0:T(8,128)(2,1)S(1)}, bf16[32,2048]{1,0:T(8,128)(2,1)S(1)}, u32[]{:S(2)}, u32[]{:S(2)}) collective-permute-start(bf16[32,2048]{1,0:T(8,128)(2,1)S(1)} %bitcast.126), channel_id=1, source_target_pairs={{0,0},{1,16},{2,32},{3,48},{4,4},{5,20},{6,36},{7,52},{8,8},{9,24}... | collective-permute-start | bytes 393224 | tf_op jit(solution)/shard_map/ppermute | solution.py:231
  43.4 9.8 %collective-permute-start.13 = (bf16[32,2048]{1,0:T(8,128)(2,1)S(1)}, bf16[32,2048]{1,0:T(8,128)(2,1)S(1)}, u32[]{:S(2)}, u32[]{:S(2)}) collective-permute-start(bf16[32,2048]{1,0:T(8,128)(2,1)S(1)} %bitcast.127), channel_id=1, source_target_pairs={{0,4},{1,20},{2,36},{3,52},{4,0},{5,16},{6,32},{7,48},{8,12},{9,28... | collective-permute-start | bytes 393224 | tf_op jit(solution)/shard_map/ppermute | solution.py:231
  53.4 8.9 %collective-permute-done.13 = bf16[32,2048]{1,0:T(8,128)(2,1)S(1)} collective-permute-done((bf16[32,2048]{1,0:T(8,128)(2,1)S(1)}, bf16[32,2048]{1,0:T(8,128)(2,1)S(1)}, u32[]{:S(2)}, u32[]{:S(2)}) %collective-permute-start.13) | collective-permute-done | bytes 131104 | tf_op jit(solution)/shard_map/ppermute | solution.py:231
  62.4 0.8 copy-done.14
  63.7 0.7 sub.60
  64.4 5.9 %all-to-all-start = ((s32[16,1,64]{2,1,0:T(1,128)}), s32[16,1,64]{2,1,0:T(1,128)S(1)}, u32[]{:S(2)}, u32[]{:S(2)}) async-start(s32[16,1,64]{2,1,0:T(1,128)} %sub.60), calls=%async_computation | async-start | bytes 16384 | tf_op jit(solution)/shard_map/all_to_all | solution.py:206
  70.3 6.0 %all-to-all-done = s32[16,1,64]{2,1,0:T(1,128)S(1)} async-done(((s32[16,1,64]{2,1,0:T(1,128)}), s32[16,1,64]{2,1,0:T(1,128)S(1)}, u32[]{:S(2)}, u32[]{:S(2)}) %all-to-all-start) | async-done | bytes 4128 | tf_op jit(solution)/shard_map/all_to_all | solution.py:206
  76.4 7.9 %gather_fusion = bf16[1024,512]{1,0:T(8,128)(2,1)} fusion(bf16[4096,512]{1,0:T(8,128)(2,1)} %param.27, s32[1024]{0:T(1024)S(1)} %broadcast_clamp_fusion), kind=kCustom, calls=%fused_computation | custom fusion | bytes 2101248 | tf_op jit(solution)/shard_map/gather | solution.py:242
  84.3 3.7 %all-to-all-start.1 = ((bf16[16,64,512]{2,1,0:T(8,128)(2,1)}), bf16[16,64,512]{2,1,0:T(8,128)(2,1)S(1)}, u32[]{:S(2)}, u32[]{:S(2)}) async-start(bf16[16,64,512]{2,1,0:T(8,128)(2,1)} %bitcast.2), calls=%async_computation.1 | async-start | bytes 2097152 | tf_op jit(solution)/shard_map/all_to_all | solution.py:243
  88.0 22.5 %all-to-all-done.1 = bf16[16,64,512]{2,1,0:T(8,128)(2,1)S(1)} async-done(((bf16[16,64,512]{2,1,0:T(8,128)(2,1)}), bf16[16,64,512]{2,1,0:T(8,128)(2,1)S(1)}, u32[]{:S(2)}, u32[]{:S(2)}) %all-to-all-start.1) | async-done | bytes 1048608 | tf_op jit(solution)/shard_map/all_to_all | solution.py:243
  110.6 2.0 gather_fusion.1
  112.5 1.9 collective-permute-start.2
  114.4 0.9 collective-permute-start
  115.6 0.6 broadcast_in_dim.21
  116.3 9.6 %all-to-all-start.2 = ((f32[8,4,128]{2,1,0:T(4,128)}), f32[8,4,128]{2,1,0:T(4,128)S(1)}, u32[]{:S(2)}, u32[]{:S(2)}) async-start(f32[8,4,128]{2,1,0:T(4,128)} %broadcast_in_dim.21), calls=%async_computation.2 | async-start | bytes 32768 | tf_op jit(solution)/shard_map/all_to_all | solution.py:251
  125.9 10.0 %collective-permute-done.2.a3 = bf16[512,512]{1,0:T(8,128)(2,1)S(1)} collective-permute-done((bf16[512,512]{1,0:T(8,128)(2,1)S(1)}, bf16[512,512]{1,0:T(8,128)(2,1)S(1)}, u32[]{:S(2)}, u32[]{:S(2)}) %collective-permute-start.2) | collective-permute-done | bytes 524320 | tf_op jit(solution)/shard_map/ppermute | solution.py:53
  135.9 3.3 %collective-permute-done.a1 = bf16[512,512]{1,0:T(8,128)(2,1)S(1)} collective-permute-done((bf16[512,512]{1,0:T(8,128)(2,1)S(1)}, bf16[512,512]{1,0:T(8,128)(2,1)S(1)}, u32[]{:S(2)}, u32[]{:S(2)}) %collective-permute-start) | collective-permute-done | bytes 524320 | tf_op jit(solution)/shard_map/ppermute | solution.py:53
  139.2 2.2 copy-done.3
  141.5 2.7 in_product.5
  144.1 3.8 %collective-permute-start.7 = (bf16[512,512]{1,0:T(8,128)(2,1)S(1)}, bf16[512,512]{1,0:T(8,128)(2,1)S(1)}, u32[]{:S(2)}, u32[]{:S(2)}) collective-permute-start(bf16[512,512]{1,0:T(8,128)(2,1)S(1)} %in_product.5), channel_id=1, source_target_pairs={{0,4},{1,5},{2,6},{3,7},{4,0},{5,1},{6,2},{7,3},{8,12},{9,13},{10,... | collective-permute-start | bytes 1572872 | tf_op jit(solution)/shard_map/ppermute | solution.py:57
  148.0 3.4 %copy-done.1 = bf16[4096,1024]{1,0:T(8,128)(2,1)S(1)} copy-done((bf16[4096,1024]{1,0:T(8,128)(2,1)S(1)}, bf16[4096,1024]{1,0:T(8,128)(2,1)}, u32[]{:S(2)}) %copy-start.1) | copy-done | bytes 8388632
  151.4 2.6 in_product.7
  154.4 2.7 in_product.4
  157.1 3.6 %collective-permute-done.7 = bf16[512,512]{1,0:T(8,128)(2,1)S(1)} collective-permute-done((bf16[512,512]{1,0:T(8,128)(2,1)S(1)}, bf16[512,512]{1,0:T(8,128)(2,1)S(1)}, u32[]{:S(2)}, u32[]{:S(2)}) %collective-permute-start.7) | collective-permute-done | bytes 524320 | tf_op jit(solution)/shard_map/ppermute | solution.py:57
  160.9 2.7 in_product.6
  163.6 7.2 %collective-permute-done.14 = bf16[512,512]{1,0:T(8,128)(2,1)S(1)} collective-permute-done((bf16[512,512]{1,0:T(8,128)(2,1)S(1)}, bf16[512,512]{1,0:T(8,128)(2,1)S(1)}, u32[]{:S(2)}, u32[]{:S(2)}) %collective-permute-start.14) | collective-permute-done | bytes 524320 | tf_op jit(solution)/shard_map/ppermute | solution.py:57
  171.0 1.0 multiply_convert_fusion
  172.0 0.8 copy-done.6
  173.5 0.6 copy-done.9
  174.6 1.6 broadcast_in_dim.22
  176.2 7.3 %all-to-all-start.3 = ((bf16[8,512,288]{1,2,0:T(8,128)(2,1)}), bf16[8,512,288]{1,2,0:T(8,128)(2,1)S(1)}, u32[]{:S(2)}, u32[]{:S(2)}) async-start(bf16[8,512,288]{1,2,0:T(8,128)(2,1)} %broadcast_in_dim.22), calls=%async_computation.3 | async-start | bytes 4718592 | tf_op jit(solution)/shard_map/all_to_all | solution.py:275
  183.6 27.4 %all-to-all-done.3 = bf16[8,512,288]{1,2,0:T(8,128)(2,1)S(1)} async-done(((bf16[8,512,288]{1,2,0:T(8,128)(2,1)}), bf16[8,512,288]{1,2,0:T(8,128)(2,1)S(1)}, u32[]{:S(2)}, u32[]{:S(2)}) %all-to-all-start.3) | async-done | bytes 2359328 | tf_op jit(solution)/shard_map/all_to_all | solution.py:275
  211.3 0.8 copy-done.13
  212.9 2.1 compare_select_fusion
  215.0 1.2 fusion.63
  216.2 7.9 %multiply_reduce_fusion.2 = (f32[128,512]{1,0:T(8,128)S(1)}, f32[128,512]{1,0:T(8,128)S(1)}, f32[128,512]{1,0:T(8,128)S(1)}, f32[128,512]{1,0:T(8,128)S(1)}, f32[128,16,512]{2,1,0:T(8,128)}) fusion(f32[128,16]{1,0:T(8,128)S(1)} %copy.46, f32[128,16]{1,0:T(8,128)S(1)} %copy.47, f32[128,512]{1,0:T(8,128)S(1)} %get-tuple-element.32, f32[128,16]{1,0:T(8,128)S(1)} %copy.45, ...), kind=kLoop, calls=%fused_computation.7 | loop fusion | flops 24903680 | bytes 11632640 | tf_op jit(solution)/shard_map/reduce_sum | solution.py:298
  224.1 0.4 fusion.31
  224.6 2.7 collective-permute-start.17
  227.3 0.4 collective-permute-start.16
  227.7 1.3 collective-permute-start.15
  229.1 20.6 %collective-permute-done.17.a3 = bf16[512,512]{1,0:T(8,128)(2,1)S(1)} collective-permute-done((bf16[512,512]{1,0:T(8,128)(2,1)S(1)}, bf16[512,512]{1,0:T(8,128)(2,1)S(1)}, u32[]{:S(2)}, u32[]{:S(2)}) %collective-permute-start.17) | collective-permute-done | bytes 524320 | tf_op jit(solution)/shard_map/ppermute | solution.py:53
  249.6 3.7 %collective-permute-done.15.a1 = bf16[512,512]{1,0:T(8,128)(2,1)S(1)} collective-permute-done((bf16[512,512]{1,0:T(8,128)(2,1)S(1)}, bf16[512,512]{1,0:T(8,128)(2,1)S(1)}, u32[]{:S(2)}, u32[]{:S(2)}) %collective-permute-start.15) | collective-permute-done | bytes 524320 | tf_op jit(solution)/shard_map/ppermute | solution.py:53
  253.3 3.0 %out_product.3 = bf16[512,512]{1,0:T(8,128)(2,1)S(1)} custom-call(s32[2]{0:T(128)S(1)} %pad_add_fusion.1.s_ref, bf16[512,512]{1,0:T(8,128)(2,1)S(1)} %pad_maximum_fusion.1.a0, bf16[512,512]{1,0:T(8,128)(2,1)S(1)} %collective-permute-done.15.a1, bf16[512,512]{1,0:T(8,128)(2,1)S(1)} %collective-permute-done.16.a2, ...), custom_call_target="tpu_custom_call" | custom-call | flops 1073741824 | bytes 6291456 | tf_op jit(solution)/shard_map/out_product/pallas_call | solution.py:148
  256.3 0.6 collective-permute-start.18
  256.9 0.8 slice.154
  257.7 2.9 %out_product.2 = f32[512,512]{1,0:T(8,128)S(1)} custom-call(s32[2]{0:T(128)S(1)} %pad_add_fusion.s_ref, bf16[512,512]{1,0:T(8,128)(2,1)S(1)} %pad_maximum_fusion.1.a0, bf16[512,512]{1,0:T(8,128)(2,1)S(1)} %collective-permute-done.15.a1, bf16[512,512]{1,0:T(8,128)(2,1)S(1)} %collective-permute-done.16.a2, bf16[512,512]{1,0:T(8,128)(2,1)S(1)} %collective-permute-done.17.a3, ...), custom_call_target="tpu_custom_call" | custom-call | flops 1073741824 | bytes 6291456 | tf_op jit(solution)/shard_map/out_product/pallas_call | solution.py:148
  260.6 11.1 %collective-permute-done.18 = bf16[512,512]{1,0:T(8,128)(2,1)S(1)} collective-permute-done((bf16[512,512]{1,0:T(8,128)(2,1)S(1)}, bf16[512,512]{1,0:T(8,128)(2,1)S(1)}, u32[]{:S(2)}, u32[]{:S(2)}) %collective-permute-start.18) | collective-permute-done | bytes 524320 | tf_op jit(solution)/shard_map/ppermute | solution.py:57
  271.7 1.0 fusion.4
  (125 shorter events, 5.3 us)
Async XLA Ops:
  7.2 167.1 %copy-start = (bf16[288,512]{1,0:T(8,128)(2,1)S(1)}, bf16[288,512]{1,0:T(8,128)(2,1)}, u32[]{:S(2)}) copy-start(bf16[288,512]{1,0:T(8,128)(2,1)} %param.33) | copy-start | bytes 884740
  7.2 132.0 %all-gather.5.cloned.1.call-start = ((), (), s32[]{:S(2)}) async-start(), calls=%async_computation.4 | async-start | bytes 4456448 | tf_op jit(solution)/shard_map/all_gather | solution.py:237
  13.0 19.7 %copy-start.15 = (f32[32,4096]{1,0:T(8,128)S(1)}, f32[32,4096]{1,0:T(8,128)}, u32[]{:S(2)}) copy-start(f32[32,4096]{1,0:T(8,128)} %param.23) | copy-start | bytes 1572868
  13.0 19.7 %copy-start.16 = (f32[32,4096]{1,0:T(8,128)S(1)}, f32[32,4096]{1,0:T(8,128)}, u32[]{:S(2)}) copy-start(f32[32,4096]{1,0:T(8,128)} %param.25) | copy-start | bytes 1572868
  13.0 19.7 %copy-start.17 = (f32[32,4096]{1,0:T(8,128)S(1)}, f32[32,4096]{1,0:T(8,128)}, u32[]{:S(2)}) copy-start(f32[32,4096]{1,0:T(8,128)} %param.24) | copy-start | bytes 1572868
  13.0 19.7 %copy-start.19 = (bf16[32,4096]{1,0:T(8,128)(2,1)S(1)}, bf16[32,4096]{1,0:T(8,128)(2,1)}, u32[]{:S(2)}) copy-start(bf16[32,4096]{1,0:T(8,128)(2,1)} %param.26) | copy-start | bytes 786436
  19.2 5.0 %collective-permute-start.3 = (bf16[32,1024]{1,0:T(8,128)(2,1)S(1)}, bf16[32,1024]{1,0:T(8,128)(2,1)S(1)}, u32[]{:S(2)}, u32[]{:S(2)}) collective-permute-start(bf16[32,1024]{1,0:T(8,128)(2,1)S(1)} %bitcast.132), channel_id=1, source_target_pairs={{0,0},{1,1},{2,2},{3,3},{4,64},{5,65},{6,66},{7,67},{8,8},{9,9},{1... | collective-permute-start | bytes 196616 | tf_op jit(solution)/shard_map/ppermute | solution.py:219
  19.9 6.0 %collective-permute-start.6 = (bf16[32,1024]{1,0:T(8,128)(2,1)S(1)}, bf16[32,1024]{1,0:T(8,128)(2,1)S(1)}, u32[]{:S(2)}, u32[]{:S(2)}) collective-permute-start(bf16[32,1024]{1,0:T(8,128)(2,1)S(1)} %bitcast.133), channel_id=1, source_target_pairs={{0,3},{1,0},{2,1},{3,2},{4,67},{5,64},{6,65},{7,66},{8,11},{9,8},{... | collective-permute-start | bytes 196616 | tf_op jit(solution)/shard_map/ppermute | solution.py:219
  20.8 5.8 %collective-permute-start.5 = (bf16[32,1024]{1,0:T(8,128)(2,1)S(1)}, bf16[32,1024]{1,0:T(8,128)(2,1)S(1)}, u32[]{:S(2)}, u32[]{:S(2)}) collective-permute-start(bf16[32,1024]{1,0:T(8,128)(2,1)S(1)} %bitcast.134), channel_id=1, source_target_pairs={{0,2},{1,3},{2,0},{3,1},{4,66},{5,67},{6,64},{7,65},{8,10},{9,11},... | collective-permute-start | bytes 196616 | tf_op jit(solution)/shard_map/ppermute | solution.py:219
  21.9 5.2 %collective-permute-start.4 = (bf16[32,1024]{1,0:T(8,128)(2,1)S(1)}, bf16[32,1024]{1,0:T(8,128)(2,1)S(1)}, u32[]{:S(2)}, u32[]{:S(2)}) collective-permute-start(bf16[32,1024]{1,0:T(8,128)(2,1)S(1)} %bitcast.135), channel_id=1, source_target_pairs={{0,1},{1,2},{2,3},{3,0},{4,65},{5,66},{6,67},{7,64},{8,9},{9,10},{... | collective-permute-start | bytes 196616 | tf_op jit(solution)/shard_map/ppermute | solution.py:219
  27.9 120.1 %all-gather.7.cloned.1.call-start = ((), (), s32[]{:S(2)}) async-start(), calls=%async_computation.5 | async-start | bytes 8912896 | tf_op jit(solution)/shard_map/all_gather | solution.py:239
  28.0 35.3 %copy-start.22 = (s32[4,128]{1,0:T(4,128)S(1)}, s32[4,128]{1,0:T(4,128)}, u32[]{:S(2)}) copy-start(s32[4,128]{1,0:T(4,128)} %param.28) | copy-start | bytes 6148
  28.0 15.5 %collective-permute-start.9 = (bf16[32,1024]{1,0:T(8,128)(2,1)S(1)}, bf16[32,1024]{1,0:T(8,128)(2,1)S(1)}, u32[]{:S(2)}, u32[]{:S(2)}) collective-permute-start(bf16[32,1024]{1,0:T(8,128)(2,1)S(1)} %bitcast.129), channel_id=1, source_target_pairs={{0,1},{1,2},{2,3},{3,0},{4,65},{5,66},{6,67},{7,64},{8,9},{9,10},{... | collective-permute-start | bytes 196616 | tf_op jit(solution)/shard_map/ppermute | solution.py:219
  30.7 22.5 %collective-permute-start.10 = (bf16[32,1024]{1,0:T(8,128)(2,1)S(1)}, bf16[32,1024]{1,0:T(8,128)(2,1)S(1)}, u32[]{:S(2)}, u32[]{:S(2)}) collective-permute-start(bf16[32,1024]{1,0:T(8,128)(2,1)S(1)} %bitcast.128), channel_id=1, source_target_pairs={{0,2},{1,3},{2,0},{3,1},{4,66},{5,67},{6,64},{7,65},{8,10},{9,11},... | collective-permute-start | bytes 196616 | tf_op jit(solution)/shard_map/ppermute | solution.py:219
  31.6 21.6 %collective-permute-start.11 = (bf16[32,1024]{1,0:T(8,128)(2,1)S(1)}, bf16[32,1024]{1,0:T(8,128)(2,1)S(1)}, u32[]{:S(2)}, u32[]{:S(2)}) collective-permute-start(bf16[32,1024]{1,0:T(8,128)(2,1)S(1)} %bitcast.130), channel_id=1, source_target_pairs={{0,3},{1,0},{2,1},{3,2},{4,67},{5,64},{6,65},{7,66},{8,11},{9,8},{... | collective-permute-start | bytes 196616 | tf_op jit(solution)/shard_map/ppermute | solution.py:219
  31.8 21.5 %collective-permute-start.8 = (bf16[32,1024]{1,0:T(8,128)(2,1)S(1)}, bf16[32,1024]{1,0:T(8,128)(2,1)S(1)}, u32[]{:S(2)}, u32[]{:S(2)}) collective-permute-start(bf16[32,1024]{1,0:T(8,128)(2,1)S(1)} %bitcast.131), channel_id=1, source_target_pairs={{0,0},{1,1},{2,2},{3,3},{4,64},{5,65},{6,66},{7,67},{8,8},{9,9},{1... | collective-permute-start | bytes 196616 | tf_op jit(solution)/shard_map/ppermute | solution.py:219
  34.8 18.6 %collective-permute-start.12 = (bf16[32,2048]{1,0:T(8,128)(2,1)S(1)}, bf16[32,2048]{1,0:T(8,128)(2,1)S(1)}, u32[]{:S(2)}, u32[]{:S(2)}) collective-permute-start(bf16[32,2048]{1,0:T(8,128)(2,1)S(1)} %bitcast.126), channel_id=1, source_target_pairs={{0,0},{1,16},{2,32},{3,48},{4,4},{5,20},{6,36},{7,52},{8,8},{9,24}... | collective-permute-start | bytes 393224 | tf_op jit(solution)/shard_map/ppermute | solution.py:231
  43.4 18.9 %collective-permute-start.13 = (bf16[32,2048]{1,0:T(8,128)(2,1)S(1)}, bf16[32,2048]{1,0:T(8,128)(2,1)S(1)}, u32[]{:S(2)}, u32[]{:S(2)}) collective-permute-start(bf16[32,2048]{1,0:T(8,128)(2,1)S(1)} %bitcast.127), channel_id=1, source_target_pairs={{0,4},{1,20},{2,36},{3,52},{4,0},{5,16},{6,32},{7,48},{8,12},{9,28... | collective-permute-start | bytes 393224 | tf_op jit(solution)/shard_map/ppermute | solution.py:231
  62.4 0.8 copy-start.14
  64.4 11.9 %all-to-all-start = ((s32[16,1,64]{2,1,0:T(1,128)}), s32[16,1,64]{2,1,0:T(1,128)S(1)}, u32[]{:S(2)}, u32[]{:S(2)}) async-start(s32[16,1,64]{2,1,0:T(1,128)} %sub.60), calls=%async_computation | async-start | bytes 16384 | tf_op jit(solution)/shard_map/all_to_all | solution.py:206
  84.3 26.2 %all-to-all-start.1 = ((bf16[16,64,512]{2,1,0:T(8,128)(2,1)}), bf16[16,64,512]{2,1,0:T(8,128)(2,1)S(1)}, u32[]{:S(2)}, u32[]{:S(2)}) async-start(bf16[16,64,512]{2,1,0:T(8,128)(2,1)} %bitcast.2), calls=%async_computation.1 | async-start | bytes 2097152 | tf_op jit(solution)/shard_map/all_to_all | solution.py:243
  112.5 23.4 %collective-permute-start.2 = (bf16[512,512]{1,0:T(8,128)(2,1)S(1)}, bf16[512,512]{1,0:T(8,128)(2,1)S(1)}, u32[]{:S(2)}, u32[]{:S(2)}) collective-permute-start(bf16[512,512]{1,0:T(8,128)(2,1)S(1)} %gather_fusion.1), channel_id=1, source_target_pairs={{0,1},{1,2},{2,3},{3,0},{4,5},{5,6},{6,7},{7,4},{8,9},{9,10},{10,1... | collective-permute-start | bytes 1572872 | tf_op jit(solution)/shard_map/ppermute | solution.py:53
  114.4 21.4 %collective-permute-start.1 = (bf16[512,512]{1,0:T(8,128)(2,1)S(1)}, bf16[512,512]{1,0:T(8,128)(2,1)S(1)}, u32[]{:S(2)}, u32[]{:S(2)}) collective-permute-start(bf16[512,512]{1,0:T(8,128)(2,1)S(1)} %gather_fusion.1), channel_id=1, source_target_pairs={{0,2},{1,3},{2,0},{3,1},{4,6},{5,7},{6,4},{7,5},{8,10},{9,11},{10,... | collective-permute-start | bytes 1572872 | tf_op jit(solution)/shard_map/ppermute | solution.py:53
  114.4 24.8 %collective-permute-start = (bf16[512,512]{1,0:T(8,128)(2,1)S(1)}, bf16[512,512]{1,0:T(8,128)(2,1)S(1)}, u32[]{:S(2)}, u32[]{:S(2)}) collective-permute-start(bf16[512,512]{1,0:T(8,128)(2,1)S(1)} %gather_fusion.1), channel_id=1, source_target_pairs={{0,3},{1,0},{2,1},{3,2},{4,7},{5,4},{6,5},{7,6},{8,11},{9,8},{10,9... | collective-permute-start | bytes 1572872 | tf_op jit(solution)/shard_map/ppermute | solution.py:53
  116.3 31.7 %all-to-all-start.2 = ((f32[8,4,128]{2,1,0:T(4,128)}), f32[8,4,128]{2,1,0:T(4,128)S(1)}, u32[]{:S(2)}, u32[]{:S(2)}) async-start(f32[8,4,128]{2,1,0:T(4,128)} %broadcast_in_dim.21), calls=%async_computation.2 | async-start | bytes 32768 | tf_op jit(solution)/shard_map/all_to_all | solution.py:251
  139.2 2.2 copy-start.3
  144.1 16.6 %collective-permute-start.7 = (bf16[512,512]{1,0:T(8,128)(2,1)S(1)}, bf16[512,512]{1,0:T(8,128)(2,1)S(1)}, u32[]{:S(2)}, u32[]{:S(2)}) collective-permute-start(bf16[512,512]{1,0:T(8,128)(2,1)S(1)} %in_product.5), channel_id=1, source_target_pairs={{0,4},{1,5},{2,6},{3,7},{4,0},{5,1},{6,2},{7,3},{8,12},{9,13},{10,... | collective-permute-start | bytes 1572872 | tf_op jit(solution)/shard_map/ppermute | solution.py:57
  148.0 3.4 %copy-start.1 = (bf16[4096,1024]{1,0:T(8,128)(2,1)S(1)}, bf16[4096,1024]{1,0:T(8,128)(2,1)}, u32[]{:S(2)}) copy-start(bf16[4096,1024]{1,0:T(8,128)(2,1)} %all-gather.7.cloned.1.call-done) | copy-start | bytes 25165828
  151.4 3.0 %copy-start.4 = (bf16[2048,1024]{1,0:T(8,128)(2,1)S(1)}, bf16[2048,1024]{1,0:T(8,128)(2,1)}, u32[]{:S(2)}) copy-start(bf16[2048,1024]{1,0:T(8,128)(2,1)} %all-gather.5.cloned.1.call-done) | copy-start | bytes 12582916
  154.1 16.7 %collective-permute-start.14 = (bf16[512,512]{1,0:T(8,128)(2,1)S(1)}, bf16[512,512]{1,0:T(8,128)(2,1)S(1)}, u32[]{:S(2)}, u32[]{:S(2)}) collective-permute-start(bf16[512,512]{1,0:T(8,128)(2,1)S(1)} %in_product.7), channel_id=1, source_target_pairs={{0,4},{1,5},{2,6},{3,7},{4,0},{5,1},{6,2},{7,3},{8,12},{9,13},{10,... | collective-permute-start | bytes 1572872 | tf_op jit(solution)/shard_map/ppermute | solution.py:57
  154.4 6.5 %copy-start.2 = (bf16[4096,1024]{1,0:T(8,128)(2,1)S(1)}, bf16[4096,1024]{1,0:T(8,128)(2,1)}, u32[]{:S(2)}) copy-start(bf16[4096,1024]{1,0:T(8,128)(2,1)} %all-gather.7.cloned.1.call-done) | copy-start | bytes 25165828
  163.5 9.3 %copy-start.18 = (bf16[128,3,512]{2,0,1:T(8,128)(2,1)S(1)}, bf16[128,3,512]{2,0,1:T(8,128)(2,1)}, u32[]{:S(2)}) copy-start(bf16[128,3,512]{2,0,1:T(8,128)(2,1)} %param.29) | copy-start | bytes 1179652
  163.5 9.3 %copy-start.21 = (f32[4,512]{1,0:T(4,128)S(1)}, f32[4,512]{1,0:T(4,128)}, u32[]{:S(2)}) copy-start(f32[4,512]{1,0:T(4,128)} %param.31) | copy-start | bytes 24580
  163.6 9.7 %copy-start.23 = (f32[512]{0:T(512)S(1)}, f32[512]{0:T(512)}, u32[]{:S(2)}) copy-start(f32[512]{0:T(512)} %param.32) | copy-start | bytes 6148
  172.0 0.8 copy-start.6
  173.5 0.7 copy-start.9
  173.5 0.7 copy-start.11
  174.6 8.9 %copy-start.20 = (f32[16,512]{1,0:T(8,128)S(1)}, f32[16,512]{1,0:T(8,128)}, u32[]{:S(2)}) copy-start(f32[16,512]{1,0:T(8,128)} %param.36) | copy-start | bytes 98308
  176.2 36.7 %copy-start.25 = (f32[512]{0:T(512)S(1)}, f32[512]{0:T(512)}, u32[]{:S(2)}) copy-start(f32[512]{0:T(512)} %param.35) | copy-start | bytes 6148
  176.2 34.7 %all-to-all-start.3 = ((bf16[8,512,288]{1,2,0:T(8,128)(2,1)}), bf16[8,512,288]{1,2,0:T(8,128)(2,1)S(1)}, u32[]{:S(2)}, u32[]{:S(2)}) async-start(bf16[8,512,288]{1,2,0:T(8,128)(2,1)} %broadcast_in_dim.22), calls=%async_computation.3 | async-start | bytes 4718592 | tf_op jit(solution)/shard_map/all_to_all | solution.py:275
  211.3 0.8 copy-start.13
  212.9 3.3 %copy-start.5 = (f32[128,16,512]{2,1,0:T(8,128)S(1)}, f32[128,16,512]{2,1,0:T(8,128)}, u32[]{:S(2)}) copy-start(f32[128,16,512]{2,1,0:T(8,128)} %param.30) | copy-start | bytes 12582916
  216.2 37.1 %slice-start = ((s8[8388608]{0:T(1024)(128)(4,1)}), s8[4194304]{0:T(1024)(128)(4,1)S(1)}, s32[]{:S(2)}) async-start(s8[8388608]{0:T(1024)(128)(4,1)} %bitcast.106), calls=%async_computation.6 | async-start | bytes 8388608
  216.2 7.9 %copy-start.8 = (bf16[4,128,512]{2,1,0:T(8,128)(2,1)S(1)}, bf16[4,128,512]{2,1,0:T(8,128)(2,1)}, u32[]{:S(2)}) copy-start(bf16[4,128,512]{2,1,0:T(8,128)(2,1)} %get-tuple-element.58) | copy-start | bytes 1572868
  216.2 7.9 %copy-start.10 = (bf16[128,512]{1,0:T(8,128)(2,1)S(1)}, bf16[128,512]{1,0:T(8,128)(2,1)}, u32[]{:S(2)}) copy-start(bf16[128,512]{1,0:T(8,128)(2,1)} %copy-done.9) | copy-start | bytes 393220
  216.2 7.9 %copy-start.12 = (bf16[128,512]{1,0:T(8,128)(2,1)S(1)}, bf16[128,512]{1,0:T(8,128)(2,1)}, u32[]{:S(2)}) copy-start(bf16[128,512]{1,0:T(8,128)(2,1)} %copy-done.11) | copy-start | bytes 393220
  216.2 7.9 %copy-start.24 = (f32[512]{0:T(512)S(1)}, f32[512]{0:T(512)}, u32[]{:S(2)}) copy-start(f32[512]{0:T(512)} %param.37) | copy-start | bytes 6148
  216.2 37.1 %slice-start.1 = ((s8[8388608]{0:T(1024)(128)(4,1)}), s8[4194304]{0:T(1024)(128)(4,1)S(1)}, s32[]{:S(2)}) async-start(s8[8388608]{0:T(1024)(128)(4,1)} %bitcast.106), calls=%async_computation.7 | async-start | bytes 8388608
  224.6 32.3 %copy-start.7 = (bf16[128,4,512]{2,0,1:T(8,128)(2,1)S(1)}, bf16[128,4,512]{2,0,1:T(8,128)(2,1)}, u32[]{:S(2)}) copy-start(bf16[128,4,512]{2,0,1:T(8,128)(2,1)} %copy-done.6) | copy-start | bytes 1572868
  224.6 25.0 %collective-permute-start.17 = (bf16[512,512]{1,0:T(8,128)(2,1)S(1)}, bf16[512,512]{1,0:T(8,128)(2,1)S(1)}, u32[]{:S(2)}, u32[]{:S(2)}) collective-permute-start(bf16[512,512]{1,0:T(8,128)(2,1)S(1)} %pad_maximum_fusion.1.a0), channel_id=1, source_target_pairs={{0,1},{1,2},{2,3},{3,0},{4,5},{5,6},{6,7},{7,4},{8,9},{9,10},{10,1... | collective-permute-start | bytes 1572872 | tf_op jit(solution)/shard_map/ppermute | solution.py:53
  227.3 22.3 %collective-permute-start.16 = (bf16[512,512]{1,0:T(8,128)(2,1)S(1)}, bf16[512,512]{1,0:T(8,128)(2,1)S(1)}, u32[]{:S(2)}, u32[]{:S(2)}) collective-permute-start(bf16[512,512]{1,0:T(8,128)(2,1)S(1)} %pad_maximum_fusion.1.a0), channel_id=1, source_target_pairs={{0,2},{1,3},{2,0},{3,1},{4,6},{5,7},{6,4},{7,5},{8,10},{9,11},{10,... | collective-permute-start | bytes 1572872 | tf_op jit(solution)/shard_map/ppermute | solution.py:53
  227.7 25.6 %collective-permute-start.15 = (bf16[512,512]{1,0:T(8,128)(2,1)S(1)}, bf16[512,512]{1,0:T(8,128)(2,1)S(1)}, u32[]{:S(2)}, u32[]{:S(2)}) collective-permute-start(bf16[512,512]{1,0:T(8,128)(2,1)S(1)} %pad_maximum_fusion.1.a0), channel_id=1, source_target_pairs={{0,3},{1,0},{2,1},{3,2},{4,7},{5,4},{6,5},{7,6},{8,11},{9,8},{10,9... | collective-permute-start | bytes 1572872 | tf_op jit(solution)/shard_map/ppermute | solution.py:53
  256.3 15.4 %collective-permute-start.18 = (bf16[512,512]{1,0:T(8,128)(2,1)S(1)}, bf16[512,512]{1,0:T(8,128)(2,1)S(1)}, u32[]{:S(2)}, u32[]{:S(2)}) collective-permute-start(bf16[512,512]{1,0:T(8,128)(2,1)S(1)} %out_product.3), channel_id=1, source_target_pairs={{0,4},{1,5},{2,6},{3,7},{4,0},{5,1},{6,2},{7,3},{8,12},{9,13},{10,... | collective-permute-start | bytes 1572872 | tf_op jit(solution)/shard_map/ppermute | solution.py:57
Sparse Core Ops, SparseCore 0:
  28.0 54.2 all-gather.4
  84.6 58.9 all-gather.6

commit v2 on v1

--- a/solution.py
+++ b/solution.py
@@ -86,7 +86,7 @@
                 o_ref[...] = (acc[...] + total).astype(o_ref.dtype)
 
 
-def in_product(chunks, weights, column, x, dtype):
+def in_product(chunks, weights, matrix, column, x, dtype):
     tokens = chunks[0].shape[0]
     scalars = jnp.stack([column, x]).astype(jnp.int32)
     whole = pl.BlockSpec((tokens, 512), lambda k, s: (0, 0))
@@ -98,8 +98,8 @@
             grid=(4,),
             in_specs=[whole] * 4
             + [
-                pl.BlockSpec((2, 128, 512), lambda k, s: (lax.rem(s[1] + k, 4), 0, s[0])),
-                pl.BlockSpec((2, 128, 512), lambda k, s: (4 + lax.rem(s[1] + k, 4), 0, s[0])),
+                pl.BlockSpec((2, 128, 512), lambda k, s: (lax.rem(s[1] + k, 4), matrix, s[0])),
+                pl.BlockSpec((2, 128, 512), lambda k, s: (4 + lax.rem(s[1] + k, 4), matrix, s[0])),
             ],
             out_specs=whole,
             scratch_shapes=[pltpu.VMEM((tokens, 512), jnp.float32)],
@@ -143,7 +143,7 @@
 
     def where(k, s):
         source = lax.rem(s[1] + k, 4)
-        return (s[0], 2 + source // 2, lax.rem(source, 2))
+        return (s[0], source // 2, lax.rem(source, 2))
 
     return pl.pallas_call(
         out_product_kernel,
@@ -211,55 +211,52 @@
     out_new = adam_update(out_master, out_moment, out_velocity, out_grad)
     own = in_new.shape[0]
 
-    def route_in(matrix):
-        blocks = in_new[:, matrix, :].astype(bf16).reshape(own, 2, 4, 512)
-        got = []
-        for k in range(4):
-            piece = lax.dynamic_index_in_dim(blocks, (x + k) % 4, 2, keepdims=False)
-            got.append(lax.ppermute(piece.reshape(own, 1024), BOTH, in_route(k)))
-        stacked = jnp.stack(got)
-        return jnp.concatenate(
+    blocks = jnp.moveaxis(in_new.astype(bf16), 1, 0).reshape(2, own, 2, 4, 512)
+    pieces = [
+        lax.dynamic_index_in_dim(blocks, (x + k) % 4, 3, keepdims=False).reshape(2, own, 1024)
+        for k in range(4)
+    ]
+    *pieces, asked = lax.optimization_barrier((*pieces, asked))
+    stacked = jnp.stack([lax.ppermute(pieces[k], BOTH, in_route(k)) for k in range(4)])
+    weights_in = lax.all_gather(
+        jnp.concatenate(
             [lax.dynamic_index_in_dim(stacked, (x - source) % 4, 0, keepdims=False) for source in range(4)],
-            axis=0,
-        )
-
-    def route_out():
-        halves = out_new.astype(bf16).reshape(own, 2, 2048)
-        got = []
-        for j in range(2):
-            piece = lax.dynamic_index_in_dim(halves, (yh + j) % 2, 1, keepdims=False)
-            got.append(lax.ppermute(piece, BOTH, out_route(j)))
-        first = jnp.where(yh == 0, got[0], got[1])
-        second = jnp.where(yh == 0, got[1], got[0])
-        both = jnp.concatenate([first, second], axis=0)
-        return jnp.concatenate([both[:, :1024], both[:, 1024:]], axis=0)
-
-    weights_x = lax.all_gather(route_in(0), "fsdp", axis=0, tiled=False)
-    rest = jnp.concatenate([route_in(1), route_out()], axis=0)
-    weights_zo = lax.all_gather(rest, "fsdp", axis=0, tiled=False)
+            axis=1,
+        ).reshape(8 * own, 1024),
+        "fsdp",
+        axis=0,
+        tiled=False,
+    )
 
     offset = jnp.clip(asked - lax.axis_index("fsdp") * vocab_rows, 0, vocab_rows - 1)
     looked = embed_table.at[offset.reshape(-1)].get(mode="promise_in_bounds")
+    halves = out_new.astype(bf16).reshape(own, 2, 2048)
+    sent = [lax.dynamic_index_in_dim(halves, (yh + j) % 2, 1, keepdims=False) for j in range(2)]
+    *sent, looked = lax.optimization_barrier((*sent, looked))
+    got = [lax.ppermute(sent[j], BOTH, out_route(j)) for j in range(2)]
+    both = jnp.concatenate(
+        [jnp.where(yh == 0, got[0], got[1]), jnp.where(yh == 0, got[1], got[0])], axis=0
+    )
+    weights_out = lax.all_gather(
+        jnp.concatenate([both[:, :1024], both[:, 1024:]], axis=0), "fsdp", axis=0, tiled=False
+    )
     replies = lax.all_to_all(
         looked.reshape(replicas, capacity, feature_part), "fsdp", split_axis=0, concat_axis=0, tiled=True
     )
     found = replies.reshape(replicas * capacity, feature_part).at[place].get(mode="promise_in_bounds")
 
     chunks = [found] + [from_x(found, k) for k in (1, 2, 3)]
-    found_real = found.astype(f32)
-    squares = jnp.sum(found_real * found_real, axis=1).reshape(steps, rows)
-    everyone = lax.all_to_all(
-        jnp.broadcast_to(squares[None], (8, steps, rows)), "chan", 0, 0, tiled=True
-    )
-    scale = lax.rsqrt(everyone.sum(axis=0) / (8 * feature_part) + norm_eps)
-
-    def project(weights):
-        away = from_partner(in_product(chunks, weights, 1 - yh, x, bf16))
-        here = in_product(chunks, weights, yh, x, f32)
+    squares = sum(jnp.sum(jnp.square(c.astype(f32)), axis=1) for c in chunks).reshape(steps, rows)
+    total_squares = squares + from_partner(squares)
+    scale = lax.rsqrt(total_squares / (8 * feature_part) + norm_eps)
+
+    def project(parts, matrix):
+        away = from_partner(in_product(parts, weights_in, matrix, 1 - yh, x, bf16))
+        here = in_product(parts, weights_in, matrix, yh, x, f32)
         total = (here + away.astype(f32)).reshape(steps, rows, -1)
         return (total * scale[:, :, None]).astype(bf16)
 
-    x_in = project(weights_x)
+    x_in = project(chunks, 0)
 
     window = jnp.concatenate([conv_state, jnp.moveaxis(x_in, 0, 1)], axis=1)
     acts = []
@@ -272,12 +269,19 @@
     act = jnp.concatenate(acts, axis=0)
     contract_last = (((1,), (1,)), ((), ()))
     partial_value = lax.dot_general(act, x_proj_w, contract_last, preferred_element_type=f32).astype(bf16)
-    arrived = lax.all_to_all(
-        jnp.broadcast_to(partial_value[None], (8, *partial_value.shape)), "chan", 0, 0, tiled=True
-    )
-    dbc = arrived.astype(f32).sum(axis=0)
-
-    z_in = project(weights_zo)
+    partials = partial_value.reshape(steps, rows, -1)
+    *chunks_z, partials = lax.optimization_barrier((*chunks, partials))
+    mine = lax.dynamic_index_in_dim(partials, x, 0, keepdims=False).astype(f32)
+    for k in (1, 2, 3):
+        piece = lax.dynamic_index_in_dim(partials, (x - k) % 4, 0, keepdims=False)
+        mine = mine + from_x(piece, k).astype(f32)
+    mine = (mine + from_partner(mine.astype(bf16)).astype(f32)).astype(bf16)
+    shared = jnp.stack([mine] + [from_x(mine, k) for k in (1, 2, 3)])
+    dbc = jnp.concatenate(
+        [lax.dynamic_index_in_dim(shared, (s - x) % 4, 0, keepdims=False) for s in range(4)], axis=0
+    ).astype(f32)
+
+    z_in = project(chunks_z, 1)
 
     dt_low = dbc[:, :RANK].astype(bf16)
     delta_all = jax.nn.softplus(
@@ -300,8 +304,8 @@
     gated = jnp.concatenate(gates, axis=0)
 
     gated_chunks = [gated] + [from_x(gated, k) for k in (1, 2, 3)]
-    away = from_partner(out_product(gated_chunks, weights_zo, 1 - yh, x, bf16))
-    here = out_product(gated_chunks, weights_zo, yh, x, f32)
+    away = from_partner(out_product(gated_chunks, weights_out, 1 - yh, x, bf16))
+    here = out_product(gated_chunks, weights_out, yh, x, f32)
     block_out = (found.astype(f32) + (here + away.astype(f32))).astype(bf16).reshape(steps, rows, -1)
     return (in_new, out_new, block_out, window_state, state)
 

time: 280 us -> 264 us (0.943)
  starting transfers between devices: 66.5 us -> 54.5 us
  waiting for transfers between devices: 127 us -> 117 us
    all_to_all x2 -> x0, waiting for transfers between devices: 27.4 us -> none  [the longest x1 27.4 us: per_device(): lax.all_to_all(jnp.broadcast_to(partial_value[None], (8, *partial_value.s...]
    all_to_all x2 -> x0, starting transfers between devices: 16.9 us -> none  [the longest x1 9.62 us: per_device(): lax.all_to_all(jnp.broadcast_to(squares[None], (8, steps, rows)), 'chan',...]
    ppermute x10 -> x6, starting transfers between devices: 27.9 us -> 12.6 us  [the longest x2 8.95 us: per_device(): got = [lax.ppermute(sent[j], BOTH, out_route(j)) for j in range(2)]]
    ppermute x6 -> x12, waiting for transfers between devices: 37.6 us -> 52 us  [from_x(): lax.ppermute(a, 'chan', [(i, i // 4 * 4 + (i % 4 - k) % 4) for i in range...]
    all_to_all x1, waiting for transfers between devices: 22.5 us -> 12.4 us  [per_device(): lax.all_to_all(looked.reshape(replicas, capacity, feature_part), 'fsdp',...]
    ppermute x10 -> x6, waiting for transfers between devices: 11.9 us -> 21.8 us  [the longest x2 14.4 us: per_device(): got = [lax.ppermute(sent[j], BOTH, out_route(j)) for j in range(2)]]
    ppermute x3 -> x5, waiting for transfers between devices: 21.9 us -> 30.4 us  [from_partner(): return lax.ppermute(a, 'chan', [(i, i ^ 4) for i in range(8)])]
    ppermute x6 -> x12, starting transfers between devices: 7.32 us -> 14.4 us  [from_x(): lax.ppermute(a, 'chan', [(i, i // 4 * 4 + (i % 4 - k) % 4) for i in range...]
  transfers between devices with their start and end apart: 25 -> 27, of which waited for: 14 -> 17; matrix products, arithmetic and copies ran while one was open for 6% -> 17% of each run, Pallas kernels for 5% -> 6%
where the time goes in v2:
time: 264 us; the launch traced here: 261 us
  waiting for transfers between devices  117 us (44%)
  starting transfers between devices  54.5 us (21%)
  local copies, waits for them, and re-layouts  32.8 us (12%)
  other arithmetic  22.8 us (9%)
  Pallas kernels  17.3 us (7%)
  between operations  15.1 us (6%)
    ppermute x12, waiting for transfers between devices, from_x(): lax.ppermute(a, 'chan', [(i, i // 4 * 4 + (i % 4 - k) % 4) for i in range...  52 us
    ppermute x5, waiting for transfers between devices, from_partner(): return lax.ppermute(a, 'chan', [(i, i ^ 4) for i in range(8)])  30.4 us
    ppermute x12, starting transfers between devices, from_x(): lax.ppermute(a, 'chan', [(i, i // 4 * 4 + (i % 4 - k) % 4) for i in range...  14.4 us
    ppermute x2, waiting for transfers between devices, per_device(): got = [lax.ppermute(sent[j], BOTH, out_route(j)) for j in range(2)]  14.4 us
    all_to_all x1, waiting for transfers between devices, per_device(): lax.all_to_all(looked.reshape(replicas, capacity, feature_part), 'fsdp',...  12.4 us
    pallas_call x4, Pallas kernels, in_product(): pl.pallas_call(in_product_kernel, out_shape=jax.ShapeDtypeStruct((tokens,...  11.4 us
    unnamed x73, local copies, waits for them, and re-layouts  10.9 us
    all_to_all x1, starting transfers between devices, per_device(): lax.all_to_all(looked.reshape(replicas, capacity, feature_part), 'fsdp',...  10.5 us
  transfers between devices with their start and end apart: 27, of which 17 were waited for; matrix products, arithmetic and copies ran while one was open for 17% of the time, Pallas kernels for 6%

profile of v2, /device:TPU:6, one launch (start us, length us, event | category | flops | bytes accessed | tf_op | source)
XLA Modules:
  0.0 261.4 jit_solution(10225139390946278341)
XLA Ops:
  7.2 0.7 add_select_fusion
  8.4 0.7 sub.64
  9.1 6.4 %all-to-all-start = ((s32[16,1,64]{2,1,0:T(1,128)}), s32[16,1,64]{2,1,0:T(1,128)S(1)}, u32[]{:S(2)}, u32[]{:S(2)}) async-start(s32[16,1,64]{2,1,0:T(1,128)} %sub.64), calls=%async_computation | async-start | bytes 16384 | tf_op jit(solution)/shard_map/all_to_all | solution.py:206
  15.7 5.7 %convert_bitcast_fusion = (bf16[2,32,4096]{2,0,1:T(2,128)(2,1)S(1)}, f32[32,2,4096]{2,1,0:T(2,128)}) fusion(f32[32,2,4096]{2,1,0:T(2,128)} %param.19, f32[32,2,4096]{2,1,0:T(2,128)} %param.21, bf16[32,2,4096]{2,1,0:T(2,128)(2,1)} %param.22, f32[32,2,4096]{2,1,0:T(2,128)} %param.20), kind=kLoop, calls=%fused_computation.72 | loop fusion | flops 4456448 | bytes 5242880 | tf_op jit(solution)/shard_map/transpose | solution.py:214
  21.7 3.7 %dynamic-slice_reduce_fusion = (bf16[2,32,2,512]{3,2,0,1:T(2,128)(2,1)S(1)}, bf16[2,32,2,512]{3,2,0,1:T(2,128)(2,1)S(1)}, bf16[2,32,2,512]{3,2,0,1:T(2,128)(2,1)S(1)}, bf16[2,32,2,512]{3,2,0,1:T(2,128)(2,1)S(1)}) fusion(bf16[2,32,2,4,512]{4,3,2,0,1:T(4,128)(2,1)S(1)} %reshape.380, s32[]{:T(128)S(6)} %select_n.198, s32[]{:T(128)S(6)} %select_n.196, ...), kind=kLoop, calls=%fused_computation.124 | loop fusion | bytes 1048592 | tf_op jit(solution)/shard_map/jit(dynamic_index_in_dim)/dynamic_slice | solution.py:216
  27.1 2.4 collective-permute-start.5
  29.6 3.4 %collective-permute-done.4 = bf16[2,32,1024]{2,1,0:T(8,128)(2,1)S(1)} collective-permute-done((bf16[2,32,1024]{2,1,0:T(8,128)(2,1)S(1)}, bf16[2,32,1024]{2,1,0:T(8,128)(2,1)S(1)}, u32[]{:S(2)}, u32[]{:S(2)}) %collective-permute-start.4) | collective-permute-done | bytes 131104 | tf_op jit(solution)/shard_map/ppermute | solution.py:220
  33.0 2.0 collective-permute-done.5
  35.0 2.0 collective-permute-done.6
  37.1 0.8 pad_maximum_fusion.2
  38.1 1.2 fusion.64
  40.3 7.8 %gather_fusion = bf16[1024,512]{1,0:T(8,128)(2,1)} fusion(bf16[4096,512]{1,0:T(8,128)(2,1)} %param.27, s32[1024]{0:T(1024)S(1)} %broadcast_clamp_fusion), kind=kCustom, calls=%fused_computation | custom fusion | bytes 2101248 | tf_op jit(solution)/shard_map/gather | solution.py:232
  48.2 10.5 %all-to-all-start.1 = ((bf16[16,64,512]{2,1,0:T(8,128)(2,1)}), bf16[16,64,512]{2,1,0:T(8,128)(2,1)S(1)}, u32[]{:S(2)}, u32[]{:S(2)}) async-start(bf16[16,64,512]{2,1,0:T(8,128)(2,1)} %bitcast.4), calls=%async_computation.1 | async-start | bytes 2097152 | tf_op jit(solution)/shard_map/all_to_all | solution.py:243
  58.8 5.7 %collective-permute-start.20 = (bf16[32,2048]{1,0:T(8,128)(2,1)S(1)}, bf16[32,2048]{1,0:T(8,128)(2,1)S(1)}, u32[]{:S(2)}, u32[]{:S(2)}) collective-permute-start(bf16[32,2048]{1,0:T(8,128)(2,1)S(1)} %get-tuple-element.29), channel_id=1, source_target_pairs={{0,0},{1,16},{2,32},{3,48},{4,4},{5,20},{6,36},{7,52},{8,8},{9,24}... | collective-permute-start | bytes 393224 | tf_op jit(solution)/shard_map/ppermute | solution.py:236
  64.5 3.2 %collective-permute-start.21 = (bf16[32,2048]{1,0:T(8,128)(2,1)S(1)}, bf16[32,2048]{1,0:T(8,128)(2,1)S(1)}, u32[]{:S(2)}, u32[]{:S(2)}) collective-permute-start(bf16[32,2048]{1,0:T(8,128)(2,1)S(1)} %get-tuple-element.30), channel_id=1, source_target_pairs={{0,4},{1,20},{2,36},{3,52},{4,0},{5,16},{6,32},{7,48},{8,12},{9,28... | collective-permute-start | bytes 393224 | tf_op jit(solution)/shard_map/ppermute | solution.py:236
  67.7 11.0 %collective-permute-done.20 = bf16[32,2048]{1,0:T(8,128)(2,1)S(1)} collective-permute-done((bf16[32,2048]{1,0:T(8,128)(2,1)S(1)}, bf16[32,2048]{1,0:T(8,128)(2,1)S(1)}, u32[]{:S(2)}, u32[]{:S(2)}) %collective-permute-start.20) | collective-permute-done | bytes 131104 | tf_op jit(solution)/shard_map/ppermute | solution.py:236
  78.7 3.4 %collective-permute-done.21 = bf16[32,2048]{1,0:T(8,128)(2,1)S(1)} collective-permute-done((bf16[32,2048]{1,0:T(8,128)(2,1)S(1)}, bf16[32,2048]{1,0:T(8,128)(2,1)S(1)}, u32[]{:S(2)}, u32[]{:S(2)}) %collective-permute-start.21) | collective-permute-done | bytes 131104 | tf_op jit(solution)/shard_map/ppermute | solution.py:236
  82.2 0.7 fusion.53
  82.9 12.4 %all-to-all-done.1 = bf16[16,64,512]{2,1,0:T(8,128)(2,1)S(1)} async-done(((bf16[16,64,512]{2,1,0:T(8,128)(2,1)}), bf16[16,64,512]{2,1,0:T(8,128)(2,1)S(1)}, u32[]{:S(2)}, u32[]{:S(2)}) %all-to-all-start.1) | async-done | bytes 1048608 | tf_op jit(solution)/shard_map/all_to_all | solution.py:243
  95.3 2.0 gather_fusion.1
  97.3 4.8 %collective-permute-start.2 = (bf16[512,512]{1,0:T(8,128)(2,1)S(1)}, bf16[512,512]{1,0:T(8,128)(2,1)S(1)}, u32[]{:S(2)}, u32[]{:S(2)}) collective-permute-start(bf16[512,512]{1,0:T(8,128)(2,1)S(1)} %gather_fusion.1), channel_id=1, source_target_pairs={{0,1},{1,2},{2,3},{3,0},{4,5},{5,6},{6,7},{7,4},{8,9},{9,10},{10,1... | collective-permute-start | bytes 1572872 | tf_op jit(solution)/shard_map/ppermute | solution.py:53
  102.1 0.9 collective-permute-start
  103.3 21.3 %collective-permute-done.2.a3 = bf16[512,512]{1,0:T(8,128)(2,1)S(1)} collective-permute-done((bf16[512,512]{1,0:T(8,128)(2,1)S(1)}, bf16[512,512]{1,0:T(8,128)(2,1)S(1)}, u32[]{:S(2)}, u32[]{:S(2)}) %collective-permute-start.2) | collective-permute-done | bytes 524320 | tf_op jit(solution)/shard_map/ppermute | solution.py:53
  125.0 3.1 %collective-permute-done.a1 = bf16[512,512]{1,0:T(8,128)(2,1)S(1)} collective-permute-done((bf16[512,512]{1,0:T(8,128)(2,1)S(1)}, bf16[512,512]{1,0:T(8,128)(2,1)S(1)}, u32[]{:S(2)}, u32[]{:S(2)}) %collective-permute-start) | collective-permute-done | bytes 524320 | tf_op jit(solution)/shard_map/ppermute | solution.py:53
  128.3 3.5 %copy-done.2 = bf16[16,256,1024]{2,1,0:T(8,128)(2,1)S(1)} copy-done((bf16[16,256,1024]{2,1,0:T(8,128)(2,1)S(1)}, bf16[16,256,1024]{2,1,0:T(8,128)(2,1)}, u32[]{:S(2)}) %copy-start.2) | copy-done | bytes 8388632
  131.7 2.7 %in_product.5 = bf16[512,512]{1,0:T(8,128)(2,1)S(1)} custom-call(s32[2]{0:T(128)S(1)} %pad_add_fusion.1.s_ref, bf16[512,512]{1,0:T(8,128)(2,1)S(1)} %gather_fusion.1, bf16[512,512]{1,0:T(8,128)(2,1)S(1)} %collective-permute-done.a1, bf16[512,512]{1,0:T(8,128)(2,1)S(1)} %collective-permute-done.1.a2, bf16[512,512]{1,0:T(8,128)(2,1)S(1)} %collective-permute-done.2.a3, ...), custom_call_target="tpu_custom_call" | custom-call | flops 1073741824 | bytes 6291456 | tf_op jit(solution)/shard_map/in_product/pallas_call | solution.py:93
  134.4 2.3 collective-permute-start.7
  136.7 1.3 collective-permute-start.8
  138.1 23.0 %collective-permute-done.8 = f32[4,128]{1,0:T(4,128)S(1)} collective-permute-done((f32[4,128]{1,0:T(4,128)S(1)}, f32[4,128]{1,0:T(4,128)S(1)}, u32[]{:S(2)}, u32[]{:S(2)}) %collective-permute-start.8) | collective-permute-done | bytes 2080 | tf_op jit(solution)/shard_map/ppermute | solution.py:57
  161.1 2.7 %in_product.4 = f32[512,512]{1,0:T(8,128)S(1)} custom-call(s32[2]{0:T(128)S(1)} %pad_add_fusion.s_ref, bf16[512,512]{1,0:T(8,128)(2,1)S(1)} %gather_fusion.1, bf16[512,512]{1,0:T(8,128)(2,1)S(1)} %collective-permute-done.a1, bf16[512,512]{1,0:T(8,128)(2,1)S(1)} %collective-permute-done.1.a2, bf16[512,512]{1,0:T(8,128)(2,1)S(1)} %collective-permute-done.2.a3, ...), custom_call_target="tpu_custom_call" | custom-call | flops 1073741824 | bytes 6291456 | tf_op jit(solution)/shard_map/in_product/pallas_call | solution.py:93
  164.1 0.8 copy-done.8
  167.0 3.2 %collective-permute-start.11 = (bf16[128,288]{0,1:T(8,128)(2,1)S(1)}, bf16[128,288]{0,1:T(8,128)(2,1)S(1)}, u32[]{:S(2)}, u32[]{:S(2)}) collective-permute-start(bf16[128,288]{0,1:T(8,128)(2,1)S(1)} %get-tuple-element.81), channel_id=1, source_target_pairs={{0,1},{1,2},{2,3},{3,0},{4,5},{5,6},{6,7},{7,4},{8,9},{9,10},{10,1... | collective-permute-start | bytes 221192 | tf_op jit(solution)/shard_map/ppermute | solution.py:53
  170.3 3.0 %collective-permute-done.9 = bf16[128,288]{0,1:T(8,128)(2,1)S(1)} collective-permute-done((bf16[128,288]{0,1:T(8,128)(2,1)S(1)}, bf16[128,288]{0,1:T(8,128)(2,1)S(1)}, u32[]{:S(2)}, u32[]{:S(2)}) %collective-permute-start.9) | collective-permute-done | bytes 73760 | tf_op jit(solution)/shard_map/ppermute | solution.py:53
  173.3 2.7 %collective-permute-done.10 = bf16[128,288]{0,1:T(8,128)(2,1)S(1)} collective-permute-done((bf16[128,288]{0,1:T(8,128)(2,1)S(1)}, bf16[128,288]{0,1:T(8,128)(2,1)S(1)}, u32[]{:S(2)}, u32[]{:S(2)}) %collective-permute-start.10) | collective-permute-done | bytes 73760 | tf_op jit(solution)/shard_map/ppermute | solution.py:53
  176.1 2.7 %collective-permute-start.12 = (bf16[128,288]{0,1:T(8,128)(2,1)S(1)}, bf16[128,288]{0,1:T(8,128)(2,1)S(1)}, u32[]{:S(2)}, u32[]{:S(2)}) collective-permute-start(bf16[128,288]{0,1:T(8,128)(2,1)S(1)} %fusion.58), channel_id=1, source_target_pairs={{0,4},{1,5},{2,6},{3,7},{4,0},{5,1},{6,2},{7,3},{8,12},{9,13},{10,... | collective-permute-start | bytes 221192 | tf_op jit(solution)/shard_map/ppermute | solution.py:57
  178.8 3.4 %copy-done.4 = bf16[16,256,1024]{2,1,0:T(8,128)(2,1)S(1)} copy-done((bf16[16,256,1024]{2,1,0:T(8,128)(2,1)S(1)}, bf16[16,256,1024]{2,1,0:T(8,128)(2,1)}, u32[]{:S(2)}) %copy-start.4) | copy-done | bytes 8388632
  182.2 3.4 %in_product.7 = bf16[512,512]{1,0:T(8,128)(2,1)} custom-call(s32[2]{0:T(128)S(1)} %pad_add_fusion.1.s_ref, bf16[512,512]{1,0:T(8,128)(2,1)S(1)} %gather_fusion.1, bf16[512,512]{1,0:T(8,128)(2,1)S(1)} %collective-permute-done.a1, bf16[512,512]{1,0:T(8,128)(2,1)S(1)} %collective-permute-done.1.a2, bf16[512,512]{1,0:T(8,128)(2,1)S(1)} %collective-permute-done.2.a3, ...), custom_call_target="tpu_custom_call" | custom-call | flops 1073741824 | bytes 6291456 | tf_op jit(solution)/shard_map/in_product/pallas_call | solution.py:93
  185.7 0.9 collective-permute-start.16
  187.6 1.1 collective-permute-start.13
  188.7 2.7 %in_product.6 = f32[512,512]{1,0:T(8,128)S(1)} custom-call(s32[2]{0:T(128)S(1)} %pad_add_fusion.s_ref, bf16[512,512]{1,0:T(8,128)(2,1)S(1)} %gather_fusion.1, bf16[512,512]{1,0:T(8,128)(2,1)S(1)} %collective-permute-done.a1, bf16[512,512]{1,0:T(8,128)(2,1)S(1)} %collective-permute-done.1.a2, bf16[512,512]{1,0:T(8,128)(2,1)S(1)} %collective-permute-done.2.a3, ...), custom_call_target="tpu_custom_call" | custom-call | flops 1073741824 | bytes 6291456 | tf_op jit(solution)/shard_map/in_product/pallas_call | solution.py:93
  191.4 1.6 collective-permute-done.14
  193.0 0.8 collective-permute-done.13
  194.1 0.7 copy.87
  194.8 0.7 copy.86
  195.6 0.7 copy.85
  196.3 0.7 copy.84
  197.0 0.7 copy.83
  197.7 0.7 copy.82
  198.5 0.7 copy.81
  199.3 1.9 compare_select_fusion
  201.6 7.8 %multiply_reduce_fusion.2 = (f32[128,512]{1,0:T(8,128)S(1)}, f32[128,512]{1,0:T(8,128)S(1)}, f32[128,512]{1,0:T(8,128)S(1)}, f32[128,512]{1,0:T(8,128)S(1)}, f32[128,16,512]{2,1,0:T(8,128)}) fusion(f32[128,16]{1,0:T(8,128)S(1)} %copy-done.27, f32[128,16]{1,0:T(8,128)S(1)} %copy-done.26, f32[128,512]{1,0:T(8,128)S(1)} %get-tuple-element.52, ...), kind=kLoop, calls=%fused_computation.6 | loop fusion | flops 24903680 | bytes 11632640 | tf_op jit(solution)/shard_map/reduce_sum | solution.py:302
  209.4 1.2 convert_add_fusion.1
  211.3 2.0 collective-permute-start.19
  213.2 0.9 collective-permute-start.18
  214.5 11.2 %collective-permute-done.19.a3 = bf16[512,512]{1,0:T(8,128)(2,1)S(1)} collective-permute-done((bf16[512,512]{1,0:T(8,128)(2,1)S(1)}, bf16[512,512]{1,0:T(8,128)(2,1)S(1)}, u32[]{:S(2)}, u32[]{:S(2)}) %collective-permute-start.19) | collective-permute-done | bytes 524320 | tf_op jit(solution)/shard_map/ppermute | solution.py:53
  225.7 2.8 %collective-permute-done.18.a2 = bf16[512,512]{1,0:T(8,128)(2,1)S(1)} collective-permute-done((bf16[512,512]{1,0:T(8,128)(2,1)S(1)}, bf16[512,512]{1,0:T(8,128)(2,1)S(1)}, u32[]{:S(2)}, u32[]{:S(2)}) %collective-permute-start.18) | collective-permute-done | bytes 524320 | tf_op jit(solution)/shard_map/ppermute | solution.py:53
  228.5 5.5 %collective-permute-done.17.a1 = bf16[512,512]{1,0:T(8,128)(2,1)S(1)} collective-permute-done((bf16[512,512]{1,0:T(8,128)(2,1)S(1)}, bf16[512,512]{1,0:T(8,128)(2,1)S(1)}, u32[]{:S(2)}, u32[]{:S(2)}) %collective-permute-start.17) | collective-permute-done | bytes 524320 | tf_op jit(solution)/shard_map/ppermute | solution.py:53
  234.0 2.2 copy-done.6
  236.2 2.9 %out_product.3 = bf16[512,512]{1,0:T(8,128)(2,1)S(1)} custom-call(s32[2]{0:T(128)S(1)} %pad_add_fusion.1.s_ref, bf16[512,512]{1,0:T(8,128)(2,1)S(1)} %pad_maximum_fusion.3.a0, bf16[512,512]{1,0:T(8,128)(2,1)S(1)} %collective-permute-done.17.a1, bf16[512,512]{1,0:T(8,128)(2,1)S(1)} %collective-permute-done.18.a2, ...), custom_call_target="tpu_custom_call" | custom-call | flops 1073741824 | bytes 6291456 | tf_op jit(solution)/shard_map/out_product/pallas_call | solution.py:148
  239.1 3.3 %collective-permute-start.22 = (bf16[512,512]{1,0:T(8,128)(2,1)S(1)}, bf16[512,512]{1,0:T(8,128)(2,1)S(1)}, u32[]{:S(2)}, u32[]{:S(2)}) collective-permute-start(bf16[512,512]{1,0:T(8,128)(2,1)S(1)} %out_product.3), channel_id=1, source_target_pairs={{0,4},{1,5},{2,6},{3,7},{4,0},{5,1},{6,2},{7,3},{8,12},{9,13},{10,... | collective-permute-start | bytes 1572872 | tf_op jit(solution)/shard_map/ppermute | solution.py:57
  242.4 0.8 slice.142
  243.2 2.9 %out_product.2 = f32[512,512]{1,0:T(8,128)S(1)} custom-call(s32[2]{0:T(128)S(1)} %pad_add_fusion.s_ref, bf16[512,512]{1,0:T(8,128)(2,1)S(1)} %pad_maximum_fusion.3.a0, bf16[512,512]{1,0:T(8,128)(2,1)S(1)} %collective-permute-done.17.a1, bf16[512,512]{1,0:T(8,128)(2,1)S(1)} %collective-permute-done.18.a2, bf16[512,512]{1,0:T(8,128)(2,1)S(1)} %collective-permute-done.19.a3, ...), custom_call_target="tpu_custom_call" | custom-call | flops 1073741824 | bytes 6291456 | tf_op jit(solution)/shard_map/out_product/pallas_call | solution.py:148
  246.1 7.4 %collective-permute-done.22 = bf16[512,512]{1,0:T(8,128)(2,1)S(1)} collective-permute-done((bf16[512,512]{1,0:T(8,128)(2,1)S(1)}, bf16[512,512]{1,0:T(8,128)(2,1)S(1)}, u32[]{:S(2)}, u32[]{:S(2)}) %collective-permute-start.22) | collective-permute-done | bytes 524320 | tf_op jit(solution)/shard_map/ppermute | solution.py:57
  253.6 1.0 fusion.4
  (145 shorter events, 9.7 us)
Async XLA Ops:
  7.2 159.2 %copy-start = (bf16[288,512]{1,0:T(8,128)(2,1)S(1)}, bf16[288,512]{1,0:T(8,128)(2,1)}, u32[]{:S(2)}) copy-start(bf16[288,512]{1,0:T(8,128)(2,1)} %param.33) | copy-start | bytes 884740
  9.1 16.8 %all-to-all-start = ((s32[16,1,64]{2,1,0:T(1,128)}), s32[16,1,64]{2,1,0:T(1,128)S(1)}, u32[]{:S(2)}, u32[]{:S(2)}) async-start(s32[16,1,64]{2,1,0:T(1,128)} %sub.64), calls=%async_computation | async-start | bytes 16384 | tf_op jit(solution)/shard_map/all_to_all | solution.py:206
  15.5 112.7 %all-gather.4.cloned.1.call-start = ((), (), s32[]{:S(2)}) async-start(), calls=%async_computation.2 | async-start | bytes 8912896 | tf_op jit(solution)/shard_map/all_gather | solution.py:221
  21.3 16.7 %copy-start.18 = (f32[32,4096]{1,0:T(8,128)S(1)}, f32[32,4096]{1,0:T(8,128)}, u32[]{:S(2)}) copy-start(f32[32,4096]{1,0:T(8,128)} %param.23) | copy-start | bytes 1572868
  21.3 16.7 %copy-start.19 = (f32[32,4096]{1,0:T(8,128)S(1)}, f32[32,4096]{1,0:T(8,128)}, u32[]{:S(2)}) copy-start(f32[32,4096]{1,0:T(8,128)} %param.25) | copy-start | bytes 1572868
  21.3 16.7 %copy-start.20 = (f32[32,4096]{1,0:T(8,128)S(1)}, f32[32,4096]{1,0:T(8,128)}, u32[]{:S(2)}) copy-start(f32[32,4096]{1,0:T(8,128)} %param.24) | copy-start | bytes 1572868
  21.3 16.7 %copy-start.29 = (bf16[32,4096]{1,0:T(8,128)(2,1)S(1)}, bf16[32,4096]{1,0:T(8,128)(2,1)}, u32[]{:S(2)}) copy-start(bf16[32,4096]{1,0:T(8,128)(2,1)} %param.26) | copy-start | bytes 786436
  25.9 3.6 %collective-permute-start.3 = (bf16[2,32,1024]{2,1,0:T(8,128)(2,1)S(1)}, bf16[2,32,1024]{2,1,0:T(8,128)(2,1)S(1)}, u32[]{:S(2)}, u32[]{:S(2)}) collective-permute-start(bf16[2,32,1024]{2,1,0:T(8,128)(2,1)S(1)} %copy.94), channel_id=1, source_target_pairs={{0,0},{1,1},{2,2},{3,3},{4,64},{5,65},{6,66},{7,67},{8,8},{9,9},{1... | collective-permute-start | bytes 393224 | tf_op jit(solution)/shard_map/ppermute | solution.py:220
  26.6 6.4 %collective-permute-start.4 = (bf16[2,32,1024]{2,1,0:T(8,128)(2,1)S(1)}, bf16[2,32,1024]{2,1,0:T(8,128)(2,1)S(1)}, u32[]{:S(2)}, u32[]{:S(2)}) collective-permute-start(bf16[2,32,1024]{2,1,0:T(8,128)(2,1)S(1)} %copy.95), channel_id=1, source_target_pairs={{0,1},{1,2},{2,3},{3,0},{4,65},{5,66},{6,67},{7,64},{8,9},{9,10},{... | collective-permute-start | bytes 393224 | tf_op jit(solution)/shard_map/ppermute | solution.py:220
  27.1 7.8 %collective-permute-start.5 = (bf16[2,32,1024]{2,1,0:T(8,128)(2,1)S(1)}, bf16[2,32,1024]{2,1,0:T(8,128)(2,1)S(1)}, u32[]{:S(2)}, u32[]{:S(2)}) collective-permute-start(bf16[2,32,1024]{2,1,0:T(8,128)(2,1)S(1)} %copy.96), channel_id=1, source_target_pairs={{0,2},{1,3},{2,0},{3,1},{4,66},{5,67},{6,64},{7,65},{8,10},{9,11},... | collective-permute-start | bytes 393224 | tf_op jit(solution)/shard_map/ppermute | solution.py:220
  29.5 7.4 %collective-permute-start.6 = (bf16[2,32,1024]{2,1,0:T(8,128)(2,1)S(1)}, bf16[2,32,1024]{2,1,0:T(8,128)(2,1)S(1)}, u32[]{:S(2)}, u32[]{:S(2)}) collective-permute-start(bf16[2,32,1024]{2,1,0:T(8,128)(2,1)S(1)} %copy.97), channel_id=1, source_target_pairs={{0,3},{1,0},{2,1},{3,2},{4,67},{5,64},{6,65},{7,66},{8,11},{9,8},{... | collective-permute-start | bytes 393224 | tf_op jit(solution)/shard_map/ppermute | solution.py:220
  40.3 27.4 %copy-start.32 = (s32[4,128]{1,0:T(4,128)S(1)}, s32[4,128]{1,0:T(4,128)}, u32[]{:S(2)}) copy-start(s32[4,128]{1,0:T(4,128)} %param.28) | copy-start | bytes 6148
  48.2 47.2 %all-to-all-start.1 = ((bf16[16,64,512]{2,1,0:T(8,128)(2,1)}), bf16[16,64,512]{2,1,0:T(8,128)(2,1)S(1)}, u32[]{:S(2)}, u32[]{:S(2)}) async-start(bf16[16,64,512]{2,1,0:T(8,128)(2,1)} %bitcast.4), calls=%async_computation.1 | async-start | bytes 2097152 | tf_op jit(solution)/shard_map/all_to_all | solution.py:243
  58.7 155.8 %all-gather.6.cloned.1.call-start = ((), (), s32[]{:S(2)}) async-start(), calls=%async_computation.3 | async-start | bytes 4456448 | tf_op jit(solution)/shard_map/all_gather | solution.py:240
  58.8 20.0 %collective-permute-start.20 = (bf16[32,2048]{1,0:T(8,128)(2,1)S(1)}, bf16[32,2048]{1,0:T(8,128)(2,1)S(1)}, u32[]{:S(2)}, u32[]{:S(2)}) collective-permute-start(bf16[32,2048]{1,0:T(8,128)(2,1)S(1)} %get-tuple-element.29), channel_id=1, source_target_pairs={{0,0},{1,16},{2,32},{3,48},{4,4},{5,20},{6,36},{7,52},{8,8},{9,24}... | collective-permute-start | bytes 393224 | tf_op jit(solution)/shard_map/ppermute | solution.py:236
  64.5 17.6 %collective-permute-start.21 = (bf16[32,2048]{1,0:T(8,128)(2,1)S(1)}, bf16[32,2048]{1,0:T(8,128)(2,1)S(1)}, u32[]{:S(2)}, u32[]{:S(2)}) collective-permute-start(bf16[32,2048]{1,0:T(8,128)(2,1)S(1)} %get-tuple-element.30), channel_id=1, source_target_pairs={{0,4},{1,20},{2,36},{3,52},{4,0},{5,16},{6,32},{7,48},{8,12},{9,28... | collective-permute-start | bytes 393224 | tf_op jit(solution)/shard_map/ppermute | solution.py:236
  97.3 27.3 %collective-permute-start.2 = (bf16[512,512]{1,0:T(8,128)(2,1)S(1)}, bf16[512,512]{1,0:T(8,128)(2,1)S(1)}, u32[]{:S(2)}, u32[]{:S(2)}) collective-permute-start(bf16[512,512]{1,0:T(8,128)(2,1)S(1)} %gather_fusion.1), channel_id=1, source_target_pairs={{0,1},{1,2},{2,3},{3,0},{4,5},{5,6},{6,7},{7,4},{8,9},{9,10},{10,1... | collective-permute-start | bytes 1572872 | tf_op jit(solution)/shard_map/ppermute | solution.py:53
  102.1 22.7 %collective-permute-start.1 = (bf16[512,512]{1,0:T(8,128)(2,1)S(1)}, bf16[512,512]{1,0:T(8,128)(2,1)S(1)}, u32[]{:S(2)}, u32[]{:S(2)}) collective-permute-start(bf16[512,512]{1,0:T(8,128)(2,1)S(1)} %gather_fusion.1), channel_id=1, source_target_pairs={{0,2},{1,3},{2,0},{3,1},{4,6},{5,7},{6,4},{7,5},{8,10},{9,11},{10,... | collective-permute-start | bytes 1572872 | tf_op jit(solution)/shard_map/ppermute | solution.py:53
  102.1 25.9 %collective-permute-start = (bf16[512,512]{1,0:T(8,128)(2,1)S(1)}, bf16[512,512]{1,0:T(8,128)(2,1)S(1)}, u32[]{:S(2)}, u32[]{:S(2)}) collective-permute-start(bf16[512,512]{1,0:T(8,128)(2,1)S(1)} %gather_fusion.1), channel_id=1, source_target_pairs={{0,3},{1,0},{2,1},{3,2},{4,7},{5,4},{6,5},{7,6},{8,11},{9,8},{10,9... | collective-permute-start | bytes 1572872 | tf_op jit(solution)/shard_map/ppermute | solution.py:53
  128.2 3.5 %copy-start.2 = (bf16[16,256,1024]{2,1,0:T(8,128)(2,1)S(1)}, bf16[16,256,1024]{2,1,0:T(8,128)(2,1)}, u32[]{:S(2)}) copy-start(bf16[16,256,1024]{2,1,0:T(8,128)(2,1)} %all-gather.4.cloned.1.call-done.w0.w1) | copy-start | bytes 25165828
  131.7 29.3 %copy-start.3 = (bf16[16,256,1024]{2,1,0:T(8,128)(2,1)S(1)}, bf16[16,256,1024]{2,1,0:T(8,128)(2,1)}, u32[]{:S(2)}) copy-start(bf16[16,256,1024]{2,1,0:T(8,128)(2,1)} %all-gather.4.cloned.1.call-done.w0.w1) | copy-start | bytes 25165828
  134.4 29.4 %collective-permute-start.7 = (bf16[512,512]{1,0:T(8,128)(2,1)S(1)}, bf16[512,512]{1,0:T(8,128)(2,1)S(1)}, u32[]{:S(2)}, u32[]{:S(2)}) collective-permute-start(bf16[512,512]{1,0:T(8,128)(2,1)S(1)} %in_product.5), channel_id=1, source_target_pairs={{0,4},{1,5},{2,6},{3,7},{4,0},{5,1},{6,2},{7,3},{8,12},{9,13},{10,... | collective-permute-start | bytes 1572872 | tf_op jit(solution)/shard_map/ppermute | solution.py:57
  136.7 24.4 %collective-permute-start.8 = (f32[4,128]{1,0:T(4,128)S(1)}, f32[4,128]{1,0:T(4,128)S(1)}, u32[]{:S(2)}, u32[]{:S(2)}) collective-permute-start(f32[4,128]{1,0:T(4,128)S(1)} %add_bitcast_fusion), channel_id=1, source_target_pairs={{0,4},{1,5},{2,6},{3,7},{4,0},{5,1},{6,2},{7,3},{8,12},{9,13},{10,... | collective-permute-start | bytes 6152 | tf_op jit(solution)/shard_map/ppermute | solution.py:57
  163.7 1.2 copy-start.21
  163.7 1.2 copy-start.31
  163.8 1.5 copy-start.33
  164.1 0.8 copy-start.8
  164.9 5.3 %copy-start.30 = (f32[16,512]{1,0:T(8,128)S(1)}, f32[16,512]{1,0:T(8,128)}, u32[]{:S(2)}) copy-start(f32[16,512]{1,0:T(8,128)} %param.36) | copy-start | bytes 98308
  165.6 0.7 copy-start.10
  165.6 0.7 copy-start.12
  165.6 0.7 copy-start.14
  165.6 0.7 copy-start.16
  166.9 6.4 %collective-permute-start.9 = (bf16[128,288]{0,1:T(8,128)(2,1)S(1)}, bf16[128,288]{0,1:T(8,128)(2,1)S(1)}, u32[]{:S(2)}, u32[]{:S(2)}) collective-permute-start(bf16[128,288]{0,1:T(8,128)(2,1)S(1)} %get-tuple-element.80), channel_id=1, source_target_pairs={{0,3},{1,0},{2,1},{3,2},{4,7},{5,4},{6,5},{7,6},{8,11},{9,8},{10,9... | collective-permute-start | bytes 221192 | tf_op jit(solution)/shard_map/ppermute | solution.py:53
  167.0 6.3 %collective-permute-start.11 = (bf16[128,288]{0,1:T(8,128)(2,1)S(1)}, bf16[128,288]{0,1:T(8,128)(2,1)S(1)}, u32[]{:S(2)}, u32[]{:S(2)}) collective-permute-start(bf16[128,288]{0,1:T(8,128)(2,1)S(1)} %get-tuple-element.81), channel_id=1, source_target_pairs={{0,1},{1,2},{2,3},{3,0},{4,5},{5,6},{6,7},{7,4},{8,9},{9,10},{10,1... | collective-permute-start | bytes 221192 | tf_op jit(solution)/shard_map/ppermute | solution.py:53
  170.2 5.9 %collective-permute-start.10 = (bf16[128,288]{0,1:T(8,128)(2,1)S(1)}, bf16[128,288]{0,1:T(8,128)(2,1)S(1)}, u32[]{:S(2)}, u32[]{:S(2)}) collective-permute-start(bf16[128,288]{0,1:T(8,128)(2,1)S(1)} %get-tuple-element.82), channel_id=1, source_target_pairs={{0,2},{1,3},{2,0},{3,1},{4,6},{5,7},{6,4},{7,5},{8,10},{9,11},{10,... | collective-permute-start | bytes 221192 | tf_op jit(solution)/shard_map/ppermute | solution.py:53
  176.1 10.4 %collective-permute-start.12 = (bf16[128,288]{0,1:T(8,128)(2,1)S(1)}, bf16[128,288]{0,1:T(8,128)(2,1)S(1)}, u32[]{:S(2)}, u32[]{:S(2)}) collective-permute-start(bf16[128,288]{0,1:T(8,128)(2,1)S(1)} %fusion.58), channel_id=1, source_target_pairs={{0,4},{1,5},{2,6},{3,7},{4,0},{5,1},{6,2},{7,3},{8,12},{9,13},{10,... | collective-permute-start | bytes 221192 | tf_op jit(solution)/shard_map/ppermute | solution.py:57
  178.8 3.4 %copy-start.4 = (bf16[16,256,1024]{2,1,0:T(8,128)(2,1)S(1)}, bf16[16,256,1024]{2,1,0:T(8,128)(2,1)}, u32[]{:S(2)}) copy-start(bf16[16,256,1024]{2,1,0:T(8,128)(2,1)} %all-gather.4.cloned.1.call-done.w0.w1) | copy-start | bytes 25165828
  182.2 6.5 %copy-start.5 = (bf16[16,256,1024]{2,1,0:T(8,128)(2,1)S(1)}, bf16[16,256,1024]{2,1,0:T(8,128)(2,1)}, u32[]{:S(2)}) copy-start(bf16[16,256,1024]{2,1,0:T(8,128)(2,1)} %all-gather.4.cloned.1.call-done.w0.w1) | copy-start | bytes 25165828
  185.7 23.7 %collective-permute-start.16 = (bf16[512,512]{1,0:T(8,128)(2,1)}, bf16[512,512]{1,0:T(8,128)(2,1)}, u32[]{:S(2)}, u32[]{:S(2)}) collective-permute-start(bf16[512,512]{1,0:T(8,128)(2,1)} %in_product.7), channel_id=1, source_target_pairs={{0,4},{1,5},{2,6},{3,7},{4,0},{5,1},{6,2},{7,3},{8,12},{9,13},{10,... | collective-permute-start | bytes 1572872 | tf_op jit(solution)/shard_map/ppermute | solution.py:57
  186.6 12.7 %copy-start.35 = (f32[512]{0:T(512)S(1)}, f32[512]{0:T(512)}, u32[]{:S(2)}) copy-start(f32[512]{0:T(512)} %param.35) | copy-start | bytes 6148
  186.6 4.8 %collective-permute-start.15 = (bf16[128,288]{0,1:T(8,128)(2,1)S(1)}, bf16[128,288]{0,1:T(8,128)(2,1)S(1)}, u32[]{:S(2)}, u32[]{:S(2)}) collective-permute-start(bf16[128,288]{0,1:T(8,128)(2,1)S(1)} %add_convert_fusion), channel_id=1, source_target_pairs={{0,1},{1,2},{2,3},{3,0},{4,5},{5,6},{6,7},{7,4},{8,9},{9,10},{10,1... | collective-permute-start | bytes 221192 | tf_op jit(solution)/shard_map/ppermute | solution.py:53
  187.2 5.9 %collective-permute-start.14 = (bf16[128,288]{0,1:T(8,128)(2,1)S(1)}, bf16[128,288]{0,1:T(8,128)(2,1)S(1)}, u32[]{:S(2)}, u32[]{:S(2)}) collective-permute-start(bf16[128,288]{0,1:T(8,128)(2,1)S(1)} %add_convert_fusion), channel_id=1, source_target_pairs={{0,2},{1,3},{2,0},{3,1},{4,6},{5,7},{6,4},{7,5},{8,10},{9,11},{10,... | collective-permute-start | bytes 221192 | tf_op jit(solution)/shard_map/ppermute | solution.py:53
  187.6 6.2 %collective-permute-start.13 = (bf16[128,288]{0,1:T(8,128)(2,1)S(1)}, bf16[128,288]{0,1:T(8,128)(2,1)S(1)}, u32[]{:S(2)}, u32[]{:S(2)}) collective-permute-start(bf16[128,288]{0,1:T(8,128)(2,1)S(1)} %add_convert_fusion), channel_id=1, source_target_pairs={{0,3},{1,0},{2,1},{3,2},{4,7},{5,4},{6,5},{7,6},{8,11},{9,8},{10,9... | collective-permute-start | bytes 221192 | tf_op jit(solution)/shard_map/ppermute | solution.py:53
  191.4 9.8 %copy-start.11 = (bf16[128,512]{1,0:T(8,128)(2,1)S(1)}, bf16[128,512]{1,0:T(8,128)(2,1)}, u32[]{:S(2)}) copy-start(bf16[128,512]{1,0:T(8,128)(2,1)} %copy-done.10) | copy-start | bytes 393220
  191.4 9.8 %copy-start.13 = (bf16[128,512]{1,0:T(8,128)(2,1)S(1)}, bf16[128,512]{1,0:T(8,128)(2,1)}, u32[]{:S(2)}) copy-start(bf16[128,512]{1,0:T(8,128)(2,1)} %copy-done.12) | copy-start | bytes 393220
  191.4 9.8 %copy-start.15 = (bf16[128,512]{1,0:T(8,128)(2,1)S(1)}, bf16[128,512]{1,0:T(8,128)(2,1)}, u32[]{:S(2)}) copy-start(bf16[128,512]{1,0:T(8,128)(2,1)} %copy-done.14) | copy-start | bytes 393220
  191.4 9.8 %copy-start.17 = (bf16[128,512]{1,0:T(8,128)(2,1)S(1)}, bf16[128,512]{1,0:T(8,128)(2,1)}, u32[]{:S(2)}) copy-start(bf16[128,512]{1,0:T(8,128)(2,1)} %copy-done.16) | copy-start | bytes 393220
  199.2 2.3 copy-start.7
  199.2 2.3 copy-start.22
  199.2 2.3 copy-start.23
  199.2 2.3 copy-start.24
  199.2 2.3 copy-start.25
  199.2 2.3 copy-start.26
  199.2 2.3 copy-start.27
  199.2 2.3 copy-start.28
  209.4 1.4 copy-start.34
  211.2 31.2 %copy-start.9 = (bf16[128,4,512]{2,0,1:T(8,128)(2,1)S(1)}, bf16[128,4,512]{2,0,1:T(8,128)(2,1)}, u32[]{:S(2)}) copy-start(bf16[128,4,512]{2,0,1:T(8,128)(2,1)} %copy-done.8) | copy-start | bytes 1572868
  211.3 14.4 %collective-permute-start.19 = (bf16[512,512]{1,0:T(8,128)(2,1)S(1)}, bf16[512,512]{1,0:T(8,128)(2,1)S(1)}, u32[]{:S(2)}, u32[]{:S(2)}) collective-permute-start(bf16[512,512]{1,0:T(8,128)(2,1)S(1)} %pad_maximum_fusion.3.a0), channel_id=1, source_target_pairs={{0,1},{1,2},{2,3},{3,0},{4,5},{5,6},{6,7},{7,4},{8,9},{9,10},{10,1... | collective-permute-start | bytes 1572872 | tf_op jit(solution)/shard_map/ppermute | solution.py:53
  213.2 15.3 %collective-permute-start.18 = (bf16[512,512]{1,0:T(8,128)(2,1)S(1)}, bf16[512,512]{1,0:T(8,128)(2,1)S(1)}, u32[]{:S(2)}, u32[]{:S(2)}) collective-permute-start(bf16[512,512]{1,0:T(8,128)(2,1)S(1)} %pad_maximum_fusion.3.a0), channel_id=1, source_target_pairs={{0,2},{1,3},{2,0},{3,1},{4,6},{5,7},{6,4},{7,5},{8,10},{9,11},{10,... | collective-permute-start | bytes 1572872 | tf_op jit(solution)/shard_map/ppermute | solution.py:53
  214.1 19.8 %collective-permute-start.17 = (bf16[512,512]{1,0:T(8,128)(2,1)S(1)}, bf16[512,512]{1,0:T(8,128)(2,1)S(1)}, u32[]{:S(2)}, u32[]{:S(2)}) collective-permute-start(bf16[512,512]{1,0:T(8,128)(2,1)S(1)} %pad_maximum_fusion.3.a0), channel_id=1, source_target_pairs={{0,3},{1,0},{2,1},{3,2},{4,7},{5,4},{6,5},{7,6},{8,11},{9,8},{10,9... | collective-permute-start | bytes 1572872 | tf_op jit(solution)/shard_map/ppermute | solution.py:53
  234.0 2.2 copy-start.6
  239.1 14.5 %collective-permute-start.22 = (bf16[512,512]{1,0:T(8,128)(2,1)S(1)}, bf16[512,512]{1,0:T(8,128)(2,1)S(1)}, u32[]{:S(2)}, u32[]{:S(2)}) collective-permute-start(bf16[512,512]{1,0:T(8,128)(2,1)S(1)} %out_product.3), channel_id=1, source_target_pairs={{0,4},{1,5},{2,6},{3,7},{4,0},{5,1},{6,2},{7,3},{8,12},{9,13},{10,... | collective-permute-start | bytes 1572872 | tf_op jit(solution)/shard_map/ppermute | solution.py:57
  242.4 12.2 %copy-start.1 = (bf16[288,512]{1,0:T(8,128)(2,1)S(1)}, bf16[288,512]{1,0:T(8,128)(2,1)}, u32[]{:S(2)}) copy-start(bf16[288,512]{1,0:T(8,128)(2,1)} %param.33) | copy-start | bytes 884740
Sparse Core Ops, SparseCore 0:
  38.1 78.3 all-gather.3
  118.8 48.0 all-gather.5

commit v3 on v2

--- a/solution.py
+++ b/solution.py
@@ -21,6 +21,7 @@
 norm_eps = 1e-06
 
 BOTH = ("fsdp", "chan")
+PARTS = 1
 DEVICES = [
     (yl, z, co, yh, x)
     for yl in range(2)
@@ -35,11 +36,15 @@
     return (yl * 8 + z * 2 + co) * 8 + yh * 4 + x
 
 
-def in_route(k):
+def x_route(j, k):
     return [
-        (place_of(yl, z, co, yh, x), place_of(yh, z, co, yl, (x + k) % 4))
+        (place_of(yl, z, co, yh, x), place_of((yh + j) % 2, z, co, yl, (x + k) % 4))
         for yl, z, co, yh, x in DEVICES
     ]
+
+
+def z_route(k):
+    return x_route(0, k)
 
 
 def out_route(j):
@@ -51,6 +56,16 @@
 
 def from_x(a, k):
     return lax.ppermute(a, "chan", [(i, (i // 4) * 4 + (i % 4 - k) % 4) for i in range(8)])
+
+
+def from_z(a, k):
+    return lax.ppermute(
+        a, "fsdp", [(i, (i // 8) * 8 + (i // 2 % 4 - k) % 4 * 2 + i % 2) for i in range(16)]
+    )
+
+
+def from_other_core(a):
+    return lax.ppermute(a, "fsdp", [(i, i ^ 1) for i in range(16)])
 
 
 def from_partner(a):
@@ -63,6 +78,178 @@
     velocity = beta_second * velocity + (1.0 - beta_second) * gradient * gradient
     update = moment / bias_first / (jnp.sqrt(velocity / bias_second) + adam_eps)
     return master - learn_rate * (update + weight_decay * master)
+
+
+def adam_in_kernel(s_ref, master, moment, velocity, grad, new, send_x, send_z):
+    for matrix, send in enumerate((send_x, send_z)):
+        updated = adam_update(
+            master[:, matrix, :], moment[:, matrix, :], velocity[:, matrix, :], grad[:, matrix, :]
+        )
+        new[:, matrix, :] = updated
+        send[0] = updated.astype(send.dtype)
+
+
+def adam_in(master, moment, velocity, grad, x):
+    own = master.shape[0]
+    block = pl.BlockSpec((own, 2, 512), lambda i, s: (0, 0, i))
+    send = pl.BlockSpec((1, own, 512), lambda i, s: (lax.rem(lax.rem(i, 4) - s[0] + 4, 4), 0, i // 4))
+    return pl.pallas_call(
+        adam_in_kernel,
+        out_shape=(
+            jax.ShapeDtypeStruct(master.shape, jnp.float32),
+            jax.ShapeDtypeStruct((4, own, 1024), jnp.bfloat16),
+            jax.ShapeDtypeStruct((4, own, 1024), jnp.bfloat16),
+        ),
+        grid_spec=pltpu.PrefetchScalarGridSpec(
+            num_scalar_prefetch=1,
+            grid=(8,),
+            in_specs=[block] * 4,
+            out_specs=(block, send, send),
+        ),
+        cost_estimate=pl.CostEstimate(
+            flops=20 * master.size, bytes_accessed=20 * master.size, transcendentals=master.size
+        ),
+        name="adam_in",
+    )(x[None], master, moment, velocity, grad)
+
+
+def x_rows(s_ref, own_ref, other_ref):
+    x, yl, core = s_ref[1], s_ref[3], s_ref[4]
+    halves = []
+    for ref in (own_ref, other_ref):
+        parts = []
+        for yh in range(2):
+            for source in range(4):
+                at = lax.rem(yl - yh + 2, 2) * 4 + lax.rem(x - source + 4, 4)
+                parts.append(ref[0, at])
+        halves.append(jnp.concatenate(parts, axis=0))
+    first = jnp.where(core == 0, halves[0], halves[1])
+    second = jnp.where(core == 0, halves[1], halves[0])
+    return first, second
+
+
+def x_away_kernel(s_ref, a0, a1, a2, a3, own_ref, other_ref, o_ref, q_ref, acc, sq):
+    k = pl.program_id(0)
+    first, second = x_rows(s_ref, own_ref, other_ref)
+    for kk, a in enumerate((a0, a1, a2, a3)):
+
+        @pl.when(k == kk)
+        def _(kk=kk, a=a):
+            total = jnp.dot(a[:, :256], first, preferred_element_type=jnp.float32)
+            total = total + jnp.dot(a[:, 256:], second, preferred_element_type=jnp.float32)
+            real = a[...].astype(jnp.float32)
+            square = jnp.sum(real * real, axis=1, keepdims=True)
+            square = jnp.broadcast_to(square, sq.shape)
+            if kk == 0:
+                acc[...] = total
+                sq[...] = square
+            elif kk < 3:
+                acc[...] += total
+                sq[...] += square
+            else:
+                square = sq[...] + square
+                q_ref[...] = square
+                high = square.astype(jnp.bfloat16)
+                low = (square - high.astype(jnp.float32)).astype(jnp.bfloat16)
+                lane = lax.broadcasted_iota(jnp.int32, square.shape, 1)
+                o_ref[:, :512] = (acc[...] + total).astype(o_ref.dtype)
+                o_ref[:, 512:] = jnp.where(lane < 64, high.astype(jnp.float32), low.astype(jnp.float32)).astype(
+                    o_ref.dtype
+                )
+
+
+def x_here_kernel(s_ref, a0, a1, a2, a3, own_ref, other_ref, o_ref, acc):
+    k = pl.program_id(0)
+    first, second = x_rows(s_ref, own_ref, other_ref)
+    for kk, a in enumerate((a0, a1, a2, a3)):
+
+        @pl.when(k == kk)
+        def _(kk=kk, a=a):
+            total = jnp.dot(a[:, :256], first, preferred_element_type=jnp.float32)
+            total = total + jnp.dot(a[:, 256:], second, preferred_element_type=jnp.float32)
+            if kk == 0:
+                acc[...] = total
+            elif kk < 3:
+                acc[...] += total
+            else:
+                o_ref[...] = acc[...] + total
+
+
+def x_product(chunks, own, other, scalars, away):
+    tokens = chunks[0].shape[0]
+    whole = pl.BlockSpec((tokens, 512), lambda k, s: (0, 0))
+    weights = pl.BlockSpec((1, 8, 32, 512), lambda k, s: (lax.rem(s[1] + k - s[2] + 4, 4), 0, 0, s[0]))
+    scratch = [pltpu.VMEM((tokens, 512), jnp.float32)]
+    if away:
+        out_shape = (
+            jax.ShapeDtypeStruct((tokens, 640), jnp.bfloat16),
+            jax.ShapeDtypeStruct((tokens, 128), jnp.float32),
+        )
+        out_specs = (
+            pl.BlockSpec((tokens, 640), lambda k, s: (0, 0)),
+            pl.BlockSpec((tokens, 128), lambda k, s: (0, 0)),
+        )
+        scratch = scratch + [pltpu.VMEM((tokens, 128), jnp.float32)]
+    else:
+        out_shape = jax.ShapeDtypeStruct((tokens, 512), jnp.float32)
+        out_specs = whole
+    return pl.pallas_call(
+        x_away_kernel if away else x_here_kernel,
+        out_shape=out_shape,
+        grid_spec=pltpu.PrefetchScalarGridSpec(
+            num_scalar_prefetch=1,
+            grid=(4,),
+            in_specs=[whole] * 4 + [weights, weights],
+            out_specs=out_specs,
+            scratch_shapes=scratch,
+        ),
+        compiler_params=pltpu.CompilerParams(vmem_limit_bytes=24 * 2**20),
+        cost_estimate=pl.CostEstimate(
+            flops=2 * tokens * 2048 * 512, bytes_accessed=6 * 2**20, transcendentals=0
+        ),
+        name="x_away" if away else "x_here",
+    )(scalars, *chunks, own, other)
+
+
+def conv_kernel(here, away, own_sq, window, weight, bias, proj, act, window_new, partial, scale):
+    rows = window.shape[1]
+    steps = here.shape[0] // rows
+    sent = away[:, 512:].astype(jnp.float32)
+    squares = own_sq[:, :1] + sent[:, :1] + sent[:, 64:65]
+    factor = lax.rsqrt(squares / 4096.0 + norm_eps)
+    scale[...] = jnp.broadcast_to(factor, scale.shape)
+    taps = [window[t] for t in range(3)]
+    for step in range(steps):
+        at = slice(step * rows, (step + 1) * rows)
+        total = here[at, :] + away[at, :512].astype(jnp.float32)
+        taps.append((total * factor[at]).astype(jnp.bfloat16))
+        mixed = taps[step].astype(jnp.float32) * weight[0:1, :]
+        for t in range(1, 4):
+            mixed = mixed + taps[step + t].astype(jnp.float32) * weight[t : t + 1, :]
+        act[at, :] = jax.nn.silu(mixed + bias[...]).astype(jnp.bfloat16)
+    for t in range(3):
+        window_new[t] = taps[steps + t]
+    partial[...] = lax.dot_general(
+        act[...], proj[...], (((1,), (1,)), ((), ())), preferred_element_type=jnp.float32
+    ).astype(jnp.bfloat16)
+
+
+def conv(here, away, own_sq, window, weight, bias, proj):
+    tokens = here.shape[0]
+    return pl.pallas_call(
+        conv_kernel,
+        out_shape=(
+            jax.ShapeDtypeStruct((tokens, 512), jnp.bfloat16),
+            jax.ShapeDtypeStruct(window.shape, jnp.bfloat16),
+            jax.ShapeDtypeStruct((tokens, proj.shape[0]), jnp.bfloat16),
+            jax.ShapeDtypeStruct((tokens, 128), jnp.float32),
+        ),
+        compiler_params=pltpu.CompilerParams(vmem_limit_bytes=24 * 2**20),
+        cost_estimate=pl.CostEstimate(
+            flops=2 * tokens * 288 * 512, bytes_accessed=4 * 2**20, transcendentals=tokens * 512
+        ),
+        name="conv",
+    )(here, away, own_sq, window, weight, bias, proj)
 
 
 def in_product_kernel(s_ref, a0, a1, a2, a3, w0, w1, o_ref, acc):
@@ -143,7 +330,7 @@
 
     def where(k, s):
         source = lax.rem(s[1] + k, 4)
-        return (s[0], source // 2, lax.rem(source, 2))
+        return (s[0], 2 + source // 2, lax.rem(source, 2))
 
     return pl.pallas_call(
         out_product_kernel,
@@ -207,107 +394,97 @@
         requests.reshape(replicas, capacity), "fsdp", split_axis=0, concat_axis=0, tiled=True
     )
 
-    in_new = adam_update(in_master, in_moment, in_velocity, in_grad)
+    fsdp = lax.axis_index("fsdp")
+    yl, z, core = fsdp // 8, fsdp // 2 % 4, fsdp % 2
+    own = in_master.shape[0]
+    in_master, requests = lax.optimization_barrier((in_master, requests))
+    in_new, pieces_x, pieces_z = adam_in(in_master, in_moment, in_velocity, in_grad, x)
+    rows_x = jnp.stack([lax.ppermute(pieces_x[k], BOTH, x_route(j, k)) for j in range(2) for k in range(4)])
+
     out_new = adam_update(out_master, out_moment, out_velocity, out_grad)
-    own = in_new.shape[0]
-
-    blocks = jnp.moveaxis(in_new.astype(bf16), 1, 0).reshape(2, own, 2, 4, 512)
-    pieces = [
-        lax.dynamic_index_in_dim(blocks, (x + k) % 4, 3, keepdims=False).reshape(2, own, 1024)
-        for k in range(4)
-    ]
-    *pieces, asked = lax.optimization_barrier((*pieces, asked))
-    stacked = jnp.stack([lax.ppermute(pieces[k], BOTH, in_route(k)) for k in range(4)])
-    weights_in = lax.all_gather(
-        jnp.concatenate(
-            [lax.dynamic_index_in_dim(stacked, (x - source) % 4, 0, keepdims=False) for source in range(4)],
-            axis=1,
-        ).reshape(8 * own, 1024),
-        "fsdp",
-        axis=0,
-        tiled=False,
-    )
-
-    offset = jnp.clip(asked - lax.axis_index("fsdp") * vocab_rows, 0, vocab_rows - 1)
-    looked = embed_table.at[offset.reshape(-1)].get(mode="promise_in_bounds")
     halves = out_new.astype(bf16).reshape(own, 2, 2048)
     sent = [lax.dynamic_index_in_dim(halves, (yh + j) % 2, 1, keepdims=False) for j in range(2)]
-    *sent, looked = lax.optimization_barrier((*sent, looked))
+    rows_x, pieces_z, *sent, asked = lax.optimization_barrier((rows_x, pieces_z, *sent, asked))
+
+    same_core = jnp.stack([rows_x] + [from_z(rows_x, k) for k in (1, 2, 3)])
+    other_core = from_other_core(same_core)
+
+    stacked = jnp.stack([lax.ppermute(pieces_z[k], BOTH, z_route(k)) for k in range(4)])
+    rows_z = [lax.dynamic_index_in_dim(stacked, (x - source) % 4, 0, keepdims=False) for source in range(4)]
     got = [lax.ppermute(sent[j], BOTH, out_route(j)) for j in range(2)]
     both = jnp.concatenate(
         [jnp.where(yh == 0, got[0], got[1]), jnp.where(yh == 0, got[1], got[0])], axis=0
     )
-    weights_out = lax.all_gather(
-        jnp.concatenate([both[:, :1024], both[:, 1024:]], axis=0), "fsdp", axis=0, tiled=False
-    )
+    weights_zo = lax.all_gather(
+        jnp.concatenate(rows_z + [both[:, :1024], both[:, 1024:]], axis=0), "fsdp", axis=0, tiled=False
+    )
+
+    offset = jnp.clip(asked - fsdp * vocab_rows, 0, vocab_rows - 1)
+    looked = embed_table.at[offset.reshape(-1)].get(mode="promise_in_bounds")
     replies = lax.all_to_all(
         looked.reshape(replicas, capacity, feature_part), "fsdp", split_axis=0, concat_axis=0, tiled=True
     )
     found = replies.reshape(replicas * capacity, feature_part).at[place].get(mode="promise_in_bounds")
 
-    chunks = [found] + [from_x(found, k) for k in (1, 2, 3)]
-    squares = sum(jnp.sum(jnp.square(c.astype(f32)), axis=1) for c in chunks).reshape(steps, rows)
-    total_squares = squares + from_partner(squares)
-    scale = lax.rsqrt(total_squares / (8 * feature_part) + norm_eps)
-
-    def project(parts, matrix):
-        away = from_partner(in_product(parts, weights_in, matrix, 1 - yh, x, bf16))
-        here = in_product(parts, weights_in, matrix, yh, x, f32)
-        total = (here + away.astype(f32)).reshape(steps, rows, -1)
-        return (total * scale[:, :, None]).astype(bf16)
-
-    x_in = project(chunks, 0)
-
-    window = jnp.concatenate([conv_state, jnp.moveaxis(x_in, 0, 1)], axis=1)
-    acts = []
-    for step in range(steps):
-        mixed_conv = (
-            jnp.sum(window[:, step : step + 4].astype(f32) * conv_weight[None], axis=1) + conv_bias
+    decay = -jnp.exp(a_log)
+    contract_last = (((1,), (1,)), ((), ()))
+    state = ssm_state
+    window = jnp.moveaxis(conv_state, 1, 0)
+    scalars = jnp.stack([yh, x, z, yl, core]).astype(jnp.int32)
+    scalars_away = jnp.stack([1 - yh, x, z, yl, core]).astype(jnp.int32)
+    outs = []
+    part_steps = steps // PARTS
+    for part in range(PARTS):
+        mine = found[part * part_steps * rows : (part + 1) * part_steps * rows]
+        chunks = [mine] + [from_x(mine, k) for k in (1, 2, 3)]
+        away, squares = x_product(chunks, same_core, other_core, scalars_away, True)
+        away = from_partner(away)
+        here = x_product(chunks, same_core, other_core, scalars, False)
+        act, window, partial_value, scale = conv(
+            here, away, squares, window, conv_weight, conv_bias[None], x_proj_w
         )
-        acts.append(jax.nn.silu(mixed_conv).astype(bf16))
-    window_state = window[:, steps:, :]
-    act = jnp.concatenate(acts, axis=0)
-    contract_last = (((1,), (1,)), ((), ()))
-    partial_value = lax.dot_general(act, x_proj_w, contract_last, preferred_element_type=f32).astype(bf16)
-    partials = partial_value.reshape(steps, rows, -1)
-    *chunks_z, partials = lax.optimization_barrier((*chunks, partials))
-    mine = lax.dynamic_index_in_dim(partials, x, 0, keepdims=False).astype(f32)
-    for k in (1, 2, 3):
-        piece = lax.dynamic_index_in_dim(partials, (x - k) % 4, 0, keepdims=False)
-        mine = mine + from_x(piece, k).astype(f32)
-    mine = (mine + from_partner(mine.astype(bf16)).astype(f32)).astype(bf16)
-    shared = jnp.stack([mine] + [from_x(mine, k) for k in (1, 2, 3)])
-    dbc = jnp.concatenate(
-        [lax.dynamic_index_in_dim(shared, (s - x) % 4, 0, keepdims=False) for s in range(4)], axis=0
-    ).astype(f32)
-
-    z_in = project(chunks_z, 1)
-
-    dt_low = dbc[:, :RANK].astype(bf16)
-    delta_all = jax.nn.softplus(
-        lax.dot_general(dt_low, dt_proj_w, contract_last, preferred_element_type=f32) + dt_bias
-    ).reshape(steps, rows, -1)
-    b_all = dbc[:, RANK : RANK + NSTATE].reshape(steps, rows, NSTATE)
-    c_all = dbc[:, RANK + NSTATE :].reshape(steps, rows, NSTATE)
-    decay = -jnp.exp(a_log)
-    state = ssm_state
-    gates = []
-    for step in range(steps):
-        delta = delta_all[step]
-        act_real = acts[step].astype(f32)
-        state = (
-            jnp.exp(delta[:, None, :] * decay[None]) * state
-            + (delta * act_real)[:, None, :] * b_all[step][:, :, None]
+
+        partials = partial_value.reshape(4, -1, partial_value.shape[1])
+        *chunks, partials = lax.optimization_barrier((*chunks, partials))
+        quarter = lax.dynamic_index_in_dim(partials, x, 0, keepdims=False).astype(f32)
+        for k in (1, 2, 3):
+            piece = lax.dynamic_index_in_dim(partials, (x - k) % 4, 0, keepdims=False)
+            quarter = quarter + from_x(piece, k).astype(f32)
+        quarter = (quarter + from_partner(quarter.astype(bf16)).astype(f32)).astype(bf16)
+        shared = jnp.stack([quarter] + [from_x(quarter, k) for k in (1, 2, 3)])
+        dbc = jnp.concatenate(
+            [lax.dynamic_index_in_dim(shared, (q - x) % 4, 0, keepdims=False) for q in range(4)], axis=0
+        ).astype(f32)
+
+        z_away = from_partner(in_product(chunks, weights_zo, 0, 1 - yh, x, bf16))
+        z_here = in_product(chunks, weights_zo, 0, yh, x, f32)
+        z_in = ((z_here + z_away.astype(f32)) * scale[:, :1]).astype(bf16)
+
+        dt_low = dbc[:, :RANK].astype(bf16)
+        delta_all = jax.nn.softplus(
+            lax.dot_general(dt_low, dt_proj_w, contract_last, preferred_element_type=f32) + dt_bias
         )
-        y_out = jnp.sum(c_all[step][:, :, None] * state, axis=1) + d_skip * act_real
-        gates.append((y_out * jax.nn.silu(z_in[step].astype(f32))).astype(bf16))
-    gated = jnp.concatenate(gates, axis=0)
-
-    gated_chunks = [gated] + [from_x(gated, k) for k in (1, 2, 3)]
-    away = from_partner(out_product(gated_chunks, weights_out, 1 - yh, x, bf16))
-    here = out_product(gated_chunks, weights_out, yh, x, f32)
-    block_out = (found.astype(f32) + (here + away.astype(f32))).astype(bf16).reshape(steps, rows, -1)
-    return (in_new, out_new, block_out, window_state, state)
+        gates = []
+        for step in range(part_steps):
+            at = slice(step * rows, (step + 1) * rows)
+            delta = delta_all[at]
+            b_mat = dbc[at, RANK : RANK + NSTATE]
+            c_mat = dbc[at, RANK + NSTATE :]
+            act_real = act[at].astype(f32)
+            state = (
+                jnp.exp(delta[:, None, :] * decay[None]) * state
+                + (delta * act_real)[:, None, :] * b_mat[:, :, None]
+            )
+            y_out = jnp.sum(c_mat[:, :, None] * state, axis=1) + d_skip * act_real
+            gates.append((y_out * jax.nn.silu(z_in[at].astype(f32))).astype(bf16))
+        gated = jnp.concatenate(gates, axis=0)
+
+        gated_chunks = [gated] + [from_x(gated, k) for k in (1, 2, 3)]
+        away = from_partner(out_product(gated_chunks, weights_zo, 1 - yh, x, bf16))
+        here = out_product(gated_chunks, weights_zo, yh, x, f32)
+        block = (mine.astype(f32) + (here + away.astype(f32))).astype(bf16)
+        outs.append(block.reshape(part_steps, rows, -1))
+    return (in_new, out_new, jnp.concatenate(outs, axis=0), jnp.moveaxis(window, 0, 1), state)
 
 
 def solution(mesh):

time: 264 us -> 305 us (1.16)
  waiting for transfers between devices: 117 us -> 148 us
  starting transfers between devices: 54.5 us -> 71 us
  Pallas kernels: 17.3 us -> 33.8 us
  local copies, waits for them, and re-layouts: 32.8 us -> 21.1 us
  other arithmetic: 22.8 us -> 14.8 us
    ppermute x4 -> x16, waiting for transfers between devices: 7.44 us -> 41.9 us  [the longest x3 33.8 us: from_z(): lax.ppermute(a, 'fsdp', [(i, i // 8 * 8 + (i // 2 % 4 - k) % 4 * 2 + i %...]
    ppermute x4 -> x16, starting transfers between devices: 3.64 us -> 27.8 us  [the longest x8 18.7 us: per_device(): lax.ppermute(pieces_x[k], BOTH, x_route(j, k))]
    pallas_call x0 -> x4, Pallas kernels: none -> 19.9 us  [the longest x2 9.87 us: x_product(): pl.pallas_call(x_away_kernel if away else x_here_kernel, out_shape=out_sh...]
    ppermute x2, waiting for transfers between devices: 14.4 us -> 6.9 us  [per_device(): got = [lax.ppermute(sent[j], BOTH, out_route(j)) for j in range(2)]]
    ppermute x5 -> x4, starting transfers between devices: 10.5 us -> 4.62 us  [from_partner(): return lax.ppermute(a, 'chan', [(i, i ^ 4) for i in range(8)])]
    transpose x2 -> x0, other arithmetic: 5.81 us -> none  [the longest x1 5.67 us: per_device(): blocks = jnp.moveaxis(in_new.astype(bf16), 1, 0).reshape(2, own, 2, 4, 512)]
    slice x10 -> x2, local copies, waits for them, and re-layouts: 5.98 us -> 0.96 us  [the longest x1 0.82 us: per_device(): c_mat = dbc[at, RANK + NSTATE:]]
    all_to_all x1, waiting for transfers between devices: 12.4 us -> 17.4 us  [per_device(): lax.all_to_all(looked.reshape(replicas, capacity, feature_part), 'fsdp',...]
  transfers between devices with their start and end apart: 27 -> 37, of which waited for: 17 -> 21; matrix products, arithmetic and copies ran while one was open for 17% -> 9% of each run, Pallas kernels for 6% -> 6%
where the time goes in v3:
time: 305 us
  waiting for transfers between devices  148 us (49%)
  starting transfers between devices  71 us (23%)
  Pallas kernels  33.8 us (11%)
  local copies, waits for them, and re-layouts  21.1 us (7%)
  other arithmetic  14.8 us (5%)
  between operations  14.8 us (5%)
    ppermute x12, waiting for transfers between devices, from_x(): lax.ppermute(a, 'chan', [(i, i // 4 * 4 + (i % 4 - k) % 4) for i in range...  56.4 us
    ppermute x3, waiting for transfers between devices, from_z(): lax.ppermute(a, 'fsdp', [(i, i // 8 * 8 + (i // 2 % 4 - k) % 4 * 2 + i %...  33.8 us
    ppermute x4, waiting for transfers between devices, from_partner(): return lax.ppermute(a, 'chan', [(i, i ^ 4) for i in range(8)])  25.7 us
    ppermute x8, starting transfers between devices, per_device(): lax.ppermute(pieces_x[k], BOTH, x_route(j, k))  18.7 us
    all_to_all x1, waiting for transfers between devices, per_device(): lax.all_to_all(looked.reshape(replicas, capacity, feature_part), 'fsdp',...  17.4 us
    ppermute x12, starting transfers between devices, from_x(): lax.ppermute(a, 'chan', [(i, i // 4 * 4 + (i % 4 - k) % 4) for i in range...  15 us
    ppermute x2, starting transfers between devices, per_device(): got = [lax.ppermute(sent[j], BOTH, out_route(j)) for j in range(2)]  10.3 us
    pallas_call x2, Pallas kernels, x_product(): pl.pallas_call(x_away_kernel if away else x_here_kernel, out_shape=out_sh...  9.87 us
  transfers between devices with their start and end apart: 37, of which 21 were waited for; matrix products, arithmetic and copies ran while one was open for 9% of the time, Pallas kernels for 6%

profile of v3, /device:TPU:6, one launch (start us, length us, event | category | flops | bytes accessed | tf_op | source)
XLA Modules:
  0.0 304.6 jit_solution(17100042174860376563)
XLA Ops:
  7.2 7.4 %adam_in.1 = (f32[32,2,4096]{2,1,0:T(2,128)}, bf16[4,32,1024]{2,1,0:T(8,128)(2,1)}, bf16[4,32,1024]{2,1,0:T(8,128)(2,1)}) custom-call(s32[1]{0:T(128)} %bitcast.s_ref, f32[32,2,4096]{2,1,0:T(2,128)} %master, f32[32,2,4096]{2,1,0:T(2,128)} %moment.1, f32[32,2,4096]{2,1,0:T(2,128)} %velocity.1, bf16[32,2,4096]{2,1,0:T(2,128)(2,1)} %grad.1), custom_call_target="tpu_custom_call" | custom-call | flops 5242880 | bytes 5242880 | tf_op jit(solution)/shard_map/adam_in/pallas_call | solution.py:96
  14.6 1.0 slice_bitcast_fusion.4
  15.6 1.9 collective-permute-start.7
  18.1 4.1 %collective-permute-start.6 = (bf16[32,1024]{1,0:T(8,128)(2,1)S(1)}, bf16[32,1024]{1,0:T(8,128)(2,1)S(1)}, u32[]{:S(2)}, u32[]{:S(2)}) collective-permute-start(bf16[32,1024]{1,0:T(8,128)(2,1)S(1)} %get-tuple-element.90), channel_id=1, source_target_pairs={{0,66},{1,67},{2,64},{3,65},{4,2},{5,3},{6,0},{7,1},{8,74},{9,75},... | collective-permute-start | bytes 196616 | tf_op jit(solution)/shard_map/ppermute | solution.py:402
  23.3 0.7 sub.66
  24.0 6.7 %all-to-all-start = ((s32[16,1,64]{2,1,0:T(1,128)}), s32[16,1,64]{2,1,0:T(1,128)S(1)}, u32[]{:S(2)}, u32[]{:S(2)}) async-start(s32[16,1,64]{2,1,0:T(1,128)} %sub.66), calls=%async_computation | async-start | bytes 16384 | tf_op jit(solution)/shard_map/all_to_all | solution.py:393
  31.5 1.2 fusion.46
  33.6 2.1 collective-permute-start.1
  35.7 2.4 collective-permute-done.1
  38.1 8.6 %collective-permute-start.5 = (bf16[32,1024]{1,0:T(8,128)(2,1)S(1)}, bf16[32,1024]{1,0:T(8,128)(2,1)S(1)}, u32[]{:S(2)}, u32[]{:S(2)}) collective-permute-start(bf16[32,1024]{1,0:T(8,128)(2,1)S(1)} %get-tuple-element.91), channel_id=1, source_target_pairs={{0,65},{1,66},{2,67},{3,64},{4,1},{5,2},{6,3},{7,0},{8,73},{9,74},... | collective-permute-start | bytes 196616 | tf_op jit(solution)/shard_map/ppermute | solution.py:402
  46.9 5.7 %collective-permute-done.4 = bf16[32,1024]{1,0:T(8,128)(2,1)S(1)} collective-permute-done((bf16[32,1024]{1,0:T(8,128)(2,1)S(1)}, bf16[32,1024]{1,0:T(8,128)(2,1)S(1)}, u32[]{:S(2)}, u32[]{:S(2)}) %collective-permute-start.4) | collective-permute-done | bytes 65568 | tf_op jit(solution)/shard_map/ppermute | solution.py:402
  53.5 1.3 collective-permute-start.25
  54.8 1.9 collective-permute-start.24
  56.7 5.3 %collective-permute-start.27 = (bf16[32,2048]{1,0:T(8,128)(2,1)S(1)}, bf16[32,2048]{1,0:T(8,128)(2,1)S(1)}, u32[]{:S(2)}, u32[]{:S(2)}) collective-permute-start(bf16[32,2048]{1,0:T(8,128)(2,1)S(1)} %get-tuple-element.39), channel_id=1, source_target_pairs={{0,0},{1,16},{2,32},{3,48},{4,4},{5,20},{6,36},{7,52},{8,8},{9,24}... | collective-permute-start | bytes 393224 | tf_op jit(solution)/shard_map/ppermute | solution.py:414
  62.0 5.0 %collective-permute-start.28 = (bf16[32,2048]{1,0:T(8,128)(2,1)S(1)}, bf16[32,2048]{1,0:T(8,128)(2,1)S(1)}, u32[]{:S(2)}, u32[]{:S(2)}) collective-permute-start(bf16[32,2048]{1,0:T(8,128)(2,1)S(1)} %get-tuple-element.40), channel_id=1, source_target_pairs={{0,4},{1,20},{2,36},{3,52},{4,0},{5,16},{6,32},{7,48},{8,12},{9,28... | collective-permute-start | bytes 393224 | tf_op jit(solution)/shard_map/ppermute | solution.py:414
  67.1 2.1 collective-permute-done.27
  69.2 4.8 %collective-permute-done.28 = bf16[32,2048]{1,0:T(8,128)(2,1)S(1)} collective-permute-done((bf16[32,2048]{1,0:T(8,128)(2,1)S(1)}, bf16[32,2048]{1,0:T(8,128)(2,1)S(1)}, u32[]{:S(2)}, u32[]{:S(2)}) %collective-permute-start.28) | collective-permute-done | bytes 131104 | tf_op jit(solution)/shard_map/ppermute | solution.py:414
  74.1 0.8 copy-done.12
  74.9 2.3 collective-permute-start.13
  77.3 2.8 collective-permute-start.11
  80.0 15.0 %collective-permute-done.13 = bf16[8,32,1024]{2,1,0:T(8,128)(2,1)S(1)} collective-permute-done((bf16[8,32,1024]{2,1,0:T(8,128)(2,1)S(1)}, bf16[8,32,1024]{2,1,0:T(8,128)(2,1)S(1)}, u32[]{:S(2)}, u32[]{:S(2)}) %collective-permute-start.13) | collective-permute-done | bytes 524320 | tf_op jit(solution)/shard_map/ppermute | solution.py:62
  95.1 15.5 %collective-permute-done.12 = bf16[8,32,1024]{2,1,0:T(8,128)(2,1)S(1)} collective-permute-done((bf16[8,32,1024]{2,1,0:T(8,128)(2,1)S(1)}, bf16[8,32,1024]{2,1,0:T(8,128)(2,1)S(1)}, u32[]{:S(2)}, u32[]{:S(2)}) %collective-permute-start.12) | collective-permute-done | bytes 524320 | tf_op jit(solution)/shard_map/ppermute | solution.py:62
  110.6 3.2 %collective-permute-done.11 = bf16[8,32,1024]{2,1,0:T(8,128)(2,1)S(1)} collective-permute-done((bf16[8,32,1024]{2,1,0:T(8,128)(2,1)S(1)}, bf16[8,32,1024]{2,1,0:T(8,128)(2,1)S(1)}, u32[]{:S(2)}, u32[]{:S(2)}) %collective-permute-start.11) | collective-permute-done | bytes 524320 | tf_op jit(solution)/shard_map/ppermute | solution.py:62
  113.9 0.8 copy-done.17
  114.7 1.5 pad_maximum_fusion.own_ref
  116.3 7.9 %gather_fusion = bf16[1024,512]{1,0:T(8,128)(2,1)} fusion(bf16[4096,512]{1,0:T(8,128)(2,1)} %param.27, s32[1024]{0:T(1024)S(1)} %broadcast_clamp_fusion), kind=kCustom, calls=%fused_computation | custom fusion | bytes 2101248 | tf_op jit(solution)/shard_map/gather | solution.py:423
  124.3 6.6 %all-to-all-start.1 = ((bf16[16,64,512]{2,1,0:T(8,128)(2,1)}), bf16[16,64,512]{2,1,0:T(8,128)(2,1)}, u32[]{:S(2)}, u32[]{:S(2)}) async-start(bf16[16,64,512]{2,1,0:T(8,128)(2,1)} %bitcast.16), calls=%async_computation.1 | async-start | bytes 2097152 | tf_op jit(solution)/shard_map/all_to_all | solution.py:424
  130.9 17.4 %all-to-all-done.1 = bf16[16,64,512]{2,1,0:T(8,128)(2,1)} async-done(((bf16[16,64,512]{2,1,0:T(8,128)(2,1)}), bf16[16,64,512]{2,1,0:T(8,128)(2,1)}, u32[]{:S(2)}, u32[]{:S(2)}) %all-to-all-start.1) | async-done | bytes 1048608 | tf_op jit(solution)/shard_map/all_to_all | solution.py:424
  148.3 3.3 %gather_fusion.1 = bf16[512,512]{1,0:T(8,128)(2,1)S(1)} fusion(bf16[1024,512]{1,0:T(8,128)(2,1)} %bitcast.17, s32[1024]{0:T(1024)S(1)} %pad_clamp_fusion), kind=kCustom, calls=%fused_computation.1 | custom fusion | bytes 1050624 | tf_op jit(solution)/shard_map/gather | solution.py:427
  151.7 6.2 %collective-permute-start.10 = (bf16[512,512]{1,0:T(8,128)(2,1)S(1)}, bf16[512,512]{1,0:T(8,128)(2,1)S(1)}, u32[]{:S(2)}, u32[]{:S(2)}) collective-permute-start(bf16[512,512]{1,0:T(8,128)(2,1)S(1)} %gather_fusion.1), channel_id=1, source_target_pairs={{0,1},{1,2},{2,3},{3,0},{4,5},{5,6},{6,7},{7,4},{8,9},{9,10},{10,1... | collective-permute-start | bytes 1572872 | tf_op jit(solution)/shard_map/ppermute | solution.py:58
  157.9 0.9 collective-permute-start.8
  158.9 21.7 %collective-permute-done.10.a3 = bf16[512,512]{1,0:T(8,128)(2,1)S(1)} collective-permute-done((bf16[512,512]{1,0:T(8,128)(2,1)S(1)}, bf16[512,512]{1,0:T(8,128)(2,1)S(1)}, u32[]{:S(2)}, u32[]{:S(2)}) %collective-permute-start.10) | collective-permute-done | bytes 524320 | tf_op jit(solution)/shard_map/ppermute | solution.py:58
  180.6 3.5 %collective-permute-done.8.a1 = bf16[512,512]{1,0:T(8,128)(2,1)} collective-permute-done((bf16[512,512]{1,0:T(8,128)(2,1)S(1)}, bf16[512,512]{1,0:T(8,128)(2,1)}, u32[]{:S(2)}, u32[]{:S(2)}) %collective-permute-start.8) | collective-permute-done | bytes 524320 | tf_op jit(solution)/shard_map/ppermute | solution.py:58
  184.1 5.3 %x_away.1 = (bf16[512,640]{1,0:T(8,128)(2,1)}, f32[512,128]{1,0:T(8,128)S(1)}) custom-call(s32[5]{0:T(128)S(1)} %stack.135.s_ref, bf16[512,512]{1,0:T(8,128)(2,1)S(1)} %gather_fusion.1, bf16[512,512]{1,0:T(8,128)(2,1)} %collective-permute-done.8.a1, bf16[512,512]{1,0:T(8,128)(2,1)} %collective-permute-done.9.a2, ...), custom_call_target="tpu_custom_call" | custom-call | flops 1073741824 | bytes 6291456 | tf_op jit(solution)/shard_map/x_away/pallas_call | solution.py:196
  189.4 0.7 copy-done.5
  191.2 4.5 %x_here.1.here = f32[512,512]{1,0:T(8,128)S(1)} custom-call(s32[5]{0:T(128)S(1)} %stack.128.s_ref, bf16[512,512]{1,0:T(8,128)(2,1)S(1)} %gather_fusion.1, bf16[512,512]{1,0:T(8,128)(2,1)} %collective-permute-done.8.a1, bf16[512,512]{1,0:T(8,128)(2,1)} %collective-permute-done.9.a2, bf16[512,512]{1,0:T(8,128)(2,1)S(1)} %collective-permute-done.10.a3, ...), custom_call_target="tpu_custom_call" | custom-call | flops 1073741824 | bytes 6291456 | tf_op jit(solution)/shard_map/x_here/pallas_call | solution.py:196
  195.7 12.6 %collective-permute-done.15.away = bf16[512,640]{1,0:T(8,128)(2,1)} collective-permute-done((bf16[512,640]{1,0:T(8,128)(2,1)}, bf16[512,640]{1,0:T(8,128)(2,1)}, u32[]{:S(2)}, u32[]{:S(2)}) %collective-permute-start.15) | collective-permute-done | bytes 655392 | tf_op jit(solution)/shard_map/ppermute | solution.py:72
  208.4 2.7 conv.1
  211.1 3.2 %collective-permute-start.18 = (bf16[128,288]{1,0:T(8,128)(2,1)S(1)}, bf16[128,288]{1,0:T(8,128)(2,1)S(1)}, u32[]{:S(2)}, u32[]{:S(2)}) collective-permute-start(bf16[128,288]{1,0:T(8,128)(2,1)S(1)} %get-tuple-element.79), channel_id=1, source_target_pairs={{0,1},{1,2},{2,3},{3,0},{4,5},{5,6},{6,7},{7,4},{8,9},{9,10},{10,1... | collective-permute-start | bytes 221192 | tf_op jit(solution)/shard_map/ppermute | solution.py:58
  214.4 3.6 %collective-permute-done.16 = bf16[128,288]{1,0:T(8,128)(2,1)S(1)} collective-permute-done((bf16[128,288]{1,0:T(8,128)(2,1)S(1)}, bf16[128,288]{1,0:T(8,128)(2,1)S(1)}, u32[]{:S(2)}, u32[]{:S(2)}) %collective-permute-start.16) | collective-permute-done | bytes 73760 | tf_op jit(solution)/shard_map/ppermute | solution.py:58
  218.0 2.5 collective-permute-done.17
  221.0 5.7 %collective-permute-done.19 = bf16[128,288]{1,0:T(8,128)(2,1)S(1)} collective-permute-done((bf16[128,288]{1,0:T(8,128)(2,1)S(1)}, bf16[128,288]{1,0:T(8,128)(2,1)S(1)}, u32[]{:S(2)}, u32[]{:S(2)}) %collective-permute-start.19) | collective-permute-done | bytes 73760 | tf_op jit(solution)/shard_map/ppermute | solution.py:72
  226.8 0.8 collective-permute-start.22
  227.8 1.1 collective-permute-start.20
  229.1 2.4 collective-permute-done.22
  231.5 2.3 collective-permute-done.21
  233.9 1.0 collective-permute-done.20
  235.1 0.8 fusion.48
  235.9 0.8 compare_select_fusion
  236.7 1.0 convert_multiply_fusion.12
  237.7 3.4 %copy-done.1 = bf16[4096,1024]{1,0:T(8,128)(2,1)S(1)} copy-done((bf16[4096,1024]{1,0:T(8,128)(2,1)S(1)}, bf16[4096,1024]{1,0:T(8,128)(2,1)}, u32[]{:S(2)}) %copy-start.1) | copy-done | bytes 8388632
  241.2 4.2 %in_product.3 = bf16[512,512]{1,0:T(8,128)(2,1)S(1)} custom-call(s32[2]{0:T(128)S(1)} %pad_add_fusion.1.s_ref, bf16[512,512]{1,0:T(8,128)(2,1)S(1)} %gather_fusion.1, bf16[512,512]{1,0:T(8,128)(2,1)} %collective-permute-done.8.a1, bf16[512,512]{1,0:T(8,128)(2,1)} %collective-permute-done.9.a2, bf16[512,512]{1,0:T(8,128)(2,1)S(1)} %collective-permute-done.10.a3, ...), custom_call_target="tpu_custom_call" | custom-call | flops 1073741824 | bytes 6291456 | tf_op jit(solution)/shard_map/in_product/pallas_call | solution.py:280
  246.1 7.8 %multiply_reduce_fusion.2 = (f32[128,512]{1,0:T(8,128)S(1)}, f32[128,512]{1,0:T(8,128)S(1)}, f32[128,512]{1,0:T(8,128)S(1)}, f32[128,512]{1,0:T(8,128)S(1)}, f32[128,16,512]{2,1,0:T(8,128)}) fusion(f32[128,16]{1,0:T(8,128)S(1)} %copy-done.22, f32[128,16]{1,0:T(8,128)S(1)} %copy-done.21, f32[128,512]{1,0:T(8,128)S(1)} %get-tuple-element.55, ...), kind=kLoop, calls=%fused_computation.6 | loop fusion | flops 24903680 | bytes 11632640 | tf_op jit(solution)/shard_map/reduce_sum | solution.py:478
  253.8 3.8 %in_product.2 = f32[512,512]{1,0:T(8,128)S(1)} custom-call(s32[2]{0:T(128)S(1)} %pad_add_fusion.s_ref, bf16[512,512]{1,0:T(8,128)(2,1)S(1)} %gather_fusion.1, bf16[512,512]{1,0:T(8,128)(2,1)} %collective-permute-done.8.a1, bf16[512,512]{1,0:T(8,128)(2,1)} %collective-permute-done.9.a2, bf16[512,512]{1,0:T(8,128)(2,1)S(1)} %collective-permute-done.10.a3, ...), custom_call_target="tpu_custom_call" | custom-call | flops 1073741824 | bytes 6291456 | tf_op jit(solution)/shard_map/in_product/pallas_call | solution.py:280
  258.3 1.5 collective-permute-start.32
  259.8 0.9 collective-permute-start.31
  260.8 11.6 %collective-permute-done.32.a3 = bf16[512,512]{1,0:T(8,128)(2,1)S(1)} collective-permute-done((bf16[512,512]{1,0:T(8,128)(2,1)S(1)}, bf16[512,512]{1,0:T(8,128)(2,1)S(1)}, u32[]{:S(2)}, u32[]{:S(2)}) %collective-permute-start.32) | collective-permute-done | bytes 524320 | tf_op jit(solution)/shard_map/ppermute | solution.py:58
  272.4 2.3 collective-permute-done.31.a2
  274.7 5.5 %collective-permute-done.30.a1 = bf16[512,512]{1,0:T(8,128)(2,1)S(1)} collective-permute-done((bf16[512,512]{1,0:T(8,128)(2,1)S(1)}, bf16[512,512]{1,0:T(8,128)(2,1)S(1)}, u32[]{:S(2)}, u32[]{:S(2)}) %collective-permute-start.30) | collective-permute-done | bytes 524320 | tf_op jit(solution)/shard_map/ppermute | solution.py:58
  280.2 3.0 out_product.3
  283.1 3.3 %collective-permute-start.33 = (bf16[512,512]{1,0:T(8,128)(2,1)S(1)}, bf16[512,512]{1,0:T(8,128)(2,1)S(1)}, u32[]{:S(2)}, u32[]{:S(2)}) collective-permute-start(bf16[512,512]{1,0:T(8,128)(2,1)S(1)} %out_product.3), channel_id=1, source_target_pairs={{0,4},{1,5},{2,6},{3,7},{4,0},{5,1},{6,2},{7,3},{8,12},{9,13},{10,... | collective-permute-start | bytes 1572872 | tf_op jit(solution)/shard_map/ppermute | solution.py:72
  286.4 3.0 out_product.2
  289.4 7.3 %collective-permute-done.33 = bf16[512,512]{1,0:T(8,128)(2,1)S(1)} collective-permute-done((bf16[512,512]{1,0:T(8,128)(2,1)S(1)}, bf16[512,512]{1,0:T(8,128)(2,1)S(1)}, u32[]{:S(2)}, u32[]{:S(2)}) %collective-permute-start.33) | collective-permute-done | bytes 524320 | tf_op jit(solution)/shard_map/ppermute | solution.py:72
  296.7 1.0 add_convert_fusion
  (138 shorter events, 8.4 us)
Async XLA Ops:
  7.2 228.7 %copy-start = (bf16[512,256]{1,0:T(8,128)(2,1)S(1)}, bf16[512,256]{1,0:T(8,128)(2,1)}, u32[]{:S(2)}) copy-start(bf16[512,256]{1,0:T(8,128)(2,1)} %param.34) | copy-start | bytes 786436
  7.2 15.6 %copy-start.28 = (s32[4,128]{1,0:T(4,128)S(1)}, s32[4,128]{1,0:T(4,128)}, u32[]{:S(2)}) copy-start(s32[4,128]{1,0:T(4,128)} %param.28) | copy-start | bytes 6148
  7.2 24.2 %copy-start.24 = (bf16[32,4096]{1,0:T(8,128)(2,1)S(1)}, bf16[32,4096]{1,0:T(8,128)(2,1)}, u32[]{:S(2)}) copy-start(bf16[32,4096]{1,0:T(8,128)(2,1)} %param.26) | copy-start | bytes 786436
  7.2 24.2 %copy-start.14 = (f32[32,4096]{1,0:T(8,128)S(1)}, f32[32,4096]{1,0:T(8,128)}, u32[]{:S(2)}) copy-start(f32[32,4096]{1,0:T(8,128)} %param.25) | copy-start | bytes 1572868
  7.2 24.2 %copy-start.15 = (f32[32,4096]{1,0:T(8,128)S(1)}, f32[32,4096]{1,0:T(8,128)}, u32[]{:S(2)}) copy-start(f32[32,4096]{1,0:T(8,128)} %param.24) | copy-start | bytes 1572868
  7.2 24.2 %copy-start.13 = (f32[32,4096]{1,0:T(8,128)S(1)}, f32[32,4096]{1,0:T(8,128)}, u32[]{:S(2)}) copy-start(f32[32,4096]{1,0:T(8,128)} %param.23) | copy-start | bytes 1572868
  14.6 38.1 %copy-start.25 = (bf16[4,32,1024]{2,1,0:T(8,128)(2,1)S(1)}, bf16[4,32,1024]{2,1,0:T(8,128)(2,1)}, u32[]{:S(2)}) copy-start(bf16[4,32,1024]{2,1,0:T(8,128)(2,1)} %get-tuple-element.38) | copy-start | bytes 786436
  15.6 37.0 %collective-permute-start.7 = (bf16[32,1024]{1,0:T(8,128)(2,1)S(1)}, bf16[32,1024]{1,0:T(8,128)(2,1)S(1)}, u32[]{:S(2)}, u32[]{:S(2)}) collective-permute-start(bf16[32,1024]{1,0:T(8,128)(2,1)S(1)} %get-tuple-element.89), channel_id=1, source_target_pairs={{0,67},{1,64},{2,65},{3,66},{4,3},{5,0},{6,1},{7,2},{8,75},{9,72},... | collective-permute-start | bytes 196616 | tf_op jit(solution)/shard_map/ppermute | solution.py:402
  17.5 29.3 %collective-permute-start.3 = (bf16[32,1024]{1,0:T(8,128)(2,1)S(1)}, bf16[32,1024]{1,0:T(8,128)(2,1)S(1)}, u32[]{:S(2)}, u32[]{:S(2)}) collective-permute-start(bf16[32,1024]{1,0:T(8,128)(2,1)S(1)} %get-tuple-element.89), channel_id=1, source_target_pairs={{0,3},{1,0},{2,1},{3,2},{4,67},{5,64},{6,65},{7,66},{8,11},{9,8},{... | collective-permute-start | bytes 196616 | tf_op jit(solution)/shard_map/ppermute | solution.py:402
  18.1 34.5 %collective-permute-start.6 = (bf16[32,1024]{1,0:T(8,128)(2,1)S(1)}, bf16[32,1024]{1,0:T(8,128)(2,1)S(1)}, u32[]{:S(2)}, u32[]{:S(2)}) collective-permute-start(bf16[32,1024]{1,0:T(8,128)(2,1)S(1)} %get-tuple-element.90), channel_id=1, source_target_pairs={{0,66},{1,67},{2,64},{3,65},{4,2},{5,3},{6,0},{7,1},{8,74},{9,75},... | collective-permute-start | bytes 196616 | tf_op jit(solution)/shard_map/ppermute | solution.py:402
  22.2 24.6 %collective-permute-start.2 = (bf16[32,1024]{1,0:T(8,128)(2,1)S(1)}, bf16[32,1024]{1,0:T(8,128)(2,1)S(1)}, u32[]{:S(2)}, u32[]{:S(2)}) collective-permute-start(bf16[32,1024]{1,0:T(8,128)(2,1)S(1)} %get-tuple-element.90), channel_id=1, source_target_pairs={{0,2},{1,3},{2,0},{3,1},{4,66},{5,67},{6,64},{7,65},{8,10},{9,11},... | collective-permute-start | bytes 196616 | tf_op jit(solution)/shard_map/ppermute | solution.py:402
  24.0 28.7 %all-to-all-start = ((s32[16,1,64]{2,1,0:T(1,128)}), s32[16,1,64]{2,1,0:T(1,128)S(1)}, u32[]{:S(2)}, u32[]{:S(2)}) async-start(s32[16,1,64]{2,1,0:T(1,128)} %sub.66), calls=%async_computation | async-start | bytes 16384 | tf_op jit(solution)/shard_map/all_to_all | solution.py:393
  30.7 207.1 %all-gather.3.cloned.1.call-start = ((), (), s32[]{:S(2)}) async-start(), calls=%async_computation.2 | async-start | bytes 8912896 | tf_op jit(solution)/shard_map/all_gather | solution.py:418
  30.7 2.9 collective-permute-start
  33.6 4.5 %collective-permute-start.1 = (bf16[32,1024]{1,0:T(8,128)(2,1)S(1)}, bf16[32,1024]{1,0:T(8,128)(2,1)S(1)}, u32[]{:S(2)}, u32[]{:S(2)}) collective-permute-start(bf16[32,1024]{1,0:T(8,128)(2,1)S(1)} %get-tuple-element.91), channel_id=1, source_target_pairs={{0,1},{1,2},{2,3},{3,0},{4,65},{5,66},{6,67},{7,64},{8,9},{9,10},{... | collective-permute-start | bytes 196616 | tf_op jit(solution)/shard_map/ppermute | solution.py:402
  38.1 14.5 %collective-permute-start.5 = (bf16[32,1024]{1,0:T(8,128)(2,1)S(1)}, bf16[32,1024]{1,0:T(8,128)(2,1)S(1)}, u32[]{:S(2)}, u32[]{:S(2)}) collective-permute-start(bf16[32,1024]{1,0:T(8,128)(2,1)S(1)} %get-tuple-element.91), channel_id=1, source_target_pairs={{0,65},{1,66},{2,67},{3,64},{4,1},{5,2},{6,3},{7,0},{8,73},{9,74},... | collective-permute-start | bytes 196616 | tf_op jit(solution)/shard_map/ppermute | solution.py:402
  46.8 5.8 %collective-permute-start.4 = (bf16[32,1024]{1,0:T(8,128)(2,1)S(1)}, bf16[32,1024]{1,0:T(8,128)(2,1)S(1)}, u32[]{:S(2)}, u32[]{:S(2)}) collective-permute-start(bf16[32,1024]{1,0:T(8,128)(2,1)S(1)} %get-tuple-element.92), channel_id=1, source_target_pairs={{0,64},{1,65},{2,66},{3,67},{4,0},{5,1},{6,2},{7,3},{8,72},{9,73},... | collective-permute-start | bytes 196616 | tf_op jit(solution)/shard_map/ppermute | solution.py:402
  52.7 9.2 %collective-permute-start.23 = (bf16[32,1024]{1,0:T(8,128)(2,1)S(1)}, bf16[32,1024]{1,0:T(8,128)(2,1)S(1)}, u32[]{:S(2)}, u32[]{:S(2)}) collective-permute-start(bf16[32,1024]{1,0:T(8,128)(2,1)S(1)} %get-tuple-element.83), channel_id=1, source_target_pairs={{0,0},{1,1},{2,2},{3,3},{4,64},{5,65},{6,66},{7,67},{8,8},{9,9},{1... | collective-permute-start | bytes 196616 | tf_op jit(solution)/shard_map/ppermute | solution.py:412
  53.4 13.6 %collective-permute-start.26 = (bf16[32,1024]{1,0:T(8,128)(2,1)S(1)}, bf16[32,1024]{1,0:T(8,128)(2,1)S(1)}, u32[]{:S(2)}, u32[]{:S(2)}) collective-permute-start(bf16[32,1024]{1,0:T(8,128)(2,1)S(1)} %get-tuple-element.84), channel_id=1, source_target_pairs={{0,3},{1,0},{2,1},{3,2},{4,67},{5,64},{6,65},{7,66},{8,11},{9,8},{... | collective-permute-start | bytes 196616 | tf_op jit(solution)/shard_map/ppermute | solution.py:412
  53.5 13.5 %collective-permute-start.25 = (bf16[32,1024]{1,0:T(8,128)(2,1)S(1)}, bf16[32,1024]{1,0:T(8,128)(2,1)S(1)}, u32[]{:S(2)}, u32[]{:S(2)}) collective-permute-start(bf16[32,1024]{1,0:T(8,128)(2,1)S(1)} %get-tuple-element.85), channel_id=1, source_target_pairs={{0,2},{1,3},{2,0},{3,1},{4,66},{5,67},{6,64},{7,65},{8,10},{9,11},... | collective-permute-start | bytes 196616 | tf_op jit(solution)/shard_map/ppermute | solution.py:412
  54.8 12.2 %collective-permute-start.24 = (bf16[32,1024]{1,0:T(8,128)(2,1)S(1)}, bf16[32,1024]{1,0:T(8,128)(2,1)S(1)}, u32[]{:S(2)}, u32[]{:S(2)}) collective-permute-start(bf16[32,1024]{1,0:T(8,128)(2,1)S(1)} %get-tuple-element.86), channel_id=1, source_target_pairs={{0,1},{1,2},{2,3},{3,0},{4,65},{5,66},{6,67},{7,64},{8,9},{9,10},{... | collective-permute-start | bytes 196616 | tf_op jit(solution)/shard_map/ppermute | solution.py:412
  56.7 12.5 %collective-permute-start.27 = (bf16[32,2048]{1,0:T(8,128)(2,1)S(1)}, bf16[32,2048]{1,0:T(8,128)(2,1)S(1)}, u32[]{:S(2)}, u32[]{:S(2)}) collective-permute-start(bf16[32,2048]{1,0:T(8,128)(2,1)S(1)} %get-tuple-element.39), channel_id=1, source_target_pairs={{0,0},{1,16},{2,32},{3,48},{4,4},{5,20},{6,36},{7,52},{8,8},{9,24}... | collective-permute-start | bytes 393224 | tf_op jit(solution)/shard_map/ppermute | solution.py:414
  62.0 12.0 %collective-permute-start.28 = (bf16[32,2048]{1,0:T(8,128)(2,1)S(1)}, bf16[32,2048]{1,0:T(8,128)(2,1)S(1)}, u32[]{:S(2)}, u32[]{:S(2)}) collective-permute-start(bf16[32,2048]{1,0:T(8,128)(2,1)S(1)} %get-tuple-element.40), channel_id=1, source_target_pairs={{0,4},{1,20},{2,36},{3,52},{4,0},{5,16},{6,32},{7,48},{8,12},{9,28... | collective-permute-start | bytes 393224 | tf_op jit(solution)/shard_map/ppermute | solution.py:414
  74.9 20.1 %collective-permute-start.13 = (bf16[8,32,1024]{2,1,0:T(8,128)(2,1)S(1)}, bf16[8,32,1024]{2,1,0:T(8,128)(2,1)S(1)}, u32[]{:S(2)}, u32[]{:S(2)}) collective-permute-start(bf16[8,32,1024]{2,1,0:T(8,128)(2,1)S(1)} %bitcast_dynamic-update-slice_fusion.4), channel_id=1, source_target_pairs={{0,16},{8,24},{16,32},{24,40},{32,48},{40,56},{48,0},{56,8},{64,80... | collective-permute-start | bytes 1572872 | tf_op jit(solution)/shard_map/ppermute | solution.py:62
  77.3 33.4 %collective-permute-start.12 = (bf16[8,32,1024]{2,1,0:T(8,128)(2,1)S(1)}, bf16[8,32,1024]{2,1,0:T(8,128)(2,1)S(1)}, u32[]{:S(2)}, u32[]{:S(2)}) collective-permute-start(bf16[8,32,1024]{2,1,0:T(8,128)(2,1)S(1)} %bitcast_dynamic-update-slice_fusion.4), channel_id=1, source_target_pairs={{0,32},{8,40},{16,48},{24,56},{32,0},{40,8},{48,16},{56,24},{64,96... | collective-permute-start | bytes 1572872 | tf_op jit(solution)/shard_map/ppermute | solution.py:62
  77.3 36.6 %collective-permute-start.11 = (bf16[8,32,1024]{2,1,0:T(8,128)(2,1)S(1)}, bf16[8,32,1024]{2,1,0:T(8,128)(2,1)S(1)}, u32[]{:S(2)}, u32[]{:S(2)}) collective-permute-start(bf16[8,32,1024]{2,1,0:T(8,128)(2,1)S(1)} %bitcast_dynamic-update-slice_fusion.4), channel_id=1, source_target_pairs={{0,48},{8,56},{16,0},{24,8},{32,16},{40,24},{48,32},{56,40},{64,11... | collective-permute-start | bytes 1572872 | tf_op jit(solution)/shard_map/ppermute | solution.py:62
  116.1 68.0 %collective-permute-start.14 = (bf16[4,8,32,1024]{3,2,1,0:T(8,128)(2,1)S(1)}, bf16[4,8,32,1024]{3,2,1,0:T(8,128)(2,1)}, u32[]{:S(2)}, u32[]{:S(2)}) collective-permute-start(bf16[4,8,32,1024]{3,2,1,0:T(8,128)(2,1)S(1)} %pad_maximum_fusion.own_ref), channel_id=1, source_target_pairs={{0,8},{8,0},{16,24},{24,16},{32,40},{40,32},{48,56},{56,48},{64,72... | collective-permute-start | bytes 6291464 | tf_op jit(solution)/shard_map/ppermute | solution.py:68
  124.3 24.0 %all-to-all-start.1 = ((bf16[16,64,512]{2,1,0:T(8,128)(2,1)}), bf16[16,64,512]{2,1,0:T(8,128)(2,1)}, u32[]{:S(2)}, u32[]{:S(2)}) async-start(bf16[16,64,512]{2,1,0:T(8,128)(2,1)} %bitcast.16), calls=%async_computation.1 | async-start | bytes 2097152 | tf_op jit(solution)/shard_map/all_to_all | solution.py:424
  151.7 38.9 %copy-start.27 = (f32[16,512]{1,0:T(8,128)S(1)}, f32[16,512]{1,0:T(8,128)}, u32[]{:S(2)}) copy-start(f32[16,512]{1,0:T(8,128)} %param.36) | copy-start | bytes 98308
  151.7 28.9 %collective-permute-start.10 = (bf16[512,512]{1,0:T(8,128)(2,1)S(1)}, bf16[512,512]{1,0:T(8,128)(2,1)S(1)}, u32[]{:S(2)}, u32[]{:S(2)}) collective-permute-start(bf16[512,512]{1,0:T(8,128)(2,1)S(1)} %gather_fusion.1), channel_id=1, source_target_pairs={{0,1},{1,2},{2,3},{3,0},{4,5},{5,6},{6,7},{7,4},{8,9},{9,10},{10,1... | collective-permute-start | bytes 1572872 | tf_op jit(solution)/shard_map/ppermute | solution.py:58
  157.9 22.7 %collective-permute-start.9 = (bf16[512,512]{1,0:T(8,128)(2,1)S(1)}, bf16[512,512]{1,0:T(8,128)(2,1)}, u32[]{:S(2)}, u32[]{:S(2)}) collective-permute-start(bf16[512,512]{1,0:T(8,128)(2,1)S(1)} %gather_fusion.1), channel_id=1, source_target_pairs={{0,2},{1,3},{2,0},{3,1},{4,6},{5,7},{6,4},{7,5},{8,10},{9,11},{10,... | collective-permute-start | bytes 1572872 | tf_op jit(solution)/shard_map/ppermute | solution.py:58
  157.9 26.2 %collective-permute-start.8 = (bf16[512,512]{1,0:T(8,128)(2,1)S(1)}, bf16[512,512]{1,0:T(8,128)(2,1)}, u32[]{:S(2)}, u32[]{:S(2)}) collective-permute-start(bf16[512,512]{1,0:T(8,128)(2,1)S(1)} %gather_fusion.1), channel_id=1, source_target_pairs={{0,3},{1,0},{2,1},{3,2},{4,7},{5,4},{6,5},{7,6},{8,11},{9,8},{10,9... | collective-permute-start | bytes 1572872 | tf_op jit(solution)/shard_map/ppermute | solution.py:58
  190.1 18.2 %copy-start.7 = (f32[4,512]{1,0:T(4,128)S(1)}, f32[4,512]{1,0:T(4,128)}, u32[]{:S(2)}) copy-start(f32[4,512]{1,0:T(4,128)} %weight.1) | copy-start | bytes 24580
  190.1 18.2 %copy-start.8 = (f32[512]{0:T(512)S(1)}, f32[512]{0:T(512)}, u32[]{:S(2)}) copy-start(f32[512]{0:T(512)} %param.32) | copy-start | bytes 6148
  190.1 18.2 %collective-permute-start.15 = (bf16[512,640]{1,0:T(8,128)(2,1)}, bf16[512,640]{1,0:T(8,128)(2,1)}, u32[]{:S(2)}, u32[]{:S(2)}) collective-permute-start(bf16[512,640]{1,0:T(8,128)(2,1)} %get-tuple-element.29), channel_id=1, source_target_pairs={{0,4},{1,5},{2,6},{3,7},{4,0},{5,1},{6,2},{7,3},{8,12},{9,13},{10,... | collective-permute-start | bytes 1966088 | tf_op jit(solution)/shard_map/ppermute | solution.py:72
  190.6 17.8 %copy-start.3 = (bf16[128,3,512]{2,0,1:T(8,128)(2,1)S(1)}, bf16[128,3,512]{2,0,1:T(8,128)(2,1)}, u32[]{:S(2)}) copy-start(bf16[128,3,512]{2,0,1:T(8,128)(2,1)} %param.29) | copy-start | bytes 1179652
  190.6 17.8 %copy-start.4 = (bf16[288,512]{1,0:T(8,128)(2,1)S(1)}, bf16[288,512]{1,0:T(8,128)(2,1)}, u32[]{:S(2)}) copy-start(bf16[288,512]{1,0:T(8,128)(2,1)} %proj.1) | copy-start | bytes 884740
  190.6 17.8 %copy-start.6 = (f32[512,128]{1,0:T(8,128)S(1)}, f32[512,128]{1,0:T(8,128)}, u32[]{:S(2)}) copy-start(f32[512,128]{1,0:T(8,128)} %copy-done.5) | copy-start | bytes 786436
  208.3 27.6 %copy-start.30 = (f32[512]{0:T(512)S(1)}, f32[512]{0:T(512)}, u32[]{:S(2)}) copy-start(f32[512]{0:T(512)} %param.35) | copy-start | bytes 6148
  211.1 6.9 %collective-permute-start.16 = (bf16[128,288]{1,0:T(8,128)(2,1)S(1)}, bf16[128,288]{1,0:T(8,128)(2,1)S(1)}, u32[]{:S(2)}, u32[]{:S(2)}) collective-permute-start(bf16[128,288]{1,0:T(8,128)(2,1)S(1)} %get-tuple-element.78), channel_id=1, source_target_pairs={{0,3},{1,0},{2,1},{3,2},{4,7},{5,4},{6,5},{7,6},{8,11},{9,8},{10,9... | collective-permute-start | bytes 221192 | tf_op jit(solution)/shard_map/ppermute | solution.py:58
  211.1 6.9 %collective-permute-start.18 = (bf16[128,288]{1,0:T(8,128)(2,1)S(1)}, bf16[128,288]{1,0:T(8,128)(2,1)S(1)}, u32[]{:S(2)}, u32[]{:S(2)}) collective-permute-start(bf16[128,288]{1,0:T(8,128)(2,1)S(1)} %get-tuple-element.79), channel_id=1, source_target_pairs={{0,1},{1,2},{2,3},{3,0},{4,5},{5,6},{6,7},{7,4},{8,9},{9,10},{10,1... | collective-permute-start | bytes 221192 | tf_op jit(solution)/shard_map/ppermute | solution.py:58
  214.4 6.1 %collective-permute-start.17 = (bf16[128,288]{1,0:T(8,128)(2,1)S(1)}, bf16[128,288]{1,0:T(8,128)(2,1)S(1)}, u32[]{:S(2)}, u32[]{:S(2)}) collective-permute-start(bf16[128,288]{1,0:T(8,128)(2,1)S(1)} %get-tuple-element.80), channel_id=1, source_target_pairs={{0,2},{1,3},{2,0},{3,1},{4,6},{5,7},{6,4},{7,5},{8,10},{9,11},{10,... | collective-permute-start | bytes 221192 | tf_op jit(solution)/shard_map/ppermute | solution.py:58
  220.6 6.2 %collective-permute-start.19 = (bf16[128,288]{1,0:T(8,128)(2,1)S(1)}, bf16[128,288]{1,0:T(8,128)(2,1)S(1)}, u32[]{:S(2)}, u32[]{:S(2)}) collective-permute-start(bf16[128,288]{1,0:T(8,128)(2,1)S(1)} %fusion.41), channel_id=1, source_target_pairs={{0,4},{1,5},{2,6},{3,7},{4,0},{5,1},{6,2},{7,3},{8,12},{9,13},{10,... | collective-permute-start | bytes 221192 | tf_op jit(solution)/shard_map/ppermute | solution.py:72
  226.8 4.7 %collective-permute-start.22 = (bf16[128,288]{1,0:T(8,128)(2,1)S(1)}, bf16[128,288]{1,0:T(8,128)(2,1)S(1)}, u32[]{:S(2)}, u32[]{:S(2)}) collective-permute-start(bf16[128,288]{1,0:T(8,128)(2,1)S(1)} %add_convert_fusion.1), channel_id=1, source_target_pairs={{0,1},{1,2},{2,3},{3,0},{4,5},{5,6},{6,7},{7,4},{8,9},{9,10},{10,1... | collective-permute-start | bytes 221192 | tf_op jit(solution)/shard_map/ppermute | solution.py:58
  227.7 6.2 %collective-permute-start.21 = (bf16[128,288]{1,0:T(8,128)(2,1)S(1)}, bf16[128,288]{1,0:T(8,128)(2,1)S(1)}, u32[]{:S(2)}, u32[]{:S(2)}) collective-permute-start(bf16[128,288]{1,0:T(8,128)(2,1)S(1)} %add_convert_fusion.1), channel_id=1, source_target_pairs={{0,2},{1,3},{2,0},{3,1},{4,6},{5,7},{6,4},{7,5},{8,10},{9,11},{10,... | collective-permute-start | bytes 221192 | tf_op jit(solution)/shard_map/ppermute | solution.py:58
  227.8 7.0 %collective-permute-start.20 = (bf16[128,288]{1,0:T(8,128)(2,1)S(1)}, bf16[128,288]{1,0:T(8,128)(2,1)S(1)}, u32[]{:S(2)}, u32[]{:S(2)}) collective-permute-start(bf16[128,288]{1,0:T(8,128)(2,1)S(1)} %add_convert_fusion.1), channel_id=1, source_target_pairs={{0,3},{1,0},{2,1},{3,2},{4,7},{5,4},{6,5},{7,6},{8,11},{9,8},{10,9... | collective-permute-start | bytes 221192 | tf_op jit(solution)/shard_map/ppermute | solution.py:58
  237.7 3.4 %copy-start.1 = (bf16[4096,1024]{1,0:T(8,128)(2,1)S(1)}, bf16[4096,1024]{1,0:T(8,128)(2,1)}, u32[]{:S(2)}) copy-start(bf16[4096,1024]{1,0:T(8,128)(2,1)} %all-gather.3.cloned.1.call-done) | copy-start | bytes 25165828
  241.1 4.9 %copy-start.9 = (f32[128,16,512]{2,1,0:T(8,128)S(1)}, f32[128,16,512]{2,1,0:T(8,128)}, u32[]{:S(2)}) copy-start(f32[128,16,512]{2,1,0:T(8,128)} %param.30) | copy-start | bytes 12582916
  241.1 4.9 %copy-start.10 = (f32[128,512]{1,0:T(8,128)S(1)}, f32[128,512]{1,0:T(8,128)}, u32[]{:S(2)}) copy-start(f32[128,512]{1,0:T(8,128)} %get-tuple-element.62) | copy-start | bytes 786436
  241.1 4.9 %copy-start.11 = (f32[128,512]{1,0:T(8,128)S(1)}, f32[128,512]{1,0:T(8,128)}, u32[]{:S(2)}) copy-start(f32[128,512]{1,0:T(8,128)} %get-tuple-element.63) | copy-start | bytes 786436
  241.1 4.9 %copy-start.18 = (f32[128,16]{1,0:T(8,128)S(1)}, f32[128,16]{1,0:T(8,128)}, u32[]{:S(2)}) copy-start(f32[128,16]{1,0:T(8,128)} %get-tuple-element.66) | copy-start | bytes 24580
  241.1 4.9 %copy-start.19 = (f32[128,16]{1,0:T(8,128)S(1)}, f32[128,16]{1,0:T(8,128)}, u32[]{:S(2)}) copy-start(f32[128,16]{1,0:T(8,128)} %get-tuple-element.67) | copy-start | bytes 24580
  241.1 4.9 %copy-start.20 = (f32[128,16]{1,0:T(8,128)S(1)}, f32[128,16]{1,0:T(8,128)}, u32[]{:S(2)}) copy-start(f32[128,16]{1,0:T(8,128)} %get-tuple-element.68) | copy-start | bytes 24580
  241.1 4.9 %copy-start.21 = (f32[128,16]{1,0:T(8,128)S(1)}, f32[128,16]{1,0:T(8,128)}, u32[]{:S(2)}) copy-start(f32[128,16]{1,0:T(8,128)} %get-tuple-element.69) | copy-start | bytes 24580
  241.1 4.9 %copy-start.22 = (f32[128,16]{1,0:T(8,128)S(1)}, f32[128,16]{1,0:T(8,128)}, u32[]{:S(2)}) copy-start(f32[128,16]{1,0:T(8,128)} %get-tuple-element.70) | copy-start | bytes 24580
  241.2 4.9 %copy-start.23 = (f32[128,16]{1,0:T(8,128)S(1)}, f32[128,16]{1,0:T(8,128)}, u32[]{:S(2)}) copy-start(f32[128,16]{1,0:T(8,128)} %get-tuple-element.71) | copy-start | bytes 24580
  241.2 4.9 %copy-start.26 = (f32[16,512]{1,0:T(8,128)S(1)}, f32[16,512]{1,0:T(8,128)}, u32[]{:S(2)}) copy-start(f32[16,512]{1,0:T(8,128)} %exponential_negate_fusion) | copy-start | bytes 98308
  245.4 12.3 %collective-permute-start.29 = (bf16[512,512]{1,0:T(8,128)(2,1)S(1)}, bf16[512,512]{1,0:T(8,128)(2,1)S(1)}, u32[]{:S(2)}, u32[]{:S(2)}) collective-permute-start(bf16[512,512]{1,0:T(8,128)(2,1)S(1)} %in_product.3), channel_id=1, source_target_pairs={{0,4},{1,5},{2,6},{3,7},{4,0},{5,1},{6,2},{7,3},{8,12},{9,13},{10,... | collective-permute-start | bytes 1572872 | tf_op jit(solution)/shard_map/ppermute | solution.py:72
  246.0 7.8 %copy-start.2 = (bf16[4096,1024]{1,0:T(8,128)(2,1)S(1)}, bf16[4096,1024]{1,0:T(8,128)(2,1)}, u32[]{:S(2)}) copy-start(bf16[4096,1024]{1,0:T(8,128)(2,1)} %all-gather.3.cloned.1.call-done) | copy-start | bytes 25165828
  253.8 4.0 %copy-start.29 = (f32[512]{0:T(512)S(1)}, f32[512]{0:T(512)}, u32[]{:S(2)}) copy-start(f32[512]{0:T(512)} %param.37) | copy-start | bytes 6148
  258.3 14.1 %collective-permute-start.32 = (bf16[512,512]{1,0:T(8,128)(2,1)S(1)}, bf16[512,512]{1,0:T(8,128)(2,1)S(1)}, u32[]{:S(2)}, u32[]{:S(2)}) collective-permute-start(bf16[512,512]{1,0:T(8,128)(2,1)S(1)} %pad_maximum_fusion.1.a0), channel_id=1, source_target_pairs={{0,1},{1,2},{2,3},{3,0},{4,5},{5,6},{6,7},{7,4},{8,9},{9,10},{10,1... | collective-permute-start | bytes 1572872 | tf_op jit(solution)/shard_map/ppermute | solution.py:58
  259.8 14.9 %collective-permute-start.31 = (bf16[512,512]{1,0:T(8,128)(2,1)S(1)}, bf16[512,512]{1,0:T(8,128)(2,1)S(1)}, u32[]{:S(2)}, u32[]{:S(2)}) collective-permute-start(bf16[512,512]{1,0:T(8,128)(2,1)S(1)} %pad_maximum_fusion.1.a0), channel_id=1, source_target_pairs={{0,2},{1,3},{2,0},{3,1},{4,6},{5,7},{6,4},{7,5},{8,10},{9,11},{10,... | collective-permute-start | bytes 1572872 | tf_op jit(solution)/shard_map/ppermute | solution.py:58
  260.7 19.5 %collective-permute-start.30 = (bf16[512,512]{1,0:T(8,128)(2,1)S(1)}, bf16[512,512]{1,0:T(8,128)(2,1)S(1)}, u32[]{:S(2)}, u32[]{:S(2)}) collective-permute-start(bf16[512,512]{1,0:T(8,128)(2,1)S(1)} %pad_maximum_fusion.1.a0), channel_id=1, source_target_pairs={{0,3},{1,0},{2,1},{3,2},{4,7},{5,4},{6,5},{7,6},{8,11},{9,8},{10,9... | collective-permute-start | bytes 1572872 | tf_op jit(solution)/shard_map/ppermute | solution.py:58
  283.1 13.6 %collective-permute-start.33 = (bf16[512,512]{1,0:T(8,128)(2,1)S(1)}, bf16[512,512]{1,0:T(8,128)(2,1)S(1)}, u32[]{:S(2)}, u32[]{:S(2)}) collective-permute-start(bf16[512,512]{1,0:T(8,128)(2,1)S(1)} %out_product.3), channel_id=1, source_target_pairs={{0,4},{1,5},{2,6},{3,7},{4,0},{5,1},{6,2},{7,3},{8,12},{9,13},{10,... | collective-permute-start | bytes 1572872 | tf_op jit(solution)/shard_map/ppermute | solution.py:72
  (4 other events, 5.6 us)
Sparse Core Ops, SparseCore 0:
  75.1 71.2 all-gather.2

commit v4 on v1

v4 whole, which is shorter than its diff:
```python
import functools
import math

import jax
import jax.numpy as jnp
from jax import lax
from jax.experimental import pallas as pl
from jax.experimental.pallas import tpu as pltpu
from jax.sharding import PartitionSpec as P

RANK = 256
NSTATE = 16

learn_rate = 0.01
beta_first = 0.8
beta_second = 0.95
adam_eps = 1e-08
weight_decay = 0.1
bias_first = 1.0 - math.pow(0.8, 10)
bias_second = 1.0 - math.pow(0.95, 10)
norm_eps = 1e-06

BOTH = ("fsdp", "chan")
PARTS = 2
DEVICES = [
    (yl, z, co, yh, x)
    for yl in range(2)
    for z in range(4)
    for co in range(2)
    for yh in range(2)
    for x in range(4)
]


def place_of(yl, z, co, yh, x):
    return (yl * 8 + z * 2 + co) * 8 + yh * 4 + x


def in_route(k):
    return [
        (place_of(yl, z, co, yh, x), place_of(yh, z, co, yl, (x + k) % 4))
        for yl, z, co, yh, x in DEVICES
    ]


def out_route(j):
    return [
        (place_of(yl, z, co, yh, x), place_of(yl, x, co, (yh + j) % 2, z))
        for yl, z, co, yh, x in DEVICES
    ]


def from_x(a, k):
    return lax.ppermute(a, "chan", [(i, (i // 4) * 4 + (i % 4 - k) % 4) for i in range(8)])


def from_partner(a):
    return lax.ppermute(a, "chan", [(i, i ^ 4) for i in range(8)])


IN_VMEM = pl.BlockSpec(memory_space=pltpu.VMEM)
IN_HBM = pl.BlockSpec(memory_space=pltpu.HBM)
IN_SMEM = pl.BlockSpec(memory_space=pltpu.SMEM)


def adam_update(master, moment, velocity, grad):
    gradient = grad.astype(jnp.float32)
    moment = beta_first * moment + (1.0 - beta_first) * gradient
    velocity = beta_second * velocity + (1.0 - beta_second) * gradient * gradient
    update = moment / bias_first / (jnp.sqrt(velocity / bias_second) + adam_eps)
    return master - learn_rate * (update + weight_decay * master)


def adam_in_kernel(s_ref, master, moment, velocity, grad, new, *rest):
    *sends, held = rest
    updated = adam_update(master[...], moment[...], velocity[...], grad[...])
    new[...] = updated
    held[...] = updated
    own = sends[0].shape[1]
    for k, send in enumerate(sends):
        at = lax.rem(s_ref[0] + k, 4) * 4
        for block in range(2):
            for tile in range(4):
                for matrix in range(2):
                    first = (block * 16 + at + tile) * 2 + matrix
                    rows = held[pl.ds(first, own, stride=64), :]
                    lanes = slice(block * 512 + tile * 128, block * 512 + tile * 128 + 128)
                    send[matrix, :, lanes] = rows.astype(jnp.bfloat16)


def tiles_of(a):
    return jnp.swapaxes(a.reshape(a.shape[0], 2, -1, 128), 1, 2).reshape(-1, 128)


def adam_in(master, moment, velocity, grad, x):
    own = master.shape[0]
    flat = (master.size // 128, 128)
    new, *sends = pl.pallas_call(
        adam_in_kernel,
        out_shape=(jax.ShapeDtypeStruct(flat, jnp.float32),)
        + (jax.ShapeDtypeStruct((2, own, 1024), jnp.bfloat16),) * 4,
        in_specs=[IN_SMEM] + [IN_VMEM] * 4,
        out_specs=(IN_VMEM,) * 5,
        scratch_shapes=[pltpu.VMEM(flat, jnp.float32)],
        compiler_params=pltpu.CompilerParams(vmem_limit_bytes=24 * 2**20),
        cost_estimate=pl.CostEstimate(
            flops=20 * master.size, bytes_accessed=20 * master.size, transcendentals=master.size
        ),
        name="adam_in",
    )(x[None], *(tiles_of(a) for a in (master, moment, velocity, grad)))
    new = jnp.swapaxes(new.reshape(own, -1, 2, 128), 1, 2).reshape(master.shape)
    return (new, *sends)


def conv_kernel(parts, here, *refs):
    aways, sums = refs[:parts], refs[parts : 2 * parts]
    window, weight, bias, proj, act, window_new, partial, scale = refs[2 * parts :]
    rows = window.shape[1]
    steps = here.shape[0] // rows
    taps = [window[t] for t in range(3)]
    for step in range(steps):
        at = slice(step * rows, (step + 1) * rows)
        p, local = divmod(step, steps // parts)
        inner = slice(local * rows, (local + 1) * rows)
        sent = aways[p][inner, 512:].astype(jnp.float32)
        squares = sums[p][inner, :1] + sent[:, :1] + sent[:, 64:65]
        factor = lax.rsqrt(squares / 4096.0 + norm_eps)
        scale[at, :] = jnp.broadcast_to(factor, (rows, 128))
        total = here[at, :] + aways[p][inner, :512].astype(jnp.float32)
        taps.append((total * factor).astype(jnp.bfloat16))
        mixed = taps[step].astype(jnp.float32) * weight[0:1, :]
        for t in range(1, 4):
            mixed = mixed + taps[step + t].astype(jnp.float32) * weight[t : t + 1, :]
        act[at, :] = jax.nn.silu(mixed + bias[...]).astype(jnp.bfloat16)
    for t in range(3):
        window_new[t] = taps[steps + t]
    partial[...] = lax.dot_general(
        act[...], proj[...], (((1,), (1,)), ((), ())), preferred_element_type=jnp.float32
    ).astype(jnp.bfloat16)


def conv(here, aways, sums, window, weight, bias, proj):
    tokens = here.shape[0]
    return pl.pallas_call(
        functools.partial(conv_kernel, len(aways)),
        out_shape=(
            jax.ShapeDtypeStruct((tokens, 512), jnp.bfloat16),
            jax.ShapeDtypeStruct(window.shape, jnp.bfloat16),
            jax.ShapeDtypeStruct((tokens, proj.shape[0]), jnp.bfloat16),
            jax.ShapeDtypeStruct((tokens, 128), jnp.float32),
        ),
        compiler_params=pltpu.CompilerParams(vmem_limit_bytes=24 * 2**20),
        cost_estimate=pl.CostEstimate(
            flops=2 * tokens * 288 * 512, bytes_accessed=4 * 2**20, transcendentals=tokens * 512
        ),
        name="conv",
    )(here, *aways, *sums, window, weight, bias, proj)


def in_product_kernel(parts, matrix, squared, s_ref, *refs):
    chunks, (w_ref, o_ref, *rest) = refs[: 4 * parts], refs[4 * parts :]
    held, acc, sems = rest[-3:]
    tokens = chunks[0].shape[0]
    column = pl.multiple_of(s_ref[0] * 512, 512)
    copies = []
    for k in range(4):
        for h in range(2):
            first = h * 8 + 2 * lax.rem(s_ref[1] + k, 4)
            copy = pltpu.make_async_copy(
                w_ref.at[pl.ds(first, 2), pl.ds(matrix * 128, 128), pl.ds(column, 512)],
                held.at[k, h],
                sems.at[k, h],
            )
            copy.start()
            copies.append(copy)
    for k in range(4):
        copies[2 * k].wait()
        copies[2 * k + 1].wait()
        rhs = held[k].reshape(512, 512)
        for p in range(parts):
            a = chunks[4 * p + k]
            at = slice(p * tokens, (p + 1) * tokens)
            lhs = jnp.concatenate([a[:, 0:128], a[:, 256:384], a[:, 128:256], a[:, 384:512]], axis=1)
            total = jnp.dot(lhs, rhs, preferred_element_type=jnp.float32)
            if k == 0:
                acc[at, :] = total
            elif k < 3:
                acc[at, :] += total
            else:
                o_ref[at, :512] = (acc[at, :] + total).astype(o_ref.dtype)
    if squared:
        q_ref = rest[0]
        for p in range(parts):
            at = slice(p * tokens, (p + 1) * tokens)
            squares = None
            for a in chunks[4 * p : 4 * p + 4]:
                real = a[...].astype(jnp.float32)
                squares = real * real if squares is None else squares + real * real
            square = jnp.broadcast_to(jnp.sum(squares, axis=1, keepdims=True), (tokens, 128))
            q_ref[at, :] = square
            high = square.astype(jnp.bfloat16).astype(jnp.float32)
            lane = lax.broadcasted_iota(jnp.int32, square.shape, 1)
            o_ref[at, 512:] = jnp.where(lane < 64, high, square - high).astype(o_ref.dtype)


def in_product(parts, weights, matrix, column, x, dtype, squared=False):
    tokens = parts[0][0].shape[0] * len(parts)
    scalars = jnp.stack([column, x]).astype(jnp.int32)
    out_shape = jax.ShapeDtypeStruct((tokens, 512), dtype)
    out_specs = IN_VMEM
    if squared:
        out_shape = (
            jax.ShapeDtypeStruct((tokens, 640), dtype),
            jax.ShapeDtypeStruct((tokens, 128), jnp.float32),
        )
        out_specs = (IN_VMEM, IN_VMEM)
    return pl.pallas_call(
        functools.partial(in_product_kernel, len(parts), matrix, squared),
        out_shape=out_shape,
        in_specs=[IN_SMEM] + [IN_VMEM] * (4 * len(parts)) + [IN_HBM],
        out_specs=out_specs,
        scratch_shapes=[
            pltpu.VMEM((4, 2, 2, 128, 512), jnp.bfloat16),
            pltpu.VMEM((tokens, 512), jnp.float32),
            pltpu.SemaphoreType.DMA((4, 2)),
        ],
        compiler_params=pltpu.CompilerParams(vmem_limit_bytes=24 * 2**20),
        cost_estimate=pl.CostEstimate(
            flops=2 * tokens * 2048 * 512, bytes_accessed=6 * 2**20, transcendentals=0
        ),
        name="in_product",
    )(scalars, *(c for part in parts for c in part), weights)


def out_product_kernel(parts, s_ref, *refs):
    chunks, (w_ref, o_ref, held, acc, sems) = refs[: 4 * parts], refs[4 * parts :]
    tokens = chunks[0].shape[0]
    copies = []
    for k in range(4):
        source = lax.rem(s_ref[1] + k, 4)
        rows = pl.multiple_of(source // 2 * 64, 64)
        columns = pl.multiple_of(lax.rem(source, 2) * 512, 512)
        copy = pltpu.make_async_copy(
            w_ref.at[pl.ds(s_ref[0] * 8, 8), pl.ds(rows, 64), pl.ds(columns, 512)], held.at[k], sems.at[k]
        )
        copy.start()
        copies.append(copy)
    for k in range(4):
        copies[k].wait()
        rows = [
            held[k, xs * 2 + co, yh * 32 : yh * 32 + 32, :]
            for co in range(2)
            for yh in range(2)
            for xs in range(4)
        ]
        rhs = jnp.concatenate(rows, axis=0)
        for p in range(parts):
            at = slice(p * tokens, (p + 1) * tokens)
            total = lax.dot_general(
                chunks[4 * p + k][...], rhs, (((1,), (1,)), ((), ())), preferred_element_type=jnp.float32
            )
            if k == 0:
                acc[at, :] = total
            elif k < 3:
                acc[at, :] += total
            else:
                o_ref[at, :] = (acc[at, :] + total).astype(o_ref.dtype)


def out_product(parts, weights, block, x, dtype):
    tokens = parts[0][0].shape[0] * len(parts)
    scalars = jnp.stack([block, x]).astype(jnp.int32)
    return pl.pallas_call(
        functools.partial(out_product_kernel, len(parts)),
        out_shape=jax.ShapeDtypeStruct((tokens, 512), dtype),
        in_specs=[IN_SMEM] + [IN_VMEM] * (4 * len(parts)) + [IN_HBM],
        out_specs=IN_VMEM,
        scratch_shapes=[
            pltpu.VMEM((4, 8, 64, 512), jnp.bfloat16),
            pltpu.VMEM((tokens, 512), jnp.float32),
            pltpu.SemaphoreType.DMA((4,)),
        ],
        compiler_params=pltpu.CompilerParams(vmem_limit_bytes=24 * 2**20),
        cost_estimate=pl.CostEstimate(
            flops=2 * tokens * 2048 * 512, bytes_accessed=6 * 2**20, transcendentals=0
        ),
        name="out_product",
    )(scalars, *(c for part in parts for c in part), weights)


def per_device(
    in_master,
    in_moment,
    in_velocity,
    in_grad,
    out_master,
    out_moment,
    out_velocity,
    out_grad,
    embed_table,
    tokens,
    conv_state,
    ssm_state,
    conv_weight,
    conv_bias,
    x_proj_w,
    dt_proj_w,
    dt_bias,
    a_log,
    d_skip,
):
    bf16 = jnp.bfloat16
    f32 = jnp.float32
    chan = lax.axis_index("chan")
    yh, x = chan // 4, chan % 4
    replicas = lax.axis_size("fsdp")
    vocab_rows, feature_part = embed_table.shape
    steps, rows = tokens.shape
    count = steps * rows
    capacity = 2 * count // replicas

    flat_tokens = tokens.reshape(count)
    owner = flat_tokens // vocab_rows
    order = jnp.arange(count, dtype=jnp.int32)
    before = jnp.logical_and(owner[:, None] == owner[None, :], order[:, None] < order[None, :])
    slot = jnp.sum(before.astype(jnp.int32), axis=0)
    place = owner * capacity + slot
    slots = jnp.arange(replicas * capacity, dtype=jnp.int32)
    hit = place[None, :] == slots[:, None]
    requests = jnp.sum(jnp.where(hit, flat_tokens[None, :] + 1, 0), axis=1) - 1
    in_master, requests = lax.optimization_barrier((in_master, requests))
    asked = lax.all_to_all(
        requests.reshape(replicas, capacity), "fsdp", split_axis=0, concat_axis=0, tiled=True
    )

    own = in_master.shape[0]
    in_new, *pieces = adam_in(in_master, in_moment, in_velocity, in_grad, x)
    first, second, third, fourth, asked = lax.optimization_barrier((*pieces, asked))
    rows_in = jnp.zeros((2, 4 * own, 1024), bf16)
    for k, piece in enumerate((first, second, third, fourth)):
        rows_in = lax.dynamic_update_slice(
            rows_in, lax.ppermute(piece, BOTH, in_route(k)), (0, (x - k) % 4 * own, 0)
        )
    weights_in = lax.all_gather(rows_in.reshape(8 * own, 1024), "fsdp", axis=0, tiled=False)

    offset = jnp.clip(asked - lax.axis_index("fsdp") * vocab_rows, 0, vocab_rows - 1)
    looked = embed_table.at[offset.reshape(-1)].get(mode="promise_in_bounds")
    replies = lax.all_to_all(
        looked.reshape(replicas, capacity, feature_part), "fsdp", split_axis=0, concat_axis=0, tiled=True
    )
    half = count // PARTS
    answers = replies.reshape(replicas * capacity, feature_part)
    found = [
        answers.at[place[p * half : (p + 1) * half]].get(mode="promise_in_bounds") for p in range(PARTS)
    ]

    def spread(parts):
        return [[part] + [from_x(part, k) for k in (1, 2, 3)] for part in parts]

    chunks = spread(found)
    aways, sums = [], []
    for part in chunks:
        away, squares = in_product([part], weights_in, 0, 1 - yh, x, bf16, squared=True)
        aways.append(away)
        sums.append(squares)
    out_new = adam_update(out_master, out_moment, out_velocity, out_grad)
    halves = out_new.astype(bf16).reshape(own, 2, 2048)
    sent = [lax.dynamic_index_in_dim(halves, (yh + j) % 2, 1, keepdims=False) for j in range(2)]
    last, sent0, sent1 = lax.optimization_barrier((aways[-1], *sent))
    aways = [from_partner(away) for away in (*aways[:-1], last)]
    got = [lax.ppermute(sent0, BOTH, out_route(0)), lax.ppermute(sent1, BOTH, out_route(1))]
    here = in_product(chunks, weights_in, 0, yh, x, f32)
    *flat_chunks, here = lax.optimization_barrier((*(c for part in chunks for c in part), here))
    chunks = [flat_chunks[4 * p : 4 * p + 4] for p in range(PARTS)]
    z_away = in_product(chunks, weights_in, 1, 1 - yh, x, bf16)
    z_here = in_product(chunks, weights_in, 1, yh, x, f32)
    act, window, partial_value, scale = conv(
        here, aways, sums, jnp.moveaxis(conv_state, 1, 0), conv_weight, conv_bias[None], x_proj_w
    )

    partials = partial_value.reshape(4, -1, partial_value.shape[1])
    partials, z_away, z_here, got0, got1 = lax.optimization_barrier((partials, z_away, z_here, *got))
    both = jnp.concatenate([jnp.where(yh == 0, got0, got1), jnp.where(yh == 0, got1, got0)], axis=0)
    rows_out = jnp.concatenate([both[:, :1024], both[:, 1024:]], axis=0)
    quarter = lax.dynamic_index_in_dim(partials, x, 0, keepdims=False).astype(f32)
    for k in (1, 2, 3):
        piece = lax.dynamic_index_in_dim(partials, (x - k) % 4, 0, keepdims=False)
        quarter = quarter + from_x(piece, k).astype(f32)
    quarter = (quarter + from_partner(quarter.astype(bf16)).astype(f32)).astype(bf16)
    z_away, quarter, rows_out = lax.optimization_barrier((z_away, quarter, rows_out))
    weights_out = lax.all_gather(rows_out, "fsdp", axis=0, tiled=False)
    shared = jnp.stack([quarter] + [from_x(quarter, k) for k in (1, 2, 3)])
    dbc = jnp.concatenate(
        [lax.dynamic_index_in_dim(shared, (q - x) % 4, 0, keepdims=False) for q in range(4)], axis=0
    ).astype(f32)

    z_away = from_partner(z_away)
    z_in = ((z_here + z_away.astype(f32)) * scale[:, :1]).astype(bf16)

    contract_last = (((1,), (1,)), ((), ()))
    dt_low = dbc[:, :RANK].astype(bf16)
    delta_all = jax.nn.softplus(
        lax.dot_general(dt_low, dt_proj_w, contract_last, preferred_element_type=f32) + dt_bias
    )
    decay = -jnp.exp(a_log)
    state = ssm_state
    gates = []
    for step in range(steps):
        at = slice(step * rows, (step + 1) * rows)
        delta = delta_all[at]
        b_mat = dbc[at, RANK : RANK + NSTATE]
        c_mat = dbc[at, RANK + NSTATE :]
        act_real = act[at].astype(f32)
        state = (
            jnp.exp(delta[:, None, :] * decay[None]) * state
            + (delta * act_real)[:, None, :] * b_mat[:, :, None]
        )
        y_out = jnp.sum(c_mat[:, :, None] * state, axis=1) + d_skip * act_real
        gates.append((y_out * jax.nn.silu(z_in[at].astype(f32))).astype(bf16))
    each = steps // PARTS
    gated = spread([jnp.concatenate(gates[p * each : (p + 1) * each], axis=0) for p in range(PARTS)])

    aways = [from_partner(out_product([part], weights_out, 1 - yh, x, bf16)) for part in gated]
    here = out_product(gated, weights_out, yh, x, f32)
    away = jnp.concatenate(aways, axis=0).astype(f32)
    rows_found = jnp.concatenate(found, axis=0).astype(f32)
    block_out = (rows_found + (here + away)).astype(bf16).reshape(steps, rows, -1)
    return (in_new, out_new, block_out, jnp.moveaxis(window, 0, 1), state)


def solution(mesh):
    split = P(("fsdp", "chan"), None, None)
    flat = P(("fsdp", "chan"), None)
    placed = (
        split,
        split,
        split,
        split,
        flat,
        flat,
        flat,
        flat,
        P("fsdp", "chan"),
        P(None, "fsdp"),
        P("fsdp", None, "chan"),
        P("fsdp", None, "chan"),
        P(None, "chan"),
        P("chan"),
        P(None, "chan"),
        P("chan", None),
        P("chan"),
        P(None, "chan"),
        P("chan"),
    )
    return jax.shard_map(
        per_device,
        mesh=mesh,
        in_specs=placed,
        out_specs=(
            split,
            flat,
            P(None, "fsdp", "chan"),
            P("fsdp", None, "chan"),
            P("fsdp", None, "chan"),
        ),
        check_vma=False,
    )
```

time: 280 us -> 229 us (0.82)
  waiting for transfers between devices: 127 us -> 75.3 us
  Pallas kernels: 16.5 us -> 24 us
  other arithmetic: 21.5 us -> 14.1 us
    all_to_all x2 -> x0, waiting for transfers between devices: 27.4 us -> none  [the longest x1 27.4 us: per_device(): lax.all_to_all(jnp.broadcast_to(partial_value[None], (8, *partial_value.s...]
    ppermute x6 -> x18, waiting for transfers between devices: 37.6 us -> 17.2 us  [from_x(): lax.ppermute(a, 'chan', [(i, i // 4 * 4 + (i % 4 - k) % 4) for i in range...]
    all_to_all x2 -> x0, starting transfers between devices: 16.9 us -> none  [the longest x1 9.62 us: per_device(): lax.all_to_all(jnp.broadcast_to(squares[None], (8, steps, rows)), 'chan',...]
    ppermute x6 -> x18, starting transfers between devices: 7.32 us -> 22.4 us  [from_x(): lax.ppermute(a, 'chan', [(i, i // 4 * 4 + (i % 4 - k) % 4) for i in range...]
    ppermute x10 -> x6, starting transfers between devices: 27.9 us -> 13.7 us  [the longest x1 5.1 us: per_device(): lax.ppermute(sent1, BOTH, out_route(1))]
    ppermute x3 -> x6, starting transfers between devices: 4.73 us -> 14.5 us  [from_partner(): return lax.ppermute(a, 'chan', [(i, i ^ 4) for i in range(8)])]
    unnamed x70 -> x53, local copies, waits for them, and re-layouts: 9.14 us -> 18 us
    pallas_call x6 -> x10, Pallas kernels: 16.5 us -> 24 us  [the longest x5 11.7 us: in_product(): pl.pallas_call(functools.partial(in_product_kernel, len(parts), matrix, s...]
  transfers between devices with their start and end apart: 25 -> 34, of which waited for: 14 -> 19; matrix products, arithmetic and copies ran while one was open for 6% -> 12% of each run, Pallas kernels for 5% -> 11%
where the time goes in v4:
time: 229 us; the launch traced here: 228 us
  waiting for transfers between devices  75.3 us (33%)
  starting transfers between devices  67.8 us (30%)
  local copies, waits for them, and re-layouts  31 us (14%)
  Pallas kernels  24 us (10%)
  between operations  14.7 us (6%)
  other arithmetic  14.1 us (6%)
    all_to_all x1, waiting for transfers between devices, per_device(): lax.all_to_all(looked.reshape(replicas, capacity, feature_part), 'fsdp',...  26.7 us
    ppermute x18, starting transfers between devices, from_x(): lax.ppermute(a, 'chan', [(i, i // 4 * 4 + (i % 4 - k) % 4) for i in range...  22.4 us
    unnamed x53, local copies, waits for them, and re-layouts  18 us
    ppermute x18, waiting for transfers between devices, from_x(): lax.ppermute(a, 'chan', [(i, i // 4 * 4 + (i % 4 - k) % 4) for i in range...  17.2 us
    ppermute x6, waiting for transfers between devices, from_partner(): return lax.ppermute(a, 'chan', [(i, i ^ 4) for i in range(8)])  16.3 us
    ppermute x6, starting transfers between devices, from_partner(): return lax.ppermute(a, 'chan', [(i, i ^ 4) for i in range(8)])  14.5 us
    pallas_call x5, Pallas kernels, in_product(): pl.pallas_call(functools.partial(in_product_kernel, len(parts), matrix, s...  11.7 us
    all_to_all x1, starting transfers between devices, per_device(): lax.all_to_all(looked.reshape(replicas, capacity, feature_part), 'fsdp',...  10.7 us
  transfers between devices with their start and end apart: 34, of which 19 were waited for; matrix products, arithmetic and copies ran while one was open for 12% of the time, Pallas kernels for 11%

profile of v4, /device:TPU:6, one launch (start us, length us, event | category | flops | bytes accessed | tf_op | source)
XLA Modules:
  0.0 227.7 jit_solution(12785883982177814090)
XLA Ops:
  9.1 6.4 %all-to-all-start = ((s32[16,1,64]{2,1,0:T(1,128)}), s32[16,1,64]{2,1,0:T(1,128)S(1)}, u32[]{:S(2)}, u32[]{:S(2)}) async-start(s32[16,1,64]{2,1,0:T(1,128)} %all_to_all.11), calls=%async_computation | async-start | bytes 16384 | tf_op jit(solution)/shard_map/all_to_all | solution.py:332
  15.6 1.2 copy-done.5
  16.8 1.2 copy-done.6
  18.0 1.2 copy-done.7
  19.3 1.0 copy-done.9
  20.3 3.3 %adam_in.1 = (f32[2048,128]{1,0:T(8,128)}, bf16[2,32,1024]{2,1,0:T(8,128)(2,1)S(1)}, bf16[2,32,1024]{2,1,0:T(8,128)(2,1)S(1)}, bf16[2,32,1024]{2,1,0:T(8,128)(2,1)S(1)}, bf16[2,32,1024]{2,1,0:T(8,128)(2,1)S(1)}) custom-call(s32[1]{0:T(128)} %bitcast.s_ref, f32[2048,128]{1,0:T(8,128)S(1)} %bitcast.91, f32[2048,128]{1,0:T(8,128)S(1)} %bitcast.92, ...), custom_call_target="tpu_custom_call" | custom-call | flops 5242880 | bytes 5242880 | tf_op jit(solution)/shard_map/adam_in/pallas_call | solution.py:98
  24.8 2.4 %collective-permute-start.8 = (bf16[2,32,1024]{2,1,0:T(8,128)(2,1)S(1)}, bf16[2,32,1024]{2,1,0:T(8,128)(2,1)S(1)}, u32[]{:S(2)}, u32[]{:S(2)}) collective-permute-start(bf16[2,32,1024]{2,1,0:T(8,128)(2,1)S(1)} %get-tuple-element.55), channel_id=1, source_target_pairs={{0,2},{1,3},{2,0},{3,1},{4,66},{5,67},{6,64},{7,65},{8,10},{9,11},... | collective-permute-start | bytes 393224 | tf_op jit(solution)/shard_map/ppermute | solution.py:342
  27.3 3.3 %collective-permute-done.7 = bf16[2,32,1024]{2,1,0:T(8,128)(2,1)S(1)} collective-permute-done((bf16[2,32,1024]{2,1,0:T(8,128)(2,1)S(1)}, bf16[2,32,1024]{2,1,0:T(8,128)(2,1)S(1)}, u32[]{:S(2)}, u32[]{:S(2)}) %collective-permute-start.7) | collective-permute-done | bytes 131104 | tf_op jit(solution)/shard_map/ppermute | solution.py:342
  30.7 2.0 collective-permute-done.8
  32.7 2.0 collective-permute-done.9
  35.7 8.0 %gather_fusion = bf16[1024,512]{1,0:T(8,128)(2,1)} fusion(bf16[4096,512]{1,0:T(8,128)(2,1)} %param.27, s32[1024]{0:T(1024)S(1)} %broadcast_clamp_fusion), kind=kCustom, calls=%fused_computation | custom fusion | bytes 2101248 | tf_op jit(solution)/shard_map/gather | solution.py:347
  43.7 10.7 %all-to-all-start.1 = ((bf16[16,64,512]{2,1,0:T(8,128)(2,1)}), bf16[16,64,512]{2,1,0:T(8,128)(2,1)S(1)}, u32[]{:S(2)}, u32[]{:S(2)}) async-start(bf16[16,64,512]{2,1,0:T(8,128)(2,1)} %bitcast.19), calls=%async_computation.1 | async-start | bytes 2097152 | tf_op jit(solution)/shard_map/all_to_all | solution.py:348
  54.5 1.2 fusion.45
  55.7 26.7 %all-to-all-done.1 = bf16[16,64,512]{2,1,0:T(8,128)(2,1)S(1)} async-done(((bf16[16,64,512]{2,1,0:T(8,128)(2,1)}), bf16[16,64,512]{2,1,0:T(8,128)(2,1)S(1)}, u32[]{:S(2)}, u32[]{:S(2)}) %all-to-all-start.1) | async-done | bytes 1048608 | tf_op jit(solution)/shard_map/all_to_all | solution.py:348
  82.4 1.2 gather_fusion.2
  83.6 0.9 collective-permute-start.3
  84.6 1.3 constant_dynamic-slice_fusion
  86.0 1.7 collective-permute-start.4
  87.7 1.5 collective-permute-start.5
  89.2 1.2 gather_fusion.1
  91.0 1.8 collective-permute-start.1
  92.8 6.3 %collective-permute-done.3.refs_5_.refs_1_ = bf16[256,512]{1,0:T(8,128)(2,1)S(1)} collective-permute-done((bf16[256,512]{1,0:T(8,128)(2,1)S(1)}, bf16[256,512]{1,0:T(8,128)(2,1)S(1)}, u32[]{:S(2)}, u32[]{:S(2)}) %collective-permute-start.3) | collective-permute-done | bytes 262176 | tf_op jit(solution)/shard_map/ppermute | solution.py:54
  99.1 1.9 copy_bitcast_fusion
  101.0 1.1 collective-permute-done.5.refs_7_.refs_3_
  102.1 3.4 %all-gather.4.cloned.1.call-done.refs_8_.refs_4_ = bf16[16,256,1024]{2,1,0:T(8,128)(2,1)} async-done(((bf16[1,256,1024]{2,1,0:T(8,128)(2,1)}), bf16[16,256,1024]{2,1,0:T(8,128)(2,1)}) %all-gather.4.cloned.1.call-update) | async-done | bytes 8388624 | tf_op jit(solution)/shard_map/all_gather | solution.py:344
  105.5 3.4 %copy-done.1 = bf16[16,256,1024]{2,1,0:T(8,128)(2,1)S(1)} copy-done((bf16[16,256,1024]{2,1,0:T(8,128)(2,1)S(1)}, bf16[16,256,1024]{2,1,0:T(8,128)(2,1)}, u32[]{:S(2)}) %copy-start.1) | copy-done | bytes 8388632
  108.9 2.5 %in_product.7 = (bf16[256,640]{1,0:T(8,128)(2,1)}, f32[256,128]{1,0:T(8,128)S(1)}) custom-call(s32[2]{0:T(128)S(1)} %pad_add_fusion.1.s_ref, bf16[256,512]{1,0:T(8,128)(2,1)S(1)} %gather_fusion.2, bf16[256,512]{1,0:T(8,128)(2,1)S(1)} %collective-permute-done.3.refs_5_.refs_1_, bf16[256,512]{1,0:T(8,128)(2,1)S(1)} %collective-permute-done.4.refs_6_.refs_2_, ...), custom_call_target="tpu_custom_call" | custom-call | flops 536870912 | bytes 6291456 | tf_op jit(solution)/shard_map/in_product/pallas_call | solution.py:217
  111.4 3.3 %collective-permute-start.11 = (bf16[256,640]{1,0:T(8,128)(2,1)}, bf16[256,640]{1,0:T(8,128)(2,1)}, u32[]{:S(2)}, u32[]{:S(2)}) collective-permute-start(bf16[256,640]{1,0:T(8,128)(2,1)} %get-tuple-element.60), channel_id=1, source_target_pairs={{0,4},{1,5},{2,6},{3,7},{4,0},{5,1},{6,2},{7,3},{8,12},{9,13},{10,... | collective-permute-start | bytes 983048 | tf_op jit(solution)/shard_map/ppermute | solution.py:58
  114.7 2.5 %in_product.6 = (bf16[256,640]{1,0:T(8,128)(2,1)}, f32[256,128]{1,0:T(8,128)S(1)}) custom-call(s32[2]{0:T(128)S(1)} %pad_add_fusion.1.s_ref, bf16[256,512]{1,0:T(8,128)(2,1)S(1)} %gather_fusion.1, bf16[256,512]{1,0:T(8,128)(2,1)S(1)} %collective-permute-done.refs_1_, bf16[256,512]{1,0:T(8,128)(2,1)S(1)} %collective-permute-done.1.refs_2_, ...), custom_call_target="tpu_custom_call" | custom-call | flops 536870912 | bytes 6291456 | tf_op jit(solution)/shard_map/in_product/pallas_call | solution.py:217
  118.5 3.4 %copy-done.2 = bf16[16,256,1024]{2,1,0:T(8,128)(2,1)S(1)} copy-done((bf16[16,256,1024]{2,1,0:T(8,128)(2,1)S(1)}, bf16[16,256,1024]{2,1,0:T(8,128)(2,1)}, u32[]{:S(2)}) %copy-start.2) | copy-done | bytes 8388632
  121.8 2.2 in_product.5.here
  124.1 4.9 %collective-permute-start.12 = (bf16[32,2048]{1,0:T(8,128)(2,1)}, bf16[32,2048]{1,0:T(8,128)(2,1)S(1)}, u32[]{:S(2)}, u32[]{:S(2)}) collective-permute-start(bf16[32,2048]{1,0:T(8,128)(2,1)} %get-tuple-element.72), channel_id=1, source_target_pairs={{0,0},{1,16},{2,32},{3,48},{4,4},{5,20},{6,36},{7,52},{8,8},{9,24}... | collective-permute-start | bytes 393224 | tf_op jit(solution)/shard_map/ppermute | solution.py:371
  129.1 5.1 %collective-permute-start.13 = (bf16[32,2048]{1,0:T(8,128)(2,1)}, bf16[32,2048]{1,0:T(8,128)(2,1)S(1)}, u32[]{:S(2)}, u32[]{:S(2)}) collective-permute-start(bf16[32,2048]{1,0:T(8,128)(2,1)} %get-tuple-element.73), channel_id=1, source_target_pairs={{0,4},{1,20},{2,36},{3,52},{4,0},{5,16},{6,32},{7,48},{8,12},{9,28... | collective-permute-start | bytes 393224 | tf_op jit(solution)/shard_map/ppermute | solution.py:371
  134.2 2.2 in_product.9
  136.5 2.2 in_product.8
  138.8 2.7 %conv.1 = (bf16[512,512]{1,0:T(8,128)(2,1)S(1)}, bf16[3,128,512]{2,1,0:T(8,128)(2,1)}, bf16[512,288]{1,0:T(8,128)(2,1)S(1)}, f32[512,128]{1,0:T(8,128)S(1)}) custom-call(f32[512,512]{1,0:T(8,128)S(1)} %in_product.5.here, bf16[256,640]{1,0:T(8,128)(2,1)} %collective-permute-done.10.refs_0_, bf16[256,640]{1,0:T(8,128)(2,1)} %collective-permute-done.11.refs_1_, ...), custom_call_target="tpu_custom_call" | custom-call | flops 150994944 | bytes 4194304 | tf_op jit(solution)/shard_map/conv/pallas_call | solution.py:144
  141.6 1.7 collective-permute-done.12
  143.3 2.6 %collective-permute-done.13 = bf16[32,2048]{1,0:T(8,128)(2,1)S(1)} collective-permute-done((bf16[32,2048]{1,0:T(8,128)(2,1)}, bf16[32,2048]{1,0:T(8,128)(2,1)S(1)}, u32[]{:S(2)}, u32[]{:S(2)}) %collective-permute-start.13) | collective-permute-done | bytes 131104 | tf_op jit(solution)/shard_map/ppermute | solution.py:371
  146.1 3.1 %collective-permute-start.16 = (bf16[128,288]{1,0:T(8,128)(2,1)S(1)}, bf16[128,288]{1,0:T(8,128)(2,1)S(1)}, u32[]{:S(2)}, u32[]{:S(2)}) collective-permute-start(bf16[128,288]{1,0:T(8,128)(2,1)S(1)} %get-tuple-element.122), channel_id=1, source_target_pairs={{0,1},{1,2},{2,3},{3,0},{4,5},{5,6},{6,7},{7,4},{8,9},{9,10},{10,1... | collective-permute-start | bytes 221192 | tf_op jit(solution)/shard_map/ppermute | solution.py:54
  149.3 3.6 %collective-permute-done.14 = bf16[128,288]{1,0:T(8,128)(2,1)S(1)} collective-permute-done((bf16[128,288]{1,0:T(8,128)(2,1)S(1)}, bf16[128,288]{1,0:T(8,128)(2,1)S(1)}, u32[]{:S(2)}, u32[]{:S(2)}) %collective-permute-start.14) | collective-permute-done | bytes 73760 | tf_op jit(solution)/shard_map/ppermute | solution.py:54
  153.8 2.7 %collective-permute-start.17 = (bf16[128,288]{1,0:T(8,128)(2,1)S(1)}, bf16[128,288]{1,0:T(8,128)(2,1)S(1)}, u32[]{:S(2)}, u32[]{:S(2)}) collective-permute-start(bf16[128,288]{1,0:T(8,128)(2,1)S(1)} %fusion.40), channel_id=1, source_target_pairs={{0,4},{1,5},{2,6},{3,7},{4,0},{5,1},{6,2},{7,3},{8,12},{9,13},{10,... | collective-permute-start | bytes 221192 | tf_op jit(solution)/shard_map/ppermute | solution.py:58
  157.2 2.8 %collective-permute-done.17 = bf16[128,288]{1,0:T(8,128)(2,1)S(1)} collective-permute-done((bf16[128,288]{1,0:T(8,128)(2,1)S(1)}, bf16[128,288]{1,0:T(8,128)(2,1)S(1)}, u32[]{:S(2)}, u32[]{:S(2)}) %collective-permute-start.17) | collective-permute-done | bytes 73760 | tf_op jit(solution)/shard_map/ppermute | solution.py:58
  161.0 1.0 collective-permute-start.18
  162.0 2.9 %collective-permute-start.19 = (bf16[128,288]{1,0:T(8,128)(2,1)S(1)}, bf16[128,288]{1,0:T(8,128)(2,1)S(1)}, u32[]{:S(2)}, u32[]{:S(2)}) collective-permute-start(bf16[128,288]{1,0:T(8,128)(2,1)S(1)} %add_convert_fusion.1), channel_id=1, source_target_pairs={{0,2},{1,3},{2,0},{3,1},{4,6},{5,7},{6,4},{7,5},{8,10},{9,11},{10,... | collective-permute-start | bytes 221192 | tf_op jit(solution)/shard_map/ppermute | solution.py:54
  165.0 2.7 %collective-permute-start.21 = (bf16[512,512]{1,0:T(8,128)(2,1)}, bf16[512,512]{1,0:T(8,128)(2,1)S(1)}, u32[]{:S(2)}, u32[]{:S(2)}) collective-permute-start(bf16[512,512]{1,0:T(8,128)(2,1)} %copy-done.8), channel_id=1, source_target_pairs={{0,4},{1,5},{2,6},{3,7},{4,0},{5,1},{6,2},{7,3},{8,12},{9,13},{10,... | collective-permute-start | bytes 1572872 | tf_op jit(solution)/shard_map/ppermute | solution.py:58
  168.5 1.0 collective-permute-done.20
  171.0 0.9 copy-done.16
  171.9 7.7 %multiply_reduce_fusion = (f32[128,512]{1,0:T(8,128)S(1)}, f32[128,16,512]{2,1,0:T(8,128)}, f32[128,512]{1,0:T(8,128)S(1)}, f32[128,512]{1,0:T(8,128)S(1)}, f32[128,512]{1,0:T(8,128)S(1)}) fusion(f32[128,16]{1,0:T(8,128)S(1)} %get-tuple-element.108, f32[128,16]{1,0:T(8,128)S(1)} %get-tuple-element.107, f32[128,512]{1,0:T(8,128)S(1)} %get-tuple-element.95, ...), kind=kLoop, calls=%fused_computation.3 | loop fusion | flops 24903680 | bytes 11632640 | tf_op jit(solution)/shard_map/reduce_sum | solution.py:418
  179.6 7.8 %collective-permute-done.21 = bf16[512,512]{1,0:T(8,128)(2,1)S(1)} collective-permute-done((bf16[512,512]{1,0:T(8,128)(2,1)}, bf16[512,512]{1,0:T(8,128)(2,1)S(1)}, u32[]{:S(2)}, u32[]{:S(2)}) %collective-permute-start.21) | collective-permute-done | bytes 524320 | tf_op jit(solution)/shard_map/ppermute | solution.py:58
  188.1 2.6 %collective-permute-start.22 = (bf16[256,512]{1,0:T(8,128)(2,1)S(1)}, bf16[256,512]{1,0:T(8,128)(2,1)S(1)}, u32[]{:S(2)}, u32[]{:S(2)}) collective-permute-start(bf16[256,512]{1,0:T(8,128)(2,1)S(1)} %pad_maximum_fusion.3.refs_0_), channel_id=1, source_target_pairs={{0,3},{1,0},{2,1},{3,2},{4,7},{5,4},{6,5},{7,6},{8,11},{9,8},{10,9... | collective-permute-start | bytes 786440 | tf_op jit(solution)/shard_map/ppermute | solution.py:54
  190.7 0.9 collective-permute-start.23
  191.6 2.5 %collective-permute-start.24 = (bf16[256,512]{1,0:T(8,128)(2,1)S(1)}, bf16[256,512]{1,0:T(8,128)(2,1)S(1)}, u32[]{:S(2)}, u32[]{:S(2)}) collective-permute-start(bf16[256,512]{1,0:T(8,128)(2,1)S(1)} %pad_maximum_fusion.3.refs_0_), channel_id=1, source_target_pairs={{0,1},{1,2},{2,3},{3,0},{4,5},{5,6},{6,7},{7,4},{8,9},{9,10},{10,1... | collective-permute-start | bytes 786440 | tf_op jit(solution)/shard_map/ppermute | solution.py:54
  194.2 2.1 collective-permute-start.26
  196.3 1.2 collective-permute-done.22.refs_1_
  198.0 2.3 %collective-permute-done.23.refs_2_ = bf16[256,512]{1,0:T(8,128)(2,1)S(1)} collective-permute-done((bf16[256,512]{1,0:T(8,128)(2,1)S(1)}, bf16[256,512]{1,0:T(8,128)(2,1)S(1)}, u32[]{:S(2)}, u32[]{:S(2)}) %collective-permute-start.23) | collective-permute-done | bytes 262176 | tf_op jit(solution)/shard_map/ppermute | solution.py:54
  200.4 2.2 copy-done.3
  202.6 1.9 out_product.4
  204.5 4.0 %collective-permute-start.28 = (bf16[256,512]{1,0:T(8,128)(2,1)S(1)}, bf16[256,512]{1,0:T(8,128)(2,1)S(1)}, u32[]{:S(2)}, u32[]{:S(2)}) collective-permute-start(bf16[256,512]{1,0:T(8,128)(2,1)S(1)} %out_product.4), channel_id=1, source_target_pairs={{0,4},{1,5},{2,6},{3,7},{4,0},{5,1},{6,2},{7,3},{8,12},{9,13},{10,... | collective-permute-start | bytes 786440 | tf_op jit(solution)/shard_map/ppermute | solution.py:58
  208.5 1.9 out_product.5
  210.4 1.4 collective-permute-start.29
  211.8 2.4 %out_product.3 = f32[512,512]{1,0:T(8,128)S(1)} custom-call(s32[2]{0:T(128)S(1)} %pad_add_fusion.s_ref, bf16[256,512]{1,0:T(8,128)(2,1)S(1)} %pad_maximum_fusion.3.refs_0_, bf16[256,512]{1,0:T(8,128)(2,1)S(1)} %collective-permute-done.22.refs_1_, bf16[256,512]{1,0:T(8,128)(2,1)S(1)} %collective-permute-done.23.refs_2_, ...), custom_call_target="tpu_custom_call" | custom-call | flops 1073741824 | bytes 6291456 | tf_op jit(solution)/shard_map/out_product/pallas_call | solution.py:273
  214.2 1.4 collective-permute-done.28
  215.7 4.2 %collective-permute-done.29 = bf16[256,512]{1,0:T(8,128)(2,1)S(1)} collective-permute-done((bf16[256,512]{1,0:T(8,128)(2,1)S(1)}, bf16[256,512]{1,0:T(8,128)(2,1)S(1)}, u32[]{:S(2)}, u32[]{:S(2)}) %collective-permute-start.29) | collective-permute-done | bytes 262176 | tf_op jit(solution)/shard_map/ppermute | solution.py:58
  219.9 1.0 add_convert_fusion
  (116 shorter events, 12.9 us)
Async XLA Ops:
  7.2 162.7 %copy-start = (bf16[512,256]{1,0:T(8,128)(2,1)S(1)}, bf16[512,256]{1,0:T(8,128)(2,1)}, u32[]{:S(2)}) copy-start(bf16[512,256]{1,0:T(8,128)(2,1)} %param.34) | copy-start | bytes 786436
  9.1 14.5 %all-to-all-start = ((s32[16,1,64]{2,1,0:T(1,128)}), s32[16,1,64]{2,1,0:T(1,128)S(1)}, u32[]{:S(2)}, u32[]{:S(2)}) async-start(s32[16,1,64]{2,1,0:T(1,128)} %all_to_all.11), calls=%async_computation | async-start | bytes 16384 | tf_op jit(solution)/shard_map/all_to_all | solution.py:332
  15.5 90.0 %all-gather.4.cloned.1.call-start = ((), (), s32[]{:S(2)}) async-start(), calls=%async_computation.2 | async-start | bytes 8912896 | tf_op jit(solution)/shard_map/all_gather | solution.py:344
  15.6 1.2 copy-start.5
  16.8 1.2 copy-start.6
  18.0 1.2 copy-start.7
  19.3 1.0 copy-start.9
  23.6 3.6 %collective-permute-start.6 = (bf16[2,32,1024]{2,1,0:T(8,128)(2,1)S(1)}, bf16[2,32,1024]{2,1,0:T(8,128)(2,1)S(1)}, u32[]{:S(2)}, u32[]{:S(2)}) collective-permute-start(bf16[2,32,1024]{2,1,0:T(8,128)(2,1)S(1)} %get-tuple-element.53), channel_id=1, source_target_pairs={{0,0},{1,1},{2,2},{3,3},{4,64},{5,65},{6,66},{7,67},{8,8},{9,9},{1... | collective-permute-start | bytes 393224 | tf_op jit(solution)/shard_map/ppermute | solution.py:342
  24.3 6.4 %collective-permute-start.7 = (bf16[2,32,1024]{2,1,0:T(8,128)(2,1)S(1)}, bf16[2,32,1024]{2,1,0:T(8,128)(2,1)S(1)}, u32[]{:S(2)}, u32[]{:S(2)}) collective-permute-start(bf16[2,32,1024]{2,1,0:T(8,128)(2,1)S(1)} %get-tuple-element.54), channel_id=1, source_target_pairs={{0,1},{1,2},{2,3},{3,0},{4,65},{5,66},{6,67},{7,64},{8,9},{9,10},{... | collective-permute-start | bytes 393224 | tf_op jit(solution)/shard_map/ppermute | solution.py:342
  24.8 7.8 %collective-permute-start.8 = (bf16[2,32,1024]{2,1,0:T(8,128)(2,1)S(1)}, bf16[2,32,1024]{2,1,0:T(8,128)(2,1)S(1)}, u32[]{:S(2)}, u32[]{:S(2)}) collective-permute-start(bf16[2,32,1024]{2,1,0:T(8,128)(2,1)S(1)} %get-tuple-element.55), channel_id=1, source_target_pairs={{0,2},{1,3},{2,0},{3,1},{4,66},{5,67},{6,64},{7,65},{8,10},{9,11},... | collective-permute-start | bytes 393224 | tf_op jit(solution)/shard_map/ppermute | solution.py:342
  27.3 7.4 %collective-permute-start.9 = (bf16[2,32,1024]{2,1,0:T(8,128)(2,1)S(1)}, bf16[2,32,1024]{2,1,0:T(8,128)(2,1)S(1)}, u32[]{:S(2)}, u32[]{:S(2)}) collective-permute-start(bf16[2,32,1024]{2,1,0:T(8,128)(2,1)S(1)} %get-tuple-element.56), channel_id=1, source_target_pairs={{0,3},{1,0},{2,1},{3,2},{4,67},{5,64},{6,65},{7,66},{8,11},{9,8},{... | collective-permute-start | bytes 393224 | tf_op jit(solution)/shard_map/ppermute | solution.py:342
  34.7 0.8 copy-start.17
  35.7 18.8 %copy-start.18 = (f32[32,4096]{1,0:T(8,128)S(1)}, f32[32,4096]{1,0:T(8,128)}, u32[]{:S(2)}) copy-start(f32[32,4096]{1,0:T(8,128)} %param.23) | copy-start | bytes 1572868
  35.7 18.8 %copy-start.19 = (f32[32,4096]{1,0:T(8,128)S(1)}, f32[32,4096]{1,0:T(8,128)}, u32[]{:S(2)}) copy-start(f32[32,4096]{1,0:T(8,128)} %param.25) | copy-start | bytes 1572868
  35.7 18.8 %copy-start.20 = (f32[32,4096]{1,0:T(8,128)S(1)}, f32[32,4096]{1,0:T(8,128)}, u32[]{:S(2)}) copy-start(f32[32,4096]{1,0:T(8,128)} %param.24) | copy-start | bytes 1572868
  35.7 18.8 %copy-start.21 = (bf16[32,4096]{1,0:T(8,128)(2,1)S(1)}, bf16[32,4096]{1,0:T(8,128)(2,1)}, u32[]{:S(2)}) copy-start(bf16[32,4096]{1,0:T(8,128)(2,1)} %param.26) | copy-start | bytes 786436
  43.7 38.7 %all-to-all-start.1 = ((bf16[16,64,512]{2,1,0:T(8,128)(2,1)}), bf16[16,64,512]{2,1,0:T(8,128)(2,1)S(1)}, u32[]{:S(2)}, u32[]{:S(2)}) async-start(bf16[16,64,512]{2,1,0:T(8,128)(2,1)} %bitcast.19), calls=%async_computation.1 | async-start | bytes 2097152 | tf_op jit(solution)/shard_map/all_to_all | solution.py:348
  54.4 146.0 %all-gather.6.cloned.1.call-start = ((), (), s32[]{:S(2)}) async-start(), calls=%async_computation.3 | async-start | bytes 4456448 | tf_op jit(solution)/shard_map/all_gather | solution.py:391
  83.6 15.5 %collective-permute-start.3 = (bf16[256,512]{1,0:T(8,128)(2,1)S(1)}, bf16[256,512]{1,0:T(8,128)(2,1)S(1)}, u32[]{:S(2)}, u32[]{:S(2)}) collective-permute-start(bf16[256,512]{1,0:T(8,128)(2,1)S(1)} %gather_fusion.2), channel_id=1, source_target_pairs={{0,3},{1,0},{2,1},{3,2},{4,7},{5,4},{6,5},{7,6},{8,11},{9,8},{10,9... | collective-permute-start | bytes 786440 | tf_op jit(solution)/shard_map/ppermute | solution.py:54
  86.0 15.1 %collective-permute-start.4 = (bf16[256,512]{1,0:T(8,128)(2,1)S(1)}, bf16[256,512]{1,0:T(8,128)(2,1)S(1)}, u32[]{:S(2)}, u32[]{:S(2)}) collective-permute-start(bf16[256,512]{1,0:T(8,128)(2,1)S(1)} %gather_fusion.2), channel_id=1, source_target_pairs={{0,2},{1,3},{2,0},{3,1},{4,6},{5,7},{6,4},{7,5},{8,10},{9,11},{10,... | collective-permute-start | bytes 786440 | tf_op jit(solution)/shard_map/ppermute | solution.py:54
  87.7 14.4 %collective-permute-start.5 = (bf16[256,512]{1,0:T(8,128)(2,1)S(1)}, bf16[256,512]{1,0:T(8,128)(2,1)S(1)}, u32[]{:S(2)}, u32[]{:S(2)}) collective-permute-start(bf16[256,512]{1,0:T(8,128)(2,1)S(1)} %gather_fusion.2), channel_id=1, source_target_pairs={{0,1},{1,2},{2,3},{3,0},{4,5},{5,6},{6,7},{7,4},{8,9},{9,10},{10,1... | collective-permute-start | bytes 786440 | tf_op jit(solution)/shard_map/ppermute | solution.py:54
  90.3 24.4 %collective-permute-start = (bf16[256,512]{1,0:T(8,128)(2,1)S(1)}, bf16[256,512]{1,0:T(8,128)(2,1)S(1)}, u32[]{:S(2)}, u32[]{:S(2)}) collective-permute-start(bf16[256,512]{1,0:T(8,128)(2,1)S(1)} %gather_fusion.1), channel_id=1, source_target_pairs={{0,3},{1,0},{2,1},{3,2},{4,7},{5,4},{6,5},{7,6},{8,11},{9,8},{10,9... | collective-permute-start | bytes 786440 | tf_op jit(solution)/shard_map/ppermute | solution.py:54
  91.0 23.8 %collective-permute-start.1 = (bf16[256,512]{1,0:T(8,128)(2,1)S(1)}, bf16[256,512]{1,0:T(8,128)(2,1)S(1)}, u32[]{:S(2)}, u32[]{:S(2)}) collective-permute-start(bf16[256,512]{1,0:T(8,128)(2,1)S(1)} %gather_fusion.1), channel_id=1, source_target_pairs={{0,2},{1,3},{2,0},{3,1},{4,6},{5,7},{6,4},{7,5},{8,10},{9,11},{10,... | collective-permute-start | bytes 786440 | tf_op jit(solution)/shard_map/ppermute | solution.py:54
  99.1 15.6 %collective-permute-start.2 = (bf16[256,512]{1,0:T(8,128)(2,1)S(1)}, bf16[256,512]{1,0:T(8,128)(2,1)S(1)}, u32[]{:S(2)}, u32[]{:S(2)}) collective-permute-start(bf16[256,512]{1,0:T(8,128)(2,1)S(1)} %gather_fusion.1), channel_id=1, source_target_pairs={{0,1},{1,2},{2,3},{3,0},{4,5},{5,6},{6,7},{7,4},{8,9},{9,10},{10,1... | collective-permute-start | bytes 786440 | tf_op jit(solution)/shard_map/ppermute | solution.py:54
  105.5 3.4 %copy-start.1 = (bf16[16,256,1024]{2,1,0:T(8,128)(2,1)S(1)}, bf16[16,256,1024]{2,1,0:T(8,128)(2,1)}, u32[]{:S(2)}) copy-start(bf16[16,256,1024]{2,1,0:T(8,128)(2,1)} %all-gather.4.cloned.1.call-done.refs_8_.refs_4_) | copy-start | bytes 25165828
  111.4 27.3 %collective-permute-start.11 = (bf16[256,640]{1,0:T(8,128)(2,1)}, bf16[256,640]{1,0:T(8,128)(2,1)}, u32[]{:S(2)}, u32[]{:S(2)}) collective-permute-start(bf16[256,640]{1,0:T(8,128)(2,1)} %get-tuple-element.60), channel_id=1, source_target_pairs={{0,4},{1,5},{2,6},{3,7},{4,0},{5,1},{6,2},{7,3},{8,12},{9,13},{10,... | collective-permute-start | bytes 983048 | tf_op jit(solution)/shard_map/ppermute | solution.py:58
  117.2 0.7 copy-start.12
  117.9 20.9 %collective-permute-start.10 = (bf16[256,640]{1,0:T(8,128)(2,1)}, bf16[256,640]{1,0:T(8,128)(2,1)}, u32[]{:S(2)}, u32[]{:S(2)}) collective-permute-start(bf16[256,640]{1,0:T(8,128)(2,1)} %get-tuple-element.58), channel_id=1, source_target_pairs={{0,4},{1,5},{2,6},{3,7},{4,0},{5,1},{6,2},{7,3},{8,12},{9,13},{10,... | collective-permute-start | bytes 983048 | tf_op jit(solution)/shard_map/ppermute | solution.py:58
  118.5 3.4 %copy-start.2 = (bf16[16,256,1024]{2,1,0:T(8,128)(2,1)S(1)}, bf16[16,256,1024]{2,1,0:T(8,128)(2,1)}, u32[]{:S(2)}) copy-start(bf16[16,256,1024]{2,1,0:T(8,128)(2,1)} %all-gather.4.cloned.1.call-done.refs_8_.refs_4_) | copy-start | bytes 25165828
  121.8 14.6 %slice-start = ((s8[8388608]{0:T(1024)(128)(4,1)}), s8[4194304]{0:T(1024)(128)(4,1)S(1)}, s32[]{:S(2)}) async-start(s8[8388608]{0:T(1024)(128)(4,1)} %bitcast.86), calls=%async_computation.4 | async-start | bytes 8388608
  124.1 12.3 %slice-start.1 = ((s8[8388608]{0:T(1024)(128)(4,1)}), s8[4194304]{0:T(1024)(128)(4,1)S(1)}, s32[]{:S(2)}) async-start(s8[8388608]{0:T(1024)(128)(4,1)} %bitcast.86), calls=%async_computation.5 | async-start | bytes 8388608
  124.1 19.2 %collective-permute-start.12 = (bf16[32,2048]{1,0:T(8,128)(2,1)}, bf16[32,2048]{1,0:T(8,128)(2,1)S(1)}, u32[]{:S(2)}, u32[]{:S(2)}) collective-permute-start(bf16[32,2048]{1,0:T(8,128)(2,1)} %get-tuple-element.72), channel_id=1, source_target_pairs={{0,0},{1,16},{2,32},{3,48},{4,4},{5,20},{6,36},{7,52},{8,8},{9,24}... | collective-permute-start | bytes 393224 | tf_op jit(solution)/shard_map/ppermute | solution.py:371
  129.1 16.8 %collective-permute-start.13 = (bf16[32,2048]{1,0:T(8,128)(2,1)}, bf16[32,2048]{1,0:T(8,128)(2,1)S(1)}, u32[]{:S(2)}, u32[]{:S(2)}) collective-permute-start(bf16[32,2048]{1,0:T(8,128)(2,1)} %get-tuple-element.73), channel_id=1, source_target_pairs={{0,4},{1,20},{2,36},{3,52},{4,0},{5,16},{6,32},{7,48},{8,12},{9,28... | collective-permute-start | bytes 393224 | tf_op jit(solution)/shard_map/ppermute | solution.py:371
  136.4 2.3 %copy-start.10 = (bf16[128,3,512]{2,0,1:T(8,128)(2,1)S(1)}, bf16[128,3,512]{2,0,1:T(8,128)(2,1)}, u32[]{:S(2)}) copy-start(bf16[128,3,512]{2,0,1:T(8,128)(2,1)} %param.29) | copy-start | bytes 1179652
  136.4 2.3 %copy-start.11 = (bf16[288,512]{1,0:T(8,128)(2,1)S(1)}, bf16[288,512]{1,0:T(8,128)(2,1)}, u32[]{:S(2)}) copy-start(bf16[288,512]{1,0:T(8,128)(2,1)} %refs_7_.1) | copy-start | bytes 884740
  136.4 2.3 %copy-start.13 = (f32[256,128]{1,0:T(8,128)S(1)}, f32[256,128]{1,0:T(8,128)}, u32[]{:S(2)}) copy-start(f32[256,128]{1,0:T(8,128)} %copy-done.12) | copy-start | bytes 393220
  136.5 2.3 %copy-start.14 = (f32[4,512]{1,0:T(4,128)S(1)}, f32[4,512]{1,0:T(4,128)}, u32[]{:S(2)}) copy-start(f32[4,512]{1,0:T(4,128)} %refs_5_.1) | copy-start | bytes 24580
  136.5 2.3 %copy-start.15 = (f32[512]{0:T(512)S(1)}, f32[512]{0:T(512)}, u32[]{:S(2)}) copy-start(f32[512]{0:T(512)} %param.32) | copy-start | bytes 6148
  138.7 2.8 %copy-start.8 = (bf16[512,512]{1,0:T(8,128)(2,1)}, bf16[512,512]{1,0:T(8,128)(2,1)S(1)}, u32[]{:S(2)}) copy-start(bf16[512,512]{1,0:T(8,128)(2,1)S(1)} %in_product.8) | copy-start | bytes 1572868
  141.6 28.3 %copy-start.23 = (f32[512]{0:T(512)S(1)}, f32[512]{0:T(512)}, u32[]{:S(2)}) copy-start(f32[512]{0:T(512)} %param.35) | copy-start | bytes 6148
  145.9 6.9 %collective-permute-start.14 = (bf16[128,288]{1,0:T(8,128)(2,1)S(1)}, bf16[128,288]{1,0:T(8,128)(2,1)S(1)}, u32[]{:S(2)}, u32[]{:S(2)}) collective-permute-start(bf16[128,288]{1,0:T(8,128)(2,1)S(1)} %get-tuple-element.121), channel_id=1, source_target_pairs={{0,3},{1,0},{2,1},{3,2},{4,7},{5,4},{6,5},{7,6},{8,11},{9,8},{10,9... | collective-permute-start | bytes 221192 | tf_op jit(solution)/shard_map/ppermute | solution.py:54
  146.0 6.9 %collective-permute-start.15 = (bf16[128,288]{1,0:T(8,128)(2,1)S(1)}, bf16[128,288]{1,0:T(8,128)(2,1)S(1)}, u32[]{:S(2)}, u32[]{:S(2)}) collective-permute-start(bf16[128,288]{1,0:T(8,128)(2,1)S(1)} %get-tuple-element.123), channel_id=1, source_target_pairs={{0,2},{1,3},{2,0},{3,1},{4,6},{5,7},{6,4},{7,5},{8,10},{9,11},{10,... | collective-permute-start | bytes 221192 | tf_op jit(solution)/shard_map/ppermute | solution.py:54
  146.1 7.7 %collective-permute-start.16 = (bf16[128,288]{1,0:T(8,128)(2,1)S(1)}, bf16[128,288]{1,0:T(8,128)(2,1)S(1)}, u32[]{:S(2)}, u32[]{:S(2)}) collective-permute-start(bf16[128,288]{1,0:T(8,128)(2,1)S(1)} %get-tuple-element.122), channel_id=1, source_target_pairs={{0,1},{1,2},{2,3},{3,0},{4,5},{5,6},{6,7},{7,4},{8,9},{9,10},{10,1... | collective-permute-start | bytes 221192 | tf_op jit(solution)/shard_map/ppermute | solution.py:54
  153.8 6.2 %collective-permute-start.17 = (bf16[128,288]{1,0:T(8,128)(2,1)S(1)}, bf16[128,288]{1,0:T(8,128)(2,1)S(1)}, u32[]{:S(2)}, u32[]{:S(2)}) collective-permute-start(bf16[128,288]{1,0:T(8,128)(2,1)S(1)} %fusion.40), channel_id=1, source_target_pairs={{0,4},{1,5},{2,6},{3,7},{4,0},{5,1},{6,2},{7,3},{8,12},{9,13},{10,... | collective-permute-start | bytes 221192 | tf_op jit(solution)/shard_map/ppermute | solution.py:58
  161.0 6.7 %collective-permute-start.18 = (bf16[128,288]{1,0:T(8,128)(2,1)S(1)}, bf16[128,288]{1,0:T(8,128)(2,1)S(1)}, u32[]{:S(2)}, u32[]{:S(2)}) collective-permute-start(bf16[128,288]{1,0:T(8,128)(2,1)S(1)} %add_convert_fusion.1), channel_id=1, source_target_pairs={{0,3},{1,0},{2,1},{3,2},{4,7},{5,4},{6,5},{7,6},{8,11},{9,8},{10,9... | collective-permute-start | bytes 221192 | tf_op jit(solution)/shard_map/ppermute | solution.py:54
  162.0 6.5 %collective-permute-start.19 = (bf16[128,288]{1,0:T(8,128)(2,1)S(1)}, bf16[128,288]{1,0:T(8,128)(2,1)S(1)}, u32[]{:S(2)}, u32[]{:S(2)}) collective-permute-start(bf16[128,288]{1,0:T(8,128)(2,1)S(1)} %add_convert_fusion.1), channel_id=1, source_target_pairs={{0,2},{1,3},{2,0},{3,1},{4,6},{5,7},{6,4},{7,5},{8,10},{9,11},{10,... | collective-permute-start | bytes 221192 | tf_op jit(solution)/shard_map/ppermute | solution.py:54
  164.8 4.6 %collective-permute-start.20 = (bf16[128,288]{1,0:T(8,128)(2,1)S(1)}, bf16[128,288]{1,0:T(8,128)(2,1)S(1)}, u32[]{:S(2)}, u32[]{:S(2)}) collective-permute-start(bf16[128,288]{1,0:T(8,128)(2,1)S(1)} %add_convert_fusion.1), channel_id=1, source_target_pairs={{0,1},{1,2},{2,3},{3,0},{4,5},{5,6},{6,7},{7,4},{8,9},{9,10},{10,1... | collective-permute-start | bytes 221192 | tf_op jit(solution)/shard_map/ppermute | solution.py:54
  165.0 22.4 %collective-permute-start.21 = (bf16[512,512]{1,0:T(8,128)(2,1)}, bf16[512,512]{1,0:T(8,128)(2,1)S(1)}, u32[]{:S(2)}, u32[]{:S(2)}) collective-permute-start(bf16[512,512]{1,0:T(8,128)(2,1)} %copy-done.8), channel_id=1, source_target_pairs={{0,4},{1,5},{2,6},{3,7},{4,0},{5,1},{6,2},{7,3},{8,12},{9,13},{10,... | collective-permute-start | bytes 1572872 | tf_op jit(solution)/shard_map/ppermute | solution.py:58
  169.7 2.2 copy-start.16
  171.9 15.7 %copy-start.22 = (f32[512]{0:T(512)S(1)}, f32[512]{0:T(512)}, u32[]{:S(2)}) copy-start(f32[512]{0:T(512)} %param.37) | copy-start | bytes 6148
  188.1 9.4 %collective-permute-start.22 = (bf16[256,512]{1,0:T(8,128)(2,1)S(1)}, bf16[256,512]{1,0:T(8,128)(2,1)S(1)}, u32[]{:S(2)}, u32[]{:S(2)}) collective-permute-start(bf16[256,512]{1,0:T(8,128)(2,1)S(1)} %pad_maximum_fusion.3.refs_0_), channel_id=1, source_target_pairs={{0,3},{1,0},{2,1},{3,2},{4,7},{5,4},{6,5},{7,6},{8,11},{9,8},{10,9... | collective-permute-start | bytes 786440 | tf_op jit(solution)/shard_map/ppermute | solution.py:54
  190.7 9.7 %collective-permute-start.23 = (bf16[256,512]{1,0:T(8,128)(2,1)S(1)}, bf16[256,512]{1,0:T(8,128)(2,1)S(1)}, u32[]{:S(2)}, u32[]{:S(2)}) collective-permute-start(bf16[256,512]{1,0:T(8,128)(2,1)S(1)} %pad_maximum_fusion.3.refs_0_), channel_id=1, source_target_pairs={{0,2},{1,3},{2,0},{3,1},{4,6},{5,7},{6,4},{7,5},{8,10},{9,11},{10,... | collective-permute-start | bytes 786440 | tf_op jit(solution)/shard_map/ppermute | solution.py:54
  191.6 8.8 %collective-permute-start.24 = (bf16[256,512]{1,0:T(8,128)(2,1)S(1)}, bf16[256,512]{1,0:T(8,128)(2,1)S(1)}, u32[]{:S(2)}, u32[]{:S(2)}) collective-permute-start(bf16[256,512]{1,0:T(8,128)(2,1)S(1)} %pad_maximum_fusion.3.refs_0_), channel_id=1, source_target_pairs={{0,1},{1,2},{2,3},{3,0},{4,5},{5,6},{6,7},{7,4},{8,9},{9,10},{10,1... | collective-permute-start | bytes 786440 | tf_op jit(solution)/shard_map/ppermute | solution.py:54
  194.1 14.3 %collective-permute-start.25 = (bf16[256,512]{1,0:T(8,128)(2,1)S(1)}, bf16[256,512]{1,0:T(8,128)(2,1)S(1)}, u32[]{:S(2)}, u32[]{:S(2)}) collective-permute-start(bf16[256,512]{1,0:T(8,128)(2,1)S(1)} %pad_maximum_fusion.4.refs_4_.refs_0_), channel_id=1, source_target_pairs={{0,3},{1,0},{2,1},{3,2},{4,7},{5,4},{6,5},{7,6},{8,11},{9,8},{10,9... | collective-permute-start | bytes 786440 | tf_op jit(solution)/shard_map/ppermute | solution.py:54
  194.2 14.2 %collective-permute-start.26 = (bf16[256,512]{1,0:T(8,128)(2,1)S(1)}, bf16[256,512]{1,0:T(8,128)(2,1)S(1)}, u32[]{:S(2)}, u32[]{:S(2)}) collective-permute-start(bf16[256,512]{1,0:T(8,128)(2,1)S(1)} %pad_maximum_fusion.4.refs_4_.refs_0_), channel_id=1, source_target_pairs={{0,2},{1,3},{2,0},{3,1},{4,6},{5,7},{6,4},{7,5},{8,10},{9,11},{10,... | collective-permute-start | bytes 786440 | tf_op jit(solution)/shard_map/ppermute | solution.py:54
  197.5 11.0 %collective-permute-start.27 = (bf16[256,512]{1,0:T(8,128)(2,1)S(1)}, bf16[256,512]{1,0:T(8,128)(2,1)S(1)}, u32[]{:S(2)}, u32[]{:S(2)}) collective-permute-start(bf16[256,512]{1,0:T(8,128)(2,1)S(1)} %pad_maximum_fusion.4.refs_4_.refs_0_), channel_id=1, source_target_pairs={{0,1},{1,2},{2,3},{3,0},{4,5},{5,6},{6,7},{7,4},{8,9},{9,10},{10,1... | collective-permute-start | bytes 786440 | tf_op jit(solution)/shard_map/ppermute | solution.py:54
  200.4 2.2 copy-start.3
  202.6 9.2 %copy-start.4 = (bf16[2048,1024]{1,0:T(8,128)(2,1)S(1)}, bf16[2048,1024]{1,0:T(8,128)(2,1)}, u32[]{:S(2)}) copy-start(bf16[2048,1024]{1,0:T(8,128)(2,1)} %all-gather.6.cloned.1.call-done) | copy-start | bytes 12582916
  204.5 11.2 %collective-permute-start.28 = (bf16[256,512]{1,0:T(8,128)(2,1)S(1)}, bf16[256,512]{1,0:T(8,128)(2,1)S(1)}, u32[]{:S(2)}, u32[]{:S(2)}) collective-permute-start(bf16[256,512]{1,0:T(8,128)(2,1)S(1)} %out_product.4), channel_id=1, source_target_pairs={{0,4},{1,5},{2,6},{3,7},{4,0},{5,1},{6,2},{7,3},{8,12},{9,13},{10,... | collective-permute-start | bytes 786440 | tf_op jit(solution)/shard_map/ppermute | solution.py:58
  210.4 9.5 %collective-permute-start.29 = (bf16[256,512]{1,0:T(8,128)(2,1)S(1)}, bf16[256,512]{1,0:T(8,128)(2,1)S(1)}, u32[]{:S(2)}, u32[]{:S(2)}) collective-permute-start(bf16[256,512]{1,0:T(8,128)(2,1)S(1)} %out_product.5), channel_id=1, source_target_pairs={{0,4},{1,5},{2,6},{3,7},{4,0},{5,1},{6,2},{7,3},{8,12},{9,13},{10,... | collective-permute-start | bytes 786440 | tf_op jit(solution)/shard_map/ppermute | solution.py:58
Sparse Core Ops, SparseCore 0:
  35.7 69.8 all-gather.3
  160.2 39.8 all-gather.5

commit v5 on v4

--- a/solution.py
+++ b/solution.py
@@ -61,6 +61,10 @@
 IN_VMEM = pl.BlockSpec(memory_space=pltpu.VMEM)
 IN_HBM = pl.BlockSpec(memory_space=pltpu.HBM)
 IN_SMEM = pl.BlockSpec(memory_space=pltpu.SMEM)
+
+
+def in_hbm(a):
+    return pltpu.with_memory_space_constraint(a, pltpu.HBM)
 
 
 def adam_update(master, moment, velocity, grad):
@@ -341,7 +345,7 @@
         rows_in = lax.dynamic_update_slice(
             rows_in, lax.ppermute(piece, BOTH, in_route(k)), (0, (x - k) % 4 * own, 0)
         )
-    weights_in = lax.all_gather(rows_in.reshape(8 * own, 1024), "fsdp", axis=0, tiled=False)
+    weights_in = in_hbm(lax.all_gather(rows_in.reshape(8 * own, 1024), "fsdp", axis=0, tiled=False))
 
     offset = jnp.clip(asked - lax.axis_index("fsdp") * vocab_rows, 0, vocab_rows - 1)
     looked = embed_table.at[offset.reshape(-1)].get(mode="promise_in_bounds")
@@ -350,9 +354,13 @@
     )
     half = count // PARTS
     answers = replies.reshape(replicas * capacity, feature_part)
-    found = [
-        answers.at[place[p * half : (p + 1) * half]].get(mode="promise_in_bounds") for p in range(PARTS)
-    ]
+    found = []
+    wanted = place
+    for p in range(PARTS):
+        rows_p, wanted = lax.optimization_barrier(
+            (answers.at[wanted[p * half : (p + 1) * half]].get(mode="promise_in_bounds"), wanted)
+        )
+        found.append(rows_p)
 
     def spread(parts):
         return [[part] + [from_x(part, k) for k in (1, 2, 3)] for part in parts]
@@ -388,7 +396,7 @@
         quarter = quarter + from_x(piece, k).astype(f32)
     quarter = (quarter + from_partner(quarter.astype(bf16)).astype(f32)).astype(bf16)
     z_away, quarter, rows_out = lax.optimization_barrier((z_away, quarter, rows_out))
-    weights_out = lax.all_gather(rows_out, "fsdp", axis=0, tiled=False)
+    weights_out = in_hbm(lax.all_gather(rows_out, "fsdp", axis=0, tiled=False))
     shared = jnp.stack([quarter] + [from_x(quarter, k) for k in (1, 2, 3)])
     dbc = jnp.concatenate(
         [lax.dynamic_index_in_dim(shared, (q - x) % 4, 0, keepdims=False) for q in range(4)], axis=0

time: 229 us -> 228 us (level)
  local copies, waits for them, and re-layouts: 31 us -> 21.6 us
  Pallas kernels: 24 us -> 30.3 us
  other arithmetic: 14.1 us -> 18.4 us
  waiting for transfers between devices: 75.3 us -> 71.7 us
    unnamed x53 -> x51, local copies, waits for them, and re-layouts: 18 us -> 9.48 us
    pallas_call x5, Pallas kernels: 11.7 us -> 15.9 us  [in_product(): pl.pallas_call(functools.partial(in_product_kernel, len(parts), matrix, s...]
    ppermute x18, waiting for transfers between devices: 17.2 us -> 20.5 us  [from_x(): lax.ppermute(a, 'chan', [(i, i // 4 * 4 + (i % 4 - k) % 4) for i in range...]
    ppermute x6, waiting for transfers between devices: 16.3 us -> 13.1 us  [from_partner(): return lax.ppermute(a, 'chan', [(i, i ^ 4) for i in range(8)])]
    all_gather x1, waiting for transfers between devices: 3.41 us -> 0.71 us  [per_device(): lax.all_gather(rows_in.reshape(8 * own, 1024), 'fsdp', axis=0, tiled=False)]
  transfers between devices with their start and end apart: 34 -> 34, of which waited for: 19 -> 19; matrix products, arithmetic and copies ran while one was open for 12% -> 12% of each run, Pallas kernels for 11% -> 13%
where the time goes in v5:
time: 228 us; the launch traced here: 225 us
  waiting for transfers between devices  71.7 us (31%)
  starting transfers between devices  68.2 us (30%)
  Pallas kernels  30.3 us (13%)
  local copies, waits for them, and re-layouts  21.6 us (9%)
  other arithmetic  18.4 us (8%)
  between operations  14.7 us (6%)
    all_to_all x1, waiting for transfers between devices, per_device(): lax.all_to_all(looked.reshape(replicas, capacity, feature_part), 'fsdp',...  28 us
    ppermute x18, starting transfers between devices, from_x(): lax.ppermute(a, 'chan', [(i, i // 4 * 4 + (i % 4 - k) % 4) for i in range...  22.5 us
    ppermute x18, waiting for transfers between devices, from_x(): lax.ppermute(a, 'chan', [(i, i // 4 * 4 + (i % 4 - k) % 4) for i in range...  20.5 us
    ppermute x6, starting transfers between devices, from_partner(): return lax.ppermute(a, 'chan', [(i, i ^ 4) for i in range(8)])  16.5 us
    pallas_call x5, Pallas kernels, in_product(): pl.pallas_call(functools.partial(in_product_kernel, len(parts), matrix, s...  15.9 us
    ppermute x6, waiting for transfers between devices, from_partner(): return lax.ppermute(a, 'chan', [(i, i ^ 4) for i in range(8)])  13.1 us
    all_to_all x1, starting transfers between devices, per_device(): lax.all_to_all(looked.reshape(replicas, capacity, feature_part), 'fsdp',...  10.8 us
    unnamed x51, local copies, waits for them, and re-layouts  9.48 us
  transfers between devices with their start and end apart: 34, of which 19 were waited for; matrix products, arithmetic and copies ran while one was open for 12% of the time, Pallas kernels for 13%

profile of v5, /device:TPU:6, one launch (start us, length us, event | category | flops | bytes accessed | tf_op | source)
XLA Modules:
  0.0 225.5 jit_solution(2497489921555579818)
XLA Ops:
  7.2 0.7 add_select_fusion
  9.1 6.4 %all-to-all-start = ((s32[16,1,64]{2,1,0:T(1,128)}), s32[16,1,64]{2,1,0:T(1,128)S(1)}, u32[]{:S(2)}, u32[]{:S(2)}) async-start(s32[16,1,64]{2,1,0:T(1,128)} %all_to_all.11), calls=%async_computation | async-start | bytes 16384 | tf_op jit(solution)/shard_map/all_to_all | solution.py:336
  15.6 1.2 copy-done.1
  16.8 1.2 copy-done.2
  18.0 1.2 copy-done.3
  19.3 1.0 copy-done.6
  20.3 3.3 %adam_in.1 = (f32[2048,128]{1,0:T(8,128)}, bf16[2,32,1024]{2,1,0:T(8,128)(2,1)S(1)}, bf16[2,32,1024]{2,1,0:T(8,128)(2,1)S(1)}, bf16[2,32,1024]{2,1,0:T(8,128)(2,1)S(1)}, bf16[2,32,1024]{2,1,0:T(8,128)(2,1)S(1)}) custom-call(s32[1]{0:T(128)} %bitcast.s_ref, f32[2048,128]{1,0:T(8,128)S(1)} %bitcast.86, f32[2048,128]{1,0:T(8,128)S(1)} %bitcast.87, ...), custom_call_target="tpu_custom_call" | custom-call | flops 5242880 | bytes 5242880 | tf_op jit(solution)/shard_map/adam_in/pallas_call | solution.py:102
  24.8 2.4 %collective-permute-start.8 = (bf16[2,32,1024]{2,1,0:T(8,128)(2,1)S(1)}, bf16[2,32,1024]{2,1,0:T(8,128)(2,1)S(1)}, u32[]{:S(2)}, u32[]{:S(2)}) collective-permute-start(bf16[2,32,1024]{2,1,0:T(8,128)(2,1)S(1)} %get-tuple-element.61), channel_id=1, source_target_pairs={{0,2},{1,3},{2,0},{3,1},{4,66},{5,67},{6,64},{7,65},{8,10},{9,11},... | collective-permute-start | bytes 393224 | tf_op jit(solution)/shard_map/ppermute | solution.py:346
  27.3 3.3 %collective-permute-done.7 = bf16[2,32,1024]{2,1,0:T(8,128)(2,1)S(1)} collective-permute-done((bf16[2,32,1024]{2,1,0:T(8,128)(2,1)S(1)}, bf16[2,32,1024]{2,1,0:T(8,128)(2,1)S(1)}, u32[]{:S(2)}, u32[]{:S(2)}) %collective-permute-start.7) | collective-permute-done | bytes 131104 | tf_op jit(solution)/shard_map/ppermute | solution.py:346
  30.7 2.0 collective-permute-done.8
  32.7 2.0 collective-permute-done.9
  34.7 0.8 copy-done.16
  35.7 7.8 %gather_fusion = bf16[1024,512]{1,0:T(8,128)(2,1)} fusion(bf16[4096,512]{1,0:T(8,128)(2,1)} %param.27, s32[1024]{0:T(1024)S(1)} %broadcast_clamp_fusion), kind=kCustom, calls=%fused_computation | custom fusion | bytes 2101248 | tf_op jit(solution)/shard_map/gather | solution.py:351
  43.5 10.8 %all-to-all-start.1 = ((bf16[16,64,512]{2,1,0:T(8,128)(2,1)}), bf16[16,64,512]{2,1,0:T(8,128)(2,1)S(1)}, u32[]{:S(2)}, u32[]{:S(2)}) async-start(bf16[16,64,512]{2,1,0:T(8,128)(2,1)} %bitcast.19), calls=%async_computation.1 | async-start | bytes 2097152 | tf_op jit(solution)/shard_map/all_to_all | solution.py:352
  54.4 28.0 %all-to-all-done.1 = bf16[16,64,512]{2,1,0:T(8,128)(2,1)S(1)} async-done(((bf16[16,64,512]{2,1,0:T(8,128)(2,1)}), bf16[16,64,512]{2,1,0:T(8,128)(2,1)S(1)}, u32[]{:S(2)}, u32[]{:S(2)}) %all-to-all-start.1) | async-done | bytes 1048608 | tf_op jit(solution)/shard_map/all_to_all | solution.py:352
  82.4 1.2 gather_fusion.1
  83.5 1.2 gather_fusion.2
  84.7 0.9 collective-permute-start.3
  85.6 2.3 %fusion.45 = (bf16[32,4096]{1,0:T(8,128)(2,1)S(1)}, f32[32,4096]{1,0:T(8,128)}) fusion(f32[32,4096]{1,0:T(8,128)S(1)} %copy-done.17, f32[32,4096]{1,0:T(8,128)S(1)} %copy-done.18, bf16[32,4096]{1,0:T(8,128)(2,1)S(1)} %copy-done.22, f32[32,4096]{1,0:T(8,128)} %param.24), kind=kLoop, calls=%fused_computation.128 | loop fusion | flops 2228224 | bytes 2621440 | tf_op jit(solution)/shard_map/convert_element_type | solution.py:375
  88.6 1.8 collective-permute-start.4
  90.4 1.5 collective-permute-start.5
  92.4 1.8 collective-permute-start.1
  94.2 5.7 %collective-permute-done.3.refs_5_.refs_1_ = bf16[256,512]{1,0:T(8,128)(2,1)S(1)} collective-permute-done((bf16[256,512]{1,0:T(8,128)(2,1)S(1)}, bf16[256,512]{1,0:T(8,128)(2,1)S(1)}, u32[]{:S(2)}, u32[]{:S(2)}) %collective-permute-start.3) | collective-permute-done | bytes 262176 | tf_op jit(solution)/shard_map/ppermute | solution.py:54
  99.9 0.9 copy_bitcast_fusion
  100.8 4.0 %collective-permute-done.5.refs_7_.refs_3_ = bf16[256,512]{1,0:T(8,128)(2,1)S(1)} collective-permute-done((bf16[256,512]{1,0:T(8,128)(2,1)S(1)}, bf16[256,512]{1,0:T(8,128)(2,1)S(1)}, u32[]{:S(2)}, u32[]{:S(2)}) %collective-permute-start.5) | collective-permute-done | bytes 262176 | tf_op jit(solution)/shard_map/ppermute | solution.py:54
  105.5 3.3 %in_product.7 = (bf16[256,640]{1,0:T(8,128)(2,1)}, f32[256,128]{1,0:T(8,128)S(1)}) custom-call(s32[2]{0:T(128)S(1)} %pad_add_fusion.1.s_ref, bf16[256,512]{1,0:T(8,128)(2,1)S(1)} %gather_fusion.2, bf16[256,512]{1,0:T(8,128)(2,1)S(1)} %collective-permute-done.3.refs_5_.refs_1_, bf16[256,512]{1,0:T(8,128)(2,1)S(1)} %collective-permute-done.4.refs_6_.refs_2_, ...), custom_call_target="tpu_custom_call" | custom-call | flops 536870912 | bytes 6291456 | tf_op jit(solution)/shard_map/in_product/pallas_call | solution.py:221
  109.5 3.0 %collective-permute-start.11 = (bf16[256,640]{1,0:T(8,128)(2,1)}, bf16[256,640]{1,0:T(8,128)(2,1)}, u32[]{:S(2)}, u32[]{:S(2)}) collective-permute-start(bf16[256,640]{1,0:T(8,128)(2,1)} %get-tuple-element.66), channel_id=1, source_target_pairs={{0,4},{1,5},{2,6},{3,7},{4,0},{5,1},{6,2},{7,3},{8,12},{9,13},{10,... | collective-permute-start | bytes 983048 | tf_op jit(solution)/shard_map/ppermute | solution.py:58
  112.5 1.8 collective-permute-done.2.refs_3_
  114.4 3.3 %in_product.6 = (bf16[256,640]{1,0:T(8,128)(2,1)}, f32[256,128]{1,0:T(8,128)S(1)}) custom-call(s32[2]{0:T(128)S(1)} %pad_add_fusion.1.s_ref, bf16[256,512]{1,0:T(8,128)(2,1)S(1)} %gather_fusion.1, bf16[256,512]{1,0:T(8,128)(2,1)S(1)} %collective-permute-done.refs_1_, bf16[256,512]{1,0:T(8,128)(2,1)S(1)} %collective-permute-done.1.refs_2_, ...), custom_call_target="tpu_custom_call" | custom-call | flops 536870912 | bytes 6291456 | tf_op jit(solution)/shard_map/in_product/pallas_call | solution.py:221
  118.4 2.0 collective-permute-start.10
  120.5 3.1 %in_product.5.here = f32[512,512]{1,0:T(8,128)S(1)} custom-call(s32[2]{0:T(128)S(1)} %pad_add_fusion.s_ref, bf16[256,512]{1,0:T(8,128)(2,1)S(1)} %gather_fusion.1, bf16[256,512]{1,0:T(8,128)(2,1)S(1)} %collective-permute-done.refs_1_, bf16[256,512]{1,0:T(8,128)(2,1)S(1)} %collective-permute-done.1.refs_2_, ...), custom_call_target="tpu_custom_call" | custom-call | flops 1073741824 | bytes 6291456 | tf_op jit(solution)/shard_map/in_product/pallas_call | solution.py:221
  123.5 4.2 %collective-permute-start.12 = (bf16[32,2048]{1,0:T(8,128)(2,1)}, bf16[32,2048]{1,0:T(8,128)(2,1)S(1)}, u32[]{:S(2)}, u32[]{:S(2)}) collective-permute-start(bf16[32,2048]{1,0:T(8,128)(2,1)} %get-tuple-element.78), channel_id=1, source_target_pairs={{0,0},{1,16},{2,32},{3,48},{4,4},{5,20},{6,36},{7,52},{8,8},{9,24}... | collective-permute-start | bytes 393224 | tf_op jit(solution)/shard_map/ppermute | solution.py:379
  127.8 4.0 %collective-permute-start.13 = (bf16[32,2048]{1,0:T(8,128)(2,1)}, bf16[32,2048]{1,0:T(8,128)(2,1)S(1)}, u32[]{:S(2)}, u32[]{:S(2)}) collective-permute-start(bf16[32,2048]{1,0:T(8,128)(2,1)} %get-tuple-element.79), channel_id=1, source_target_pairs={{0,4},{1,20},{2,36},{3,52},{4,0},{5,16},{6,32},{7,48},{8,12},{9,28... | collective-permute-start | bytes 393224 | tf_op jit(solution)/shard_map/ppermute | solution.py:379
  131.8 3.1 %in_product.9 = f32[512,512]{1,0:T(8,128)S(1)} custom-call(s32[2]{0:T(128)S(1)} %pad_add_fusion.s_ref, bf16[256,512]{1,0:T(8,128)(2,1)S(1)} %gather_fusion.1, bf16[256,512]{1,0:T(8,128)(2,1)S(1)} %collective-permute-done.refs_1_, bf16[256,512]{1,0:T(8,128)(2,1)S(1)} %collective-permute-done.1.refs_2_, bf16[256,512]{1,0:T(8,128)(2,1)S(1)} %collective-permute-done.2.refs_3_, ...), custom_call_target="tpu_custom_call" | custom-call | flops 1073741824 | bytes 6291456 | tf_op jit(solution)/shard_map/in_product/pallas_call | solution.py:221
  134.9 3.1 %in_product.8 = bf16[512,512]{1,0:T(8,128)(2,1)S(1)} custom-call(s32[2]{0:T(128)S(1)} %pad_add_fusion.1.s_ref, bf16[256,512]{1,0:T(8,128)(2,1)S(1)} %gather_fusion.1, bf16[256,512]{1,0:T(8,128)(2,1)S(1)} %collective-permute-done.refs_1_, bf16[256,512]{1,0:T(8,128)(2,1)S(1)} %collective-permute-done.1.refs_2_, ...), custom_call_target="tpu_custom_call" | custom-call | flops 1073741824 | bytes 6291456 | tf_op jit(solution)/shard_map/in_product/pallas_call | solution.py:221
  138.0 0.8 copy-done.4
  138.9 2.7 %conv.1 = (bf16[512,512]{1,0:T(8,128)(2,1)S(1)}, bf16[3,128,512]{2,1,0:T(8,128)(2,1)}, bf16[512,288]{1,0:T(8,128)(2,1)S(1)}, f32[512,128]{1,0:T(8,128)S(1)}) custom-call(f32[512,512]{1,0:T(8,128)S(1)} %in_product.5.here, bf16[256,640]{1,0:T(8,128)(2,1)} %collective-permute-done.10.refs_0_, bf16[256,640]{1,0:T(8,128)(2,1)} %collective-permute-done.11.refs_1_, ...), custom_call_target="tpu_custom_call" | custom-call | flops 150994944 | bytes 4194304 | tf_op jit(solution)/shard_map/conv/pallas_call | solution.py:148
  141.6 0.8 collective-permute-done.13
  143.0 2.2 collective-permute-start.15
  145.8 4.2 %collective-permute-done.14 = bf16[128,288]{1,0:T(8,128)(2,1)S(1)} collective-permute-done((bf16[128,288]{1,0:T(8,128)(2,1)S(1)}, bf16[128,288]{1,0:T(8,128)(2,1)S(1)}, u32[]{:S(2)}, u32[]{:S(2)}) %collective-permute-start.14) | collective-permute-done | bytes 73760 | tf_op jit(solution)/shard_map/ppermute | solution.py:54
  151.3 2.6 %collective-permute-start.17 = (bf16[128,288]{1,0:T(8,128)(2,1)}, bf16[128,288]{1,0:T(8,128)(2,1)}, u32[]{:S(2)}, u32[]{:S(2)}) collective-permute-start(bf16[128,288]{1,0:T(8,128)(2,1)} %fusion.40), channel_id=1, source_target_pairs={{0,4},{1,5},{2,6},{3,7},{4,0},{5,1},{6,2},{7,3},{8,12},{9,13},{10,... | collective-permute-start | bytes 221192 | tf_op jit(solution)/shard_map/ppermute | solution.py:58
  154.6 3.1 %collective-permute-done.17 = bf16[128,288]{1,0:T(8,128)(2,1)} collective-permute-done((bf16[128,288]{1,0:T(8,128)(2,1)}, bf16[128,288]{1,0:T(8,128)(2,1)}, u32[]{:S(2)}, u32[]{:S(2)}) %collective-permute-start.17) | collective-permute-done | bytes 73760 | tf_op jit(solution)/shard_map/ppermute | solution.py:58
  157.7 1.7 add_convert_fusion.1
  159.6 0.8 exponential_negate_fusion
  161.1 3.2 %collective-permute-start.19 = (bf16[128,288]{1,0:T(8,128)(2,1)}, bf16[128,288]{1,0:T(8,128)(2,1)S(1)}, u32[]{:S(2)}, u32[]{:S(2)}) collective-permute-start(bf16[128,288]{1,0:T(8,128)(2,1)} %add_convert_fusion.1), channel_id=1, source_target_pairs={{0,2},{1,3},{2,0},{3,1},{4,6},{5,7},{6,4},{7,5},{8,10},{9,11},{10,... | collective-permute-start | bytes 221192 | tf_op jit(solution)/shard_map/ppermute | solution.py:54
  164.4 3.0 %collective-permute-start.21 = (bf16[512,512]{1,0:T(8,128)(2,1)S(1)}, bf16[512,512]{1,0:T(8,128)(2,1)S(1)}, u32[]{:S(2)}, u32[]{:S(2)}) collective-permute-start(bf16[512,512]{1,0:T(8,128)(2,1)S(1)} %copy-done.5), channel_id=1, source_target_pairs={{0,4},{1,5},{2,6},{3,7},{4,0},{5,1},{6,2},{7,3},{8,12},{9,13},{10,... | collective-permute-start | bytes 1572872 | tf_op jit(solution)/shard_map/ppermute | solution.py:58
  168.1 1.0 collective-permute-done.20
  169.1 1.0 pad_maximum_fusion
  170.4 0.8 compare_select_fusion
  171.5 1.0 copy-done.15
  172.4 7.7 %multiply_reduce_fusion = (f32[128,512]{1,0:T(8,128)S(1)}, f32[128,16,512]{2,1,0:T(8,128)}, f32[128,512]{1,0:T(8,128)S(1)}, f32[128,512]{1,0:T(8,128)S(1)}, f32[128,512]{1,0:T(8,128)S(1)}) fusion(f32[128,16]{1,0:T(8,128)S(1)} %get-tuple-element.114, f32[128,16]{1,0:T(8,128)S(1)} %get-tuple-element.113, f32[128,512]{1,0:T(8,128)S(1)} %get-tuple-element.101, ...), kind=kLoop, calls=%fused_computation.3 | loop fusion | flops 24903680 | bytes 11632640 | tf_op jit(solution)/shard_map/reduce_sum | solution.py:426
  180.1 6.0 %collective-permute-done.21 = bf16[512,512]{1,0:T(8,128)(2,1)S(1)} collective-permute-done((bf16[512,512]{1,0:T(8,128)(2,1)S(1)}, bf16[512,512]{1,0:T(8,128)(2,1)S(1)}, u32[]{:S(2)}, u32[]{:S(2)}) %collective-permute-start.21) | collective-permute-done | bytes 524320 | tf_op jit(solution)/shard_map/ppermute | solution.py:58
  186.8 2.9 %collective-permute-start.22 = (bf16[256,512]{1,0:T(8,128)(2,1)S(1)}, bf16[256,512]{1,0:T(8,128)(2,1)S(1)}, u32[]{:S(2)}, u32[]{:S(2)}) collective-permute-start(bf16[256,512]{1,0:T(8,128)(2,1)S(1)} %pad_maximum_fusion.3.refs_0_), channel_id=1, source_target_pairs={{0,3},{1,0},{2,1},{3,2},{4,7},{5,4},{6,5},{7,6},{8,11},{9,8},{10,9... | collective-permute-start | bytes 786440 | tf_op jit(solution)/shard_map/ppermute | solution.py:54
  189.8 2.6 %collective-permute-start.24 = (bf16[256,512]{1,0:T(8,128)(2,1)S(1)}, bf16[256,512]{1,0:T(8,128)(2,1)S(1)}, u32[]{:S(2)}, u32[]{:S(2)}) collective-permute-start(bf16[256,512]{1,0:T(8,128)(2,1)S(1)} %pad_maximum_fusion.3.refs_0_), channel_id=1, source_target_pairs={{0,1},{1,2},{2,3},{3,0},{4,5},{5,6},{6,7},{7,4},{8,9},{9,10},{10,1... | collective-permute-start | bytes 786440 | tf_op jit(solution)/shard_map/ppermute | solution.py:54
  192.8 2.8 %collective-permute-start.26 = (bf16[256,512]{1,0:T(8,128)(2,1)S(1)}, bf16[256,512]{1,0:T(8,128)(2,1)S(1)}, u32[]{:S(2)}, u32[]{:S(2)}) collective-permute-start(bf16[256,512]{1,0:T(8,128)(2,1)S(1)} %pad_maximum_fusion.4.refs_4_.refs_0_), channel_id=1, source_target_pairs={{0,2},{1,3},{2,0},{3,1},{4,6},{5,7},{6,4},{7,5},{8,10},{9,11},{10,... | collective-permute-start | bytes 786440 | tf_op jit(solution)/shard_map/ppermute | solution.py:54
  195.6 2.1 collective-permute-done.22.refs_1_
  198.1 1.2 all-gather.6.cloned.1.call-done
  199.3 2.6 %out_product.4 = bf16[256,512]{1,0:T(8,128)(2,1)S(1)} custom-call(s32[2]{0:T(128)S(1)} %pad_add_fusion.1.s_ref, bf16[256,512]{1,0:T(8,128)(2,1)S(1)} %pad_maximum_fusion.3.refs_0_, bf16[256,512]{1,0:T(8,128)(2,1)S(1)} %collective-permute-done.22.refs_1_, bf16[256,512]{1,0:T(8,128)(2,1)S(1)} %collective-permute-done.23.refs_2_, ...), custom_call_target="tpu_custom_call" | custom-call | flops 536870912 | bytes 6291456 | tf_op jit(solution)/shard_map/out_product/pallas_call | solution.py:277
  202.0 2.9 %collective-permute-start.28 = (bf16[256,512]{1,0:T(8,128)(2,1)S(1)}, bf16[256,512]{1,0:T(8,128)(2,1)S(1)}, u32[]{:S(2)}, u32[]{:S(2)}) collective-permute-start(bf16[256,512]{1,0:T(8,128)(2,1)S(1)} %out_product.4), channel_id=1, source_target_pairs={{0,4},{1,5},{2,6},{3,7},{4,0},{5,1},{6,2},{7,3},{8,12},{9,13},{10,... | collective-permute-start | bytes 786440 | tf_op jit(solution)/shard_map/ppermute | solution.py:58
  204.9 2.6 %out_product.5 = bf16[256,512]{1,0:T(8,128)(2,1)S(1)} custom-call(s32[2]{0:T(128)S(1)} %pad_add_fusion.1.s_ref, bf16[256,512]{1,0:T(8,128)(2,1)S(1)} %pad_maximum_fusion.4.refs_4_.refs_0_, bf16[256,512]{1,0:T(8,128)(2,1)S(1)} %collective-permute-done.25.refs_5_.refs_1_, bf16[256,512]{1,0:T(8,128)(2,1)S(1)} %collective-permute-done.26.refs_6_.refs_2_, ...), custom_call_target="tpu_custom_call" | custom-call | flops 536870912 | bytes 6291456 | tf_op jit(solution)/shard_map/out_product/pallas_call | solution.py:277
  207.5 3.0 %collective-permute-start.29 = (bf16[256,512]{1,0:T(8,128)(2,1)S(1)}, bf16[256,512]{1,0:T(8,128)(2,1)S(1)}, u32[]{:S(2)}, u32[]{:S(2)}) collective-permute-start(bf16[256,512]{1,0:T(8,128)(2,1)S(1)} %out_product.5), channel_id=1, source_target_pairs={{0,4},{1,5},{2,6},{3,7},{4,0},{5,1},{6,2},{7,3},{8,12},{9,13},{10,... | collective-permute-start | bytes 786440 | tf_op jit(solution)/shard_map/ppermute | solution.py:58
  210.5 3.2 %out_product.3 = f32[512,512]{1,0:T(8,128)S(1)} custom-call(s32[2]{0:T(128)S(1)} %pad_add_fusion.s_ref, bf16[256,512]{1,0:T(8,128)(2,1)S(1)} %pad_maximum_fusion.3.refs_0_, bf16[256,512]{1,0:T(8,128)(2,1)S(1)} %collective-permute-done.22.refs_1_, bf16[256,512]{1,0:T(8,128)(2,1)S(1)} %collective-permute-done.23.refs_2_, ...), custom_call_target="tpu_custom_call" | custom-call | flops 1073741824 | bytes 6291456 | tf_op jit(solution)/shard_map/out_product/pallas_call | solution.py:277
  213.7 4.0 %collective-permute-done.29 = bf16[256,512]{1,0:T(8,128)(2,1)S(1)} collective-permute-done((bf16[256,512]{1,0:T(8,128)(2,1)S(1)}, bf16[256,512]{1,0:T(8,128)(2,1)S(1)}, u32[]{:S(2)}, u32[]{:S(2)}) %collective-permute-start.29) | collective-permute-done | bytes 262176 | tf_op jit(solution)/shard_map/ppermute | solution.py:58
  217.6 1.0 add_convert_fusion
  (114 shorter events, 13.1 us)
Async XLA Ops:
  7.2 163.2 %copy-start = (bf16[512,256]{1,0:T(8,128)(2,1)S(1)}, bf16[512,256]{1,0:T(8,128)(2,1)}, u32[]{:S(2)}) copy-start(bf16[512,256]{1,0:T(8,128)(2,1)} %param.34) | copy-start | bytes 786436
  9.1 14.5 %all-to-all-start = ((s32[16,1,64]{2,1,0:T(1,128)}), s32[16,1,64]{2,1,0:T(1,128)S(1)}, u32[]{:S(2)}, u32[]{:S(2)}) async-start(s32[16,1,64]{2,1,0:T(1,128)} %all_to_all.11), calls=%async_computation | async-start | bytes 16384 | tf_op jit(solution)/shard_map/all_to_all | solution.py:336
  15.5 90.0 %all-gather.4.cloned.1.call-start = ((), (), s32[]{:S(2)}) async-start(), calls=%async_computation.2 | async-start | bytes 8912896 | tf_op jit(solution)/shard_map/all_gather | solution.py:348
  15.6 1.2 copy-start.1
  16.8 1.2 copy-start.2
  18.0 1.2 copy-start.3
  19.3 1.0 copy-start.6
  23.6 3.6 %collective-permute-start.6 = (bf16[2,32,1024]{2,1,0:T(8,128)(2,1)S(1)}, bf16[2,32,1024]{2,1,0:T(8,128)(2,1)S(1)}, u32[]{:S(2)}, u32[]{:S(2)}) collective-permute-start(bf16[2,32,1024]{2,1,0:T(8,128)(2,1)S(1)} %get-tuple-element.59), channel_id=1, source_target_pairs={{0,0},{1,1},{2,2},{3,3},{4,64},{5,65},{6,66},{7,67},{8,8},{9,9},{1... | collective-permute-start | bytes 393224 | tf_op jit(solution)/shard_map/ppermute | solution.py:346
  24.3 6.4 %collective-permute-start.7 = (bf16[2,32,1024]{2,1,0:T(8,128)(2,1)S(1)}, bf16[2,32,1024]{2,1,0:T(8,128)(2,1)S(1)}, u32[]{:S(2)}, u32[]{:S(2)}) collective-permute-start(bf16[2,32,1024]{2,1,0:T(8,128)(2,1)S(1)} %get-tuple-element.60), channel_id=1, source_target_pairs={{0,1},{1,2},{2,3},{3,0},{4,65},{5,66},{6,67},{7,64},{8,9},{9,10},{... | collective-permute-start | bytes 393224 | tf_op jit(solution)/shard_map/ppermute | solution.py:346
  24.8 7.8 %collective-permute-start.8 = (bf16[2,32,1024]{2,1,0:T(8,128)(2,1)S(1)}, bf16[2,32,1024]{2,1,0:T(8,128)(2,1)S(1)}, u32[]{:S(2)}, u32[]{:S(2)}) collective-permute-start(bf16[2,32,1024]{2,1,0:T(8,128)(2,1)S(1)} %get-tuple-element.61), channel_id=1, source_target_pairs={{0,2},{1,3},{2,0},{3,1},{4,66},{5,67},{6,64},{7,65},{8,10},{9,11},... | collective-permute-start | bytes 393224 | tf_op jit(solution)/shard_map/ppermute | solution.py:346
  27.3 7.4 %collective-permute-start.9 = (bf16[2,32,1024]{2,1,0:T(8,128)(2,1)S(1)}, bf16[2,32,1024]{2,1,0:T(8,128)(2,1)S(1)}, u32[]{:S(2)}, u32[]{:S(2)}) collective-permute-start(bf16[2,32,1024]{2,1,0:T(8,128)(2,1)S(1)} %get-tuple-element.62), channel_id=1, source_target_pairs={{0,3},{1,0},{2,1},{3,2},{4,67},{5,64},{6,65},{7,66},{8,11},{9,8},{... | collective-permute-start | bytes 393224 | tf_op jit(solution)/shard_map/ppermute | solution.py:346
  34.7 0.8 copy-start.16
  43.5 42.1 %copy-start.17 = (f32[32,4096]{1,0:T(8,128)S(1)}, f32[32,4096]{1,0:T(8,128)}, u32[]{:S(2)}) copy-start(f32[32,4096]{1,0:T(8,128)} %param.23) | copy-start | bytes 1572868
  43.5 42.1 %copy-start.18 = (f32[32,4096]{1,0:T(8,128)S(1)}, f32[32,4096]{1,0:T(8,128)}, u32[]{:S(2)}) copy-start(f32[32,4096]{1,0:T(8,128)} %param.25) | copy-start | bytes 1572868
  43.5 42.1 %copy-start.22 = (bf16[32,4096]{1,0:T(8,128)(2,1)S(1)}, bf16[32,4096]{1,0:T(8,128)(2,1)}, u32[]{:S(2)}) copy-start(bf16[32,4096]{1,0:T(8,128)(2,1)} %param.26) | copy-start | bytes 786436
  43.5 38.8 %all-to-all-start.1 = ((bf16[16,64,512]{2,1,0:T(8,128)(2,1)}), bf16[16,64,512]{2,1,0:T(8,128)(2,1)S(1)}, u32[]{:S(2)}, u32[]{:S(2)}) async-start(bf16[16,64,512]{2,1,0:T(8,128)(2,1)} %bitcast.19), calls=%async_computation.1 | async-start | bytes 2097152 | tf_op jit(solution)/shard_map/all_to_all | solution.py:352
  54.3 145.0 %all-gather.6.cloned.1.call-start = ((), (), s32[]{:S(2)}) async-start(), calls=%async_computation.3 | async-start | bytes 4456448 | tf_op jit(solution)/shard_map/all_gather | solution.py:399
  84.7 15.2 %collective-permute-start.3 = (bf16[256,512]{1,0:T(8,128)(2,1)S(1)}, bf16[256,512]{1,0:T(8,128)(2,1)S(1)}, u32[]{:S(2)}, u32[]{:S(2)}) collective-permute-start(bf16[256,512]{1,0:T(8,128)(2,1)S(1)} %gather_fusion.2), channel_id=1, source_target_pairs={{0,3},{1,0},{2,1},{3,2},{4,7},{5,4},{6,5},{7,6},{8,11},{9,8},{10,9... | collective-permute-start | bytes 786440 | tf_op jit(solution)/shard_map/ppermute | solution.py:54
  88.6 12.2 %collective-permute-start.4 = (bf16[256,512]{1,0:T(8,128)(2,1)S(1)}, bf16[256,512]{1,0:T(8,128)(2,1)S(1)}, u32[]{:S(2)}, u32[]{:S(2)}) collective-permute-start(bf16[256,512]{1,0:T(8,128)(2,1)S(1)} %gather_fusion.2), channel_id=1, source_target_pairs={{0,2},{1,3},{2,0},{3,1},{4,6},{5,7},{6,4},{7,5},{8,10},{9,11},{10,... | collective-permute-start | bytes 786440 | tf_op jit(solution)/shard_map/ppermute | solution.py:54
  90.4 14.4 %collective-permute-start.5 = (bf16[256,512]{1,0:T(8,128)(2,1)S(1)}, bf16[256,512]{1,0:T(8,128)(2,1)S(1)}, u32[]{:S(2)}, u32[]{:S(2)}) collective-permute-start(bf16[256,512]{1,0:T(8,128)(2,1)S(1)} %gather_fusion.2), channel_id=1, source_target_pairs={{0,1},{1,2},{2,3},{3,0},{4,5},{5,6},{6,7},{7,4},{8,9},{9,10},{10,1... | collective-permute-start | bytes 786440 | tf_op jit(solution)/shard_map/ppermute | solution.py:54
  91.9 20.6 %collective-permute-start = (bf16[256,512]{1,0:T(8,128)(2,1)S(1)}, bf16[256,512]{1,0:T(8,128)(2,1)S(1)}, u32[]{:S(2)}, u32[]{:S(2)}) collective-permute-start(bf16[256,512]{1,0:T(8,128)(2,1)S(1)} %gather_fusion.1), channel_id=1, source_target_pairs={{0,3},{1,0},{2,1},{3,2},{4,7},{5,4},{6,5},{7,6},{8,11},{9,8},{10,9... | collective-permute-start | bytes 786440 | tf_op jit(solution)/shard_map/ppermute | solution.py:54
  92.4 20.1 %collective-permute-start.1 = (bf16[256,512]{1,0:T(8,128)(2,1)S(1)}, bf16[256,512]{1,0:T(8,128)(2,1)S(1)}, u32[]{:S(2)}, u32[]{:S(2)}) collective-permute-start(bf16[256,512]{1,0:T(8,128)(2,1)S(1)} %gather_fusion.1), channel_id=1, source_target_pairs={{0,2},{1,3},{2,0},{3,1},{4,6},{5,7},{6,4},{7,5},{8,10},{9,11},{10,... | collective-permute-start | bytes 786440 | tf_op jit(solution)/shard_map/ppermute | solution.py:54
  99.9 14.5 %collective-permute-start.2 = (bf16[256,512]{1,0:T(8,128)(2,1)S(1)}, bf16[256,512]{1,0:T(8,128)(2,1)S(1)}, u32[]{:S(2)}, u32[]{:S(2)}) collective-permute-start(bf16[256,512]{1,0:T(8,128)(2,1)S(1)} %gather_fusion.1), channel_id=1, source_target_pairs={{0,1},{1,2},{2,3},{3,0},{4,5},{5,6},{6,7},{7,4},{8,9},{9,10},{10,1... | collective-permute-start | bytes 786440 | tf_op jit(solution)/shard_map/ppermute | solution.py:54
  108.9 0.7 copy-start.9
  109.5 29.3 %collective-permute-start.11 = (bf16[256,640]{1,0:T(8,128)(2,1)}, bf16[256,640]{1,0:T(8,128)(2,1)}, u32[]{:S(2)}, u32[]{:S(2)}) collective-permute-start(bf16[256,640]{1,0:T(8,128)(2,1)} %get-tuple-element.66), channel_id=1, source_target_pairs={{0,4},{1,5},{2,6},{3,7},{4,0},{5,1},{6,2},{7,3},{8,12},{9,13},{10,... | collective-permute-start | bytes 983048 | tf_op jit(solution)/shard_map/ppermute | solution.py:58
  117.7 0.7 copy-start.11
  118.4 20.5 %collective-permute-start.10 = (bf16[256,640]{1,0:T(8,128)(2,1)}, bf16[256,640]{1,0:T(8,128)(2,1)}, u32[]{:S(2)}, u32[]{:S(2)}) collective-permute-start(bf16[256,640]{1,0:T(8,128)(2,1)} %get-tuple-element.64), channel_id=1, source_target_pairs={{0,4},{1,5},{2,6},{3,7},{4,0},{5,1},{6,2},{7,3},{8,12},{9,13},{10,... | collective-permute-start | bytes 983048 | tf_op jit(solution)/shard_map/ppermute | solution.py:58
  123.5 18.0 %collective-permute-start.12 = (bf16[32,2048]{1,0:T(8,128)(2,1)}, bf16[32,2048]{1,0:T(8,128)(2,1)S(1)}, u32[]{:S(2)}, u32[]{:S(2)}) collective-permute-start(bf16[32,2048]{1,0:T(8,128)(2,1)} %get-tuple-element.78), channel_id=1, source_target_pairs={{0,0},{1,16},{2,32},{3,48},{4,4},{5,20},{6,36},{7,52},{8,8},{9,24}... | collective-permute-start | bytes 393224 | tf_op jit(solution)/shard_map/ppermute | solution.py:379
  127.8 14.6 %collective-permute-start.13 = (bf16[32,2048]{1,0:T(8,128)(2,1)}, bf16[32,2048]{1,0:T(8,128)(2,1)S(1)}, u32[]{:S(2)}, u32[]{:S(2)}) collective-permute-start(bf16[32,2048]{1,0:T(8,128)(2,1)} %get-tuple-element.79), channel_id=1, source_target_pairs={{0,4},{1,20},{2,36},{3,52},{4,0},{5,16},{6,32},{7,48},{8,12},{9,28... | collective-permute-start | bytes 393224 | tf_op jit(solution)/shard_map/ppermute | solution.py:379
  134.9 4.0 %copy-start.7 = (bf16[128,3,512]{2,0,1:T(8,128)(2,1)S(1)}, bf16[128,3,512]{2,0,1:T(8,128)(2,1)}, u32[]{:S(2)}) copy-start(bf16[128,3,512]{2,0,1:T(8,128)(2,1)} %param.29) | copy-start | bytes 1179652
  134.9 4.0 %copy-start.8 = (bf16[288,512]{1,0:T(8,128)(2,1)S(1)}, bf16[288,512]{1,0:T(8,128)(2,1)}, u32[]{:S(2)}) copy-start(bf16[288,512]{1,0:T(8,128)(2,1)} %refs_7_.1) | copy-start | bytes 884740
  134.9 4.0 %copy-start.10 = (f32[256,128]{1,0:T(8,128)S(1)}, f32[256,128]{1,0:T(8,128)}, u32[]{:S(2)}) copy-start(f32[256,128]{1,0:T(8,128)} %copy-done.9) | copy-start | bytes 393220
  134.9 4.0 %copy-start.12 = (f32[256,128]{1,0:T(8,128)S(1)}, f32[256,128]{1,0:T(8,128)}, u32[]{:S(2)}) copy-start(f32[256,128]{1,0:T(8,128)} %copy-done.11) | copy-start | bytes 393220
  134.9 4.0 %copy-start.13 = (f32[4,512]{1,0:T(4,128)S(1)}, f32[4,512]{1,0:T(4,128)}, u32[]{:S(2)}) copy-start(f32[4,512]{1,0:T(4,128)} %refs_5_.1) | copy-start | bytes 24580
  134.9 3.9 %copy-start.14 = (f32[512]{0:T(512)S(1)}, f32[512]{0:T(512)}, u32[]{:S(2)}) copy-start(f32[512]{0:T(512)} %param.32) | copy-start | bytes 6148
  138.0 0.8 copy-start.4
  138.8 25.6 %copy-start.5 = (bf16[512,512]{1,0:T(8,128)(2,1)S(1)}, bf16[512,512]{1,0:T(8,128)(2,1)}, u32[]{:S(2)}) copy-start(bf16[512,512]{1,0:T(8,128)(2,1)} %copy-done.4) | copy-start | bytes 1572868
  141.6 28.8 %copy-start.24 = (f32[512]{0:T(512)S(1)}, f32[512]{0:T(512)}, u32[]{:S(2)}) copy-start(f32[512]{0:T(512)} %param.35) | copy-start | bytes 6148
  142.4 7.6 %collective-permute-start.14 = (bf16[128,288]{1,0:T(8,128)(2,1)S(1)}, bf16[128,288]{1,0:T(8,128)(2,1)S(1)}, u32[]{:S(2)}, u32[]{:S(2)}) collective-permute-start(bf16[128,288]{1,0:T(8,128)(2,1)S(1)} %get-tuple-element.127), channel_id=1, source_target_pairs={{0,3},{1,0},{2,1},{3,2},{4,7},{5,4},{6,5},{7,6},{8,11},{9,8},{10,9... | collective-permute-start | bytes 221192 | tf_op jit(solution)/shard_map/ppermute | solution.py:54
  143.0 7.0 %collective-permute-start.15 = (bf16[128,288]{1,0:T(8,128)(2,1)S(1)}, bf16[128,288]{1,0:T(8,128)(2,1)S(1)}, u32[]{:S(2)}, u32[]{:S(2)}) collective-permute-start(bf16[128,288]{1,0:T(8,128)(2,1)S(1)} %get-tuple-element.129), channel_id=1, source_target_pairs={{0,2},{1,3},{2,0},{3,1},{4,6},{5,7},{6,4},{7,5},{8,10},{9,11},{10,... | collective-permute-start | bytes 221192 | tf_op jit(solution)/shard_map/ppermute | solution.py:54
  145.2 5.4 %collective-permute-start.16 = (bf16[128,288]{1,0:T(8,128)(2,1)S(1)}, bf16[128,288]{1,0:T(8,128)(2,1)S(1)}, u32[]{:S(2)}, u32[]{:S(2)}) collective-permute-start(bf16[128,288]{1,0:T(8,128)(2,1)S(1)} %get-tuple-element.128), channel_id=1, source_target_pairs={{0,1},{1,2},{2,3},{3,0},{4,5},{5,6},{6,7},{7,4},{8,9},{9,10},{10,1... | collective-permute-start | bytes 221192 | tf_op jit(solution)/shard_map/ppermute | solution.py:54
  150.0 0.6 copy-start.19
  150.0 1.3 copy-start.20
  150.6 0.7 copy-start.21
  151.3 6.4 %collective-permute-start.17 = (bf16[128,288]{1,0:T(8,128)(2,1)}, bf16[128,288]{1,0:T(8,128)(2,1)}, u32[]{:S(2)}, u32[]{:S(2)}) collective-permute-start(bf16[128,288]{1,0:T(8,128)(2,1)} %fusion.40), channel_id=1, source_target_pairs={{0,4},{1,5},{2,6},{3,7},{4,0},{5,1},{6,2},{7,3},{8,12},{9,13},{10,... | collective-permute-start | bytes 221192 | tf_op jit(solution)/shard_map/ppermute | solution.py:58
  160.4 7.0 %collective-permute-start.18 = (bf16[128,288]{1,0:T(8,128)(2,1)}, bf16[128,288]{1,0:T(8,128)(2,1)S(1)}, u32[]{:S(2)}, u32[]{:S(2)}) collective-permute-start(bf16[128,288]{1,0:T(8,128)(2,1)} %add_convert_fusion.1), channel_id=1, source_target_pairs={{0,3},{1,0},{2,1},{3,2},{4,7},{5,4},{6,5},{7,6},{8,11},{9,8},{10,9... | collective-permute-start | bytes 221192 | tf_op jit(solution)/shard_map/ppermute | solution.py:54
  161.1 7.0 %collective-permute-start.19 = (bf16[128,288]{1,0:T(8,128)(2,1)}, bf16[128,288]{1,0:T(8,128)(2,1)S(1)}, u32[]{:S(2)}, u32[]{:S(2)}) collective-permute-start(bf16[128,288]{1,0:T(8,128)(2,1)} %add_convert_fusion.1), channel_id=1, source_target_pairs={{0,2},{1,3},{2,0},{3,1},{4,6},{5,7},{6,4},{7,5},{8,10},{9,11},{10,... | collective-permute-start | bytes 221192 | tf_op jit(solution)/shard_map/ppermute | solution.py:54
  164.2 4.8 %collective-permute-start.20 = (bf16[128,288]{1,0:T(8,128)(2,1)}, bf16[128,288]{1,0:T(8,128)(2,1)S(1)}, u32[]{:S(2)}, u32[]{:S(2)}) collective-permute-start(bf16[128,288]{1,0:T(8,128)(2,1)} %add_convert_fusion.1), channel_id=1, source_target_pairs={{0,1},{1,2},{2,3},{3,0},{4,5},{5,6},{6,7},{7,4},{8,9},{9,10},{10,1... | collective-permute-start | bytes 221192 | tf_op jit(solution)/shard_map/ppermute | solution.py:54
  164.4 21.8 %collective-permute-start.21 = (bf16[512,512]{1,0:T(8,128)(2,1)S(1)}, bf16[512,512]{1,0:T(8,128)(2,1)S(1)}, u32[]{:S(2)}, u32[]{:S(2)}) collective-permute-start(bf16[512,512]{1,0:T(8,128)(2,1)S(1)} %copy-done.5), channel_id=1, source_target_pairs={{0,4},{1,5},{2,6},{3,7},{4,0},{5,1},{6,2},{7,3},{8,12},{9,13},{10,... | collective-permute-start | bytes 1572872 | tf_op jit(solution)/shard_map/ppermute | solution.py:58
  170.2 2.2 copy-start.15
  172.4 13.9 %copy-start.23 = (f32[512]{0:T(512)S(1)}, f32[512]{0:T(512)}, u32[]{:S(2)}) copy-start(f32[512]{0:T(512)} %param.37) | copy-start | bytes 6148
  186.8 10.9 %collective-permute-start.22 = (bf16[256,512]{1,0:T(8,128)(2,1)S(1)}, bf16[256,512]{1,0:T(8,128)(2,1)S(1)}, u32[]{:S(2)}, u32[]{:S(2)}) collective-permute-start(bf16[256,512]{1,0:T(8,128)(2,1)S(1)} %pad_maximum_fusion.3.refs_0_), channel_id=1, source_target_pairs={{0,3},{1,0},{2,1},{3,2},{4,7},{5,4},{6,5},{7,6},{8,11},{9,8},{10,9... | collective-permute-start | bytes 786440 | tf_op jit(solution)/shard_map/ppermute | solution.py:54
  189.7 8.0 %collective-permute-start.23 = (bf16[256,512]{1,0:T(8,128)(2,1)S(1)}, bf16[256,512]{1,0:T(8,128)(2,1)S(1)}, u32[]{:S(2)}, u32[]{:S(2)}) collective-permute-start(bf16[256,512]{1,0:T(8,128)(2,1)S(1)} %pad_maximum_fusion.3.refs_0_), channel_id=1, source_target_pairs={{0,2},{1,3},{2,0},{3,1},{4,6},{5,7},{6,4},{7,5},{8,10},{9,11},{10,... | collective-permute-start | bytes 786440 | tf_op jit(solution)/shard_map/ppermute | solution.py:54
  189.8 8.3 %collective-permute-start.24 = (bf16[256,512]{1,0:T(8,128)(2,1)S(1)}, bf16[256,512]{1,0:T(8,128)(2,1)S(1)}, u32[]{:S(2)}, u32[]{:S(2)}) collective-permute-start(bf16[256,512]{1,0:T(8,128)(2,1)S(1)} %pad_maximum_fusion.3.refs_0_), channel_id=1, source_target_pairs={{0,1},{1,2},{2,3},{3,0},{4,5},{5,6},{6,7},{7,4},{8,9},{9,10},{10,1... | collective-permute-start | bytes 786440 | tf_op jit(solution)/shard_map/ppermute | solution.py:54
  192.5 12.4 %collective-permute-start.25 = (bf16[256,512]{1,0:T(8,128)(2,1)S(1)}, bf16[256,512]{1,0:T(8,128)(2,1)S(1)}, u32[]{:S(2)}, u32[]{:S(2)}) collective-permute-start(bf16[256,512]{1,0:T(8,128)(2,1)S(1)} %pad_maximum_fusion.4.refs_4_.refs_0_), channel_id=1, source_target_pairs={{0,3},{1,0},{2,1},{3,2},{4,7},{5,4},{6,5},{7,6},{8,11},{9,8},{10,9... | collective-permute-start | bytes 786440 | tf_op jit(solution)/shard_map/ppermute | solution.py:54
  192.8 12.1 %collective-permute-start.26 = (bf16[256,512]{1,0:T(8,128)(2,1)S(1)}, bf16[256,512]{1,0:T(8,128)(2,1)S(1)}, u32[]{:S(2)}, u32[]{:S(2)}) collective-permute-start(bf16[256,512]{1,0:T(8,128)(2,1)S(1)} %pad_maximum_fusion.4.refs_4_.refs_0_), channel_id=1, source_target_pairs={{0,2},{1,3},{2,0},{3,1},{4,6},{5,7},{6,4},{7,5},{8,10},{9,11},{10,... | collective-permute-start | bytes 786440 | tf_op jit(solution)/shard_map/ppermute | solution.py:54
  197.7 7.2 %collective-permute-start.27 = (bf16[256,512]{1,0:T(8,128)(2,1)S(1)}, bf16[256,512]{1,0:T(8,128)(2,1)S(1)}, u32[]{:S(2)}, u32[]{:S(2)}) collective-permute-start(bf16[256,512]{1,0:T(8,128)(2,1)S(1)} %pad_maximum_fusion.4.refs_4_.refs_0_), channel_id=1, source_target_pairs={{0,1},{1,2},{2,3},{3,0},{4,5},{5,6},{6,7},{7,4},{8,9},{9,10},{10,1... | collective-permute-start | bytes 786440 | tf_op jit(solution)/shard_map/ppermute | solution.py:54
  202.0 11.7 %collective-permute-start.28 = (bf16[256,512]{1,0:T(8,128)(2,1)S(1)}, bf16[256,512]{1,0:T(8,128)(2,1)S(1)}, u32[]{:S(2)}, u32[]{:S(2)}) collective-permute-start(bf16[256,512]{1,0:T(8,128)(2,1)S(1)} %out_product.4), channel_id=1, source_target_pairs={{0,4},{1,5},{2,6},{3,7},{4,0},{5,1},{6,2},{7,3},{8,12},{9,13},{10,... | collective-permute-start | bytes 786440 | tf_op jit(solution)/shard_map/ppermute | solution.py:58
  207.5 10.1 %collective-permute-start.29 = (bf16[256,512]{1,0:T(8,128)(2,1)S(1)}, bf16[256,512]{1,0:T(8,128)(2,1)S(1)}, u32[]{:S(2)}, u32[]{:S(2)}) collective-permute-start(bf16[256,512]{1,0:T(8,128)(2,1)S(1)} %out_product.5), channel_id=1, source_target_pairs={{0,4},{1,5},{2,6},{3,7},{4,0},{5,1},{6,2},{7,3},{8,12},{9,13},{10,... | collective-permute-start | bytes 786440 | tf_op jit(solution)/shard_map/ppermute | solution.py:58
Sparse Core Ops, SparseCore 0:
  35.7 69.8 all-gather.3
  159.6 39.6 all-gather.5

commit v6 on v5

--- a/solution.py
+++ b/solution.py
@@ -126,8 +126,7 @@
         at = slice(step * rows, (step + 1) * rows)
         p, local = divmod(step, steps // parts)
         inner = slice(local * rows, (local + 1) * rows)
-        sent = aways[p][inner, 512:].astype(jnp.float32)
-        squares = sums[p][inner, :1] + sent[:, :1] + sent[:, 64:65]
+        squares = sums[p][inner, :1]
         factor = lax.rsqrt(squares / 4096.0 + norm_eps)
         scale[at, :] = jnp.broadcast_to(factor, (rows, 128))
         total = here[at, :] + aways[p][inner, :512].astype(jnp.float32)
@@ -367,10 +366,13 @@
 
     chunks = spread(found)
     aways, sums = [], []
-    for part in chunks:
-        away, squares = in_product([part], weights_in, 0, 1 - yh, x, bf16, squared=True)
-        aways.append(away)
-        sums.append(squares)
+    for p, part in enumerate(chunks):
+        squares = sum(jnp.sum(jnp.square(c.astype(f32)), axis=1) for c in part).reshape(-1, 128)
+        squares = squares + from_partner(squares)
+        *part, squares = lax.optimization_barrier((*part, squares))
+        chunks[p] = part
+        aways.append(in_product([part], weights_in, 0, 1 - yh, x, bf16))
+        sums.append(jnp.broadcast_to(squares.reshape(-1, 1), (half, 128)))
     out_new = adam_update(out_master, out_moment, out_velocity, out_grad)
     halves = out_new.astype(bf16).reshape(own, 2, 2048)
     sent = [lax.dynamic_index_in_dim(halves, (yh + j) % 2, 1, keepdims=False) for j in range(2)]

time: 228 us -> 230 us (level)
  waiting for transfers between devices: 71.7 us -> 75.3 us
  starting transfers between devices: 68.2 us -> 71.7 us
  Pallas kernels: 30.3 us -> 27.5 us
    ppermute x18, starting transfers between devices: 22.5 us -> 26.1 us  [from_x(): lax.ppermute(a, 'chan', [(i, i // 4 * 4 + (i % 4 - k) % 4) for i in range...]
    ppermute x6 -> x8, waiting for transfers between devices: 13.1 us -> 16.6 us  [from_partner(): return lax.ppermute(a, 'chan', [(i, i ^ 4) for i in range(8)])]
    ppermute x18, waiting for transfers between devices: 20.5 us -> 23.9 us  [from_x(): lax.ppermute(a, 'chan', [(i, i // 4 * 4 + (i % 4 - k) % 4) for i in range...]
    unnamed x51 -> x45, local copies, waits for them, and re-layouts: 9.48 us -> 8.24 us
    ppermute x6 -> x8, starting transfers between devices: 16.5 us -> 16.8 us  [from_partner(): return lax.ppermute(a, 'chan', [(i, i ^ 4) for i in range(8)])]
  transfers between devices with their start and end apart: 34 -> 36, of which waited for: 19 -> 19; matrix products, arithmetic and copies ran while one was open for 12% -> 12% of each run, Pallas kernels for 13% -> 11%
where the time goes in v6:
time: 230 us; the launch traced here: 229 us
  waiting for transfers between devices  75.3 us (33%)
  starting transfers between devices  71.7 us (31%)
  Pallas kernels  27.5 us (12%)
  local copies, waits for them, and re-layouts  20.5 us (9%)
  other arithmetic  18.2 us (8%)
  between operations  14.8 us (6%)
    all_to_all x1, waiting for transfers between devices, per_device(): lax.all_to_all(looked.reshape(replicas, capacity, feature_part), 'fsdp',...  26.5 us
    ppermute x18, starting transfers between devices, from_x(): lax.ppermute(a, 'chan', [(i, i // 4 * 4 + (i % 4 - k) % 4) for i in range...  26.1 us
    ppermute x18, waiting for transfers between devices, from_x(): lax.ppermute(a, 'chan', [(i, i // 4 * 4 + (i % 4 - k) % 4) for i in range...  23.9 us
    ppermute x8, starting transfers between devices, from_partner(): return lax.ppermute(a, 'chan', [(i, i ^ 4) for i in range(8)])  16.8 us
    ppermute x8, waiting for transfers between devices, from_partner(): return lax.ppermute(a, 'chan', [(i, i ^ 4) for i in range(8)])  16.6 us
    pallas_call x5, Pallas kernels, in_product(): pl.pallas_call(functools.partial(in_product_kernel, len(parts), matrix, s...  14.2 us
    all_to_all x1, starting transfers between devices, per_device(): lax.all_to_all(looked.reshape(replicas, capacity, feature_part), 'fsdp',...  10.7 us
    pallas_call x3, Pallas kernels, out_product(): pl.pallas_call(functools.partial(out_product_kernel, len(parts)), out_sha...  8.43 us
  transfers between devices with their start and end apart: 36, of which 19 were waited for; matrix products, arithmetic and copies ran while one was open for 12% of the time, Pallas kernels for 11%

profile of v6, /device:TPU:6, one launch (start us, length us, event | category | flops | bytes accessed | tf_op | source)
XLA Modules:
  0.0 228.8 jit_solution(3677487328620811330)
XLA Ops:
  9.1 6.4 %all-to-all-start = ((s32[16,1,64]{2,1,0:T(1,128)}), s32[16,1,64]{2,1,0:T(1,128)S(1)}, u32[]{:S(2)}, u32[]{:S(2)}) async-start(s32[16,1,64]{2,1,0:T(1,128)} %all_to_all.11), calls=%async_computation | async-start | bytes 16384 | tf_op jit(solution)/shard_map/all_to_all | solution.py:335
  15.6 1.2 copy-done.1
  16.8 1.2 copy-done.2
  18.0 1.2 copy-done.3
  19.3 1.0 copy-done.6
  20.3 3.4 %adam_in.1 = (f32[2048,128]{1,0:T(8,128)}, bf16[2,32,1024]{2,1,0:T(8,128)(2,1)S(1)}, bf16[2,32,1024]{2,1,0:T(8,128)(2,1)S(1)}, bf16[2,32,1024]{2,1,0:T(8,128)(2,1)S(1)}, bf16[2,32,1024]{2,1,0:T(8,128)(2,1)S(1)}) custom-call(s32[1]{0:T(128)} %bitcast.s_ref, f32[2048,128]{1,0:T(8,128)S(1)} %bitcast.96, f32[2048,128]{1,0:T(8,128)S(1)} %bitcast.97, ...), custom_call_target="tpu_custom_call" | custom-call | flops 5242880 | bytes 5242880 | tf_op jit(solution)/shard_map/adam_in/pallas_call | solution.py:102
  24.9 2.4 %collective-permute-start.10 = (bf16[2,32,1024]{2,1,0:T(8,128)(2,1)S(1)}, bf16[2,32,1024]{2,1,0:T(8,128)(2,1)S(1)}, u32[]{:S(2)}, u32[]{:S(2)}) collective-permute-start(bf16[2,32,1024]{2,1,0:T(8,128)(2,1)S(1)} %get-tuple-element.75), channel_id=1, source_target_pairs={{0,2},{1,3},{2,0},{3,1},{4,66},{5,67},{6,64},{7,65},{8,10},{9,11},... | collective-permute-start | bytes 393224 | tf_op jit(solution)/shard_map/ppermute | solution.py:345
  27.4 3.3 %collective-permute-done.9 = bf16[2,32,1024]{2,1,0:T(8,128)(2,1)S(1)} collective-permute-done((bf16[2,32,1024]{2,1,0:T(8,128)(2,1)S(1)}, bf16[2,32,1024]{2,1,0:T(8,128)(2,1)S(1)}, u32[]{:S(2)}, u32[]{:S(2)}) %collective-permute-start.9) | collective-permute-done | bytes 131104 | tf_op jit(solution)/shard_map/ppermute | solution.py:345
  30.8 2.0 collective-permute-done.10
  32.8 2.0 collective-permute-done.11
  35.7 1.2 fusion.45
  37.3 7.8 %gather_fusion = bf16[1024,512]{1,0:T(8,128)(2,1)} fusion(bf16[4096,512]{1,0:T(8,128)(2,1)} %param.27, s32[1024]{0:T(1024)S(1)} %broadcast_clamp_fusion), kind=kCustom, calls=%fused_computation | custom fusion | bytes 2101248 | tf_op jit(solution)/shard_map/gather | solution.py:350
  45.2 10.7 %all-to-all-start.1 = ((bf16[16,64,512]{2,1,0:T(8,128)(2,1)}), bf16[16,64,512]{2,1,0:T(8,128)(2,1)S(1)}, u32[]{:S(2)}, u32[]{:S(2)}) async-start(bf16[16,64,512]{2,1,0:T(8,128)(2,1)} %bitcast.19), calls=%async_computation.1 | async-start | bytes 2097152 | tf_op jit(solution)/shard_map/all_to_all | solution.py:351
  57.3 26.5 %all-to-all-done.1 = bf16[16,64,512]{2,1,0:T(8,128)(2,1)S(1)} async-done(((bf16[16,64,512]{2,1,0:T(8,128)(2,1)}), bf16[16,64,512]{2,1,0:T(8,128)(2,1)S(1)}, u32[]{:S(2)}, u32[]{:S(2)}) %all-to-all-start.1) | async-done | bytes 1048608 | tf_op jit(solution)/shard_map/all_to_all | solution.py:351
  83.9 1.2 gather_fusion.1
  85.0 1.2 gather_fusion.2
  86.2 1.2 collective-permute-start.6
  87.4 1.8 collective-permute-start.5
  89.4 1.7 collective-permute-start
  91.1 1.6 collective-permute-start.2
  92.9 5.0 %collective-permute-done.6.refs_7_.refs_3_ = bf16[256,512]{1,0:T(8,128)(2,1)S(1)} collective-permute-done((bf16[256,512]{1,0:T(8,128)(2,1)S(1)}, bf16[256,512]{1,0:T(8,128)(2,1)S(1)}, u32[]{:S(2)}, u32[]{:S(2)}) %collective-permute-start.6) | collective-permute-done | bytes 262176 | tf_op jit(solution)/shard_map/ppermute | solution.py:54
  97.9 2.8 %collective-permute-start.1 = (bf16[256,512]{1,0:T(8,128)(2,1)S(1)}, bf16[256,512]{1,0:T(8,128)(2,1)S(1)}, u32[]{:S(2)}, u32[]{:S(2)}) collective-permute-start(bf16[256,512]{1,0:T(8,128)(2,1)S(1)} %gather_fusion.1), channel_id=1, source_target_pairs={{0,2},{1,3},{2,0},{3,1},{4,6},{5,7},{6,4},{7,5},{8,10},{9,11},{10,... | collective-permute-start | bytes 786440 | tf_op jit(solution)/shard_map/ppermute | solution.py:54
  100.9 1.2 collective-permute-done.4.refs_5_.refs_1_
  102.3 1.7 collective-permute-start.7
  104.0 5.3 %collective-permute-done.refs_1_ = bf16[256,512]{1,0:T(8,128)(2,1)S(1)} collective-permute-done((bf16[256,512]{1,0:T(8,128)(2,1)S(1)}, bf16[256,512]{1,0:T(8,128)(2,1)S(1)}, u32[]{:S(2)}, u32[]{:S(2)}) %collective-permute-start) | collective-permute-done | bytes 262176 | tf_op jit(solution)/shard_map/ppermute | solution.py:54
  109.6 3.7 %collective-permute-done.1.refs_2_ = bf16[256,512]{1,0:T(8,128)(2,1)S(1)} collective-permute-done((bf16[256,512]{1,0:T(8,128)(2,1)S(1)}, bf16[256,512]{1,0:T(8,128)(2,1)S(1)}, u32[]{:S(2)}, u32[]{:S(2)}) %collective-permute-start.1) | collective-permute-done | bytes 262176 | tf_op jit(solution)/shard_map/ppermute | solution.py:54
  113.5 1.3 collective-permute-start.3
  114.8 3.8 %collective-permute-done.3 = f32[2,128]{1,0:T(2,128)S(1)} collective-permute-done((f32[2,128]{1,0:T(2,128)S(1)}, f32[2,128]{1,0:T(2,128)S(1)}, u32[]{:S(2)}, u32[]{:S(2)}) %collective-permute-start.3) | collective-permute-done | bytes 1056 | tf_op jit(solution)/shard_map/ppermute | solution.py:58
  118.7 2.5 %in_product.7 = bf16[256,512]{1,0:T(8,128)(2,1)S(1)} custom-call(s32[2]{0:T(128)S(1)} %pad_add_fusion.1.s_ref, bf16[256,512]{1,0:T(8,128)(2,1)S(1)} %gather_fusion.2, bf16[256,512]{1,0:T(8,128)(2,1)S(1)} %collective-permute-done.4.refs_5_.refs_1_, bf16[256,512]{1,0:T(8,128)(2,1)S(1)} %collective-permute-done.5.refs_6_.refs_2_, ...), custom_call_target="tpu_custom_call" | custom-call | flops 536870912 | bytes 6291456 | tf_op jit(solution)/shard_map/in_product/pallas_call | solution.py:220
  121.2 1.3 collective-permute-start.13
  122.5 2.5 %in_product.6 = bf16[256,512]{1,0:T(8,128)(2,1)S(1)} custom-call(s32[2]{0:T(128)S(1)} %pad_add_fusion.1.s_ref, bf16[256,512]{1,0:T(8,128)(2,1)S(1)} %gather_fusion.1, bf16[256,512]{1,0:T(8,128)(2,1)S(1)} %collective-permute-done.refs_1_, bf16[256,512]{1,0:T(8,128)(2,1)S(1)} %collective-permute-done.1.refs_2_, ...), custom_call_target="tpu_custom_call" | custom-call | flops 536870912 | bytes 6291456 | tf_op jit(solution)/shard_map/in_product/pallas_call | solution.py:220
  125.1 2.3 %collective-permute-start.12 = (bf16[256,512]{1,0:T(8,128)(2,1)S(1)}, bf16[256,512]{1,0:T(8,128)(2,1)S(1)}, u32[]{:S(2)}, u32[]{:S(2)}) collective-permute-start(bf16[256,512]{1,0:T(8,128)(2,1)S(1)} %in_product.6), channel_id=1, source_target_pairs={{0,4},{1,5},{2,6},{3,7},{4,0},{5,1},{6,2},{7,3},{8,12},{9,13},{10,... | collective-permute-start | bytes 786440 | tf_op jit(solution)/shard_map/ppermute | solution.py:58
  127.4 3.1 %in_product.5.here = f32[512,512]{1,0:T(8,128)S(1)} custom-call(s32[2]{0:T(128)S(1)} %pad_add_fusion.s_ref, bf16[256,512]{1,0:T(8,128)(2,1)S(1)} %gather_fusion.1, bf16[256,512]{1,0:T(8,128)(2,1)S(1)} %collective-permute-done.refs_1_, bf16[256,512]{1,0:T(8,128)(2,1)S(1)} %collective-permute-done.1.refs_2_, ...), custom_call_target="tpu_custom_call" | custom-call | flops 1073741824 | bytes 6291456 | tf_op jit(solution)/shard_map/in_product/pallas_call | solution.py:220
  130.5 2.0 collective-permute-start.14
  132.5 6.1 %collective-permute-start.15 = (bf16[32,2048]{1,0:T(8,128)(2,1)}, bf16[32,2048]{1,0:T(8,128)(2,1)S(1)}, u32[]{:S(2)}, u32[]{:S(2)}) collective-permute-start(bf16[32,2048]{1,0:T(8,128)(2,1)} %get-tuple-element.91), channel_id=1, source_target_pairs={{0,4},{1,20},{2,36},{3,52},{4,0},{5,16},{6,32},{7,48},{8,12},{9,28... | collective-permute-start | bytes 393224 | tf_op jit(solution)/shard_map/ppermute | solution.py:381
  138.5 3.1 %in_product.9 = f32[512,512]{1,0:T(8,128)S(1)} custom-call(s32[2]{0:T(128)S(1)} %pad_add_fusion.s_ref, bf16[256,512]{1,0:T(8,128)(2,1)S(1)} %gather_fusion.1, bf16[256,512]{1,0:T(8,128)(2,1)S(1)} %collective-permute-done.refs_1_, bf16[256,512]{1,0:T(8,128)(2,1)S(1)} %collective-permute-done.1.refs_2_, bf16[256,512]{1,0:T(8,128)(2,1)S(1)} %collective-permute-done.2.refs_3_, ...), custom_call_target="tpu_custom_call" | custom-call | flops 1073741824 | bytes 6291456 | tf_op jit(solution)/shard_map/in_product/pallas_call | solution.py:220
  141.6 3.1 %in_product.8 = bf16[512,512]{1,0:T(8,128)(2,1)S(1)} custom-call(s32[2]{0:T(128)S(1)} %pad_add_fusion.1.s_ref, bf16[256,512]{1,0:T(8,128)(2,1)S(1)} %gather_fusion.1, bf16[256,512]{1,0:T(8,128)(2,1)S(1)} %collective-permute-done.refs_1_, bf16[256,512]{1,0:T(8,128)(2,1)S(1)} %collective-permute-done.1.refs_2_, ...), custom_call_target="tpu_custom_call" | custom-call | flops 1073741824 | bytes 6291456 | tf_op jit(solution)/shard_map/in_product/pallas_call | solution.py:220
  145.8 1.4 conv.1
  147.4 1.4 collective-permute-start.17
  148.8 1.8 collective-permute-start.18
  150.6 3.6 %collective-permute-done.16 = bf16[128,288]{1,0:T(8,128)(2,1)S(1)} collective-permute-done((bf16[128,288]{1,0:T(8,128)(2,1)S(1)}, bf16[128,288]{1,0:T(8,128)(2,1)S(1)}, u32[]{:S(2)}, u32[]{:S(2)}) %collective-permute-start.16) | collective-permute-done | bytes 73760 | tf_op jit(solution)/shard_map/ppermute | solution.py:54
  155.8 2.3 collective-permute-start.19
  158.8 3.4 %collective-permute-done.19 = bf16[128,288]{1,0:T(8,128)(2,1)} collective-permute-done((bf16[128,288]{1,0:T(8,128)(2,1)}, bf16[128,288]{1,0:T(8,128)(2,1)}, u32[]{:S(2)}, u32[]{:S(2)}) %collective-permute-start.19) | collective-permute-done | bytes 73760 | tf_op jit(solution)/shard_map/ppermute | solution.py:58
  162.3 1.7 add_convert_fusion.1
  164.9 1.0 collective-permute-start.20
  165.9 2.9 %collective-permute-start.21 = (bf16[128,288]{1,0:T(8,128)(2,1)}, bf16[128,288]{1,0:T(8,128)(2,1)S(1)}, u32[]{:S(2)}, u32[]{:S(2)}) collective-permute-start(bf16[128,288]{1,0:T(8,128)(2,1)} %add_convert_fusion.1), channel_id=1, source_target_pairs={{0,2},{1,3},{2,0},{3,1},{4,6},{5,7},{6,4},{7,5},{8,10},{9,11},{10,... | collective-permute-start | bytes 221192 | tf_op jit(solution)/shard_map/ppermute | solution.py:54
  168.9 2.3 %collective-permute-start.23 = (bf16[512,512]{1,0:T(8,128)(2,1)S(1)}, bf16[512,512]{1,0:T(8,128)(2,1)S(1)}, u32[]{:S(2)}, u32[]{:S(2)}) collective-permute-start(bf16[512,512]{1,0:T(8,128)(2,1)S(1)} %copy-done.5), channel_id=1, source_target_pairs={{0,4},{1,5},{2,6},{3,7},{4,0},{5,1},{6,2},{7,3},{8,12},{9,13},{10,... | collective-permute-start | bytes 1572872 | tf_op jit(solution)/shard_map/ppermute | solution.py:58
  171.3 1.3 collective-permute-done.21
  172.6 1.0 collective-permute-done.22
  173.6 1.0 pad_maximum_fusion
  176.0 1.0 copy-done.11
  177.0 7.5 %multiply_reduce_fusion = (f32[128,512]{1,0:T(8,128)S(1)}, f32[128,16,512]{2,1,0:T(8,128)}, f32[128,512]{1,0:T(8,128)S(1)}, f32[128,512]{1,0:T(8,128)S(1)}, f32[128,512]{1,0:T(8,128)S(1)}) fusion(f32[128,16]{1,0:T(8,128)S(1)} %get-tuple-element.126, f32[128,16]{1,0:T(8,128)S(1)} %get-tuple-element.125, f32[128,512]{1,0:T(8,128)S(1)} %get-tuple-element.113, ...), kind=kLoop, calls=%fused_computation.3 | loop fusion | flops 24903680 | bytes 11632640 | tf_op jit(solution)/shard_map/reduce_sum | solution.py:428
  184.5 5.0 %collective-permute-done.23 = bf16[512,512]{1,0:T(8,128)(2,1)S(1)} collective-permute-done((bf16[512,512]{1,0:T(8,128)(2,1)S(1)}, bf16[512,512]{1,0:T(8,128)(2,1)S(1)}, u32[]{:S(2)}, u32[]{:S(2)}) %collective-permute-start.23) | collective-permute-done | bytes 524320 | tf_op jit(solution)/shard_map/ppermute | solution.py:58
  190.1 3.5 %collective-permute-start.24 = (bf16[256,512]{1,0:T(8,128)(2,1)S(1)}, bf16[256,512]{1,0:T(8,128)(2,1)S(1)}, u32[]{:S(2)}, u32[]{:S(2)}) collective-permute-start(bf16[256,512]{1,0:T(8,128)(2,1)S(1)} %pad_maximum_fusion.3.refs_0_), channel_id=1, source_target_pairs={{0,3},{1,0},{2,1},{3,2},{4,7},{5,4},{6,5},{7,6},{8,11},{9,8},{10,9... | collective-permute-start | bytes 786440 | tf_op jit(solution)/shard_map/ppermute | solution.py:54
  194.4 2.2 collective-permute-start.26
  196.7 2.6 %collective-permute-start.28 = (bf16[256,512]{1,0:T(8,128)(2,1)S(1)}, bf16[256,512]{1,0:T(8,128)(2,1)S(1)}, u32[]{:S(2)}, u32[]{:S(2)}) collective-permute-start(bf16[256,512]{1,0:T(8,128)(2,1)S(1)} %pad_maximum_fusion.4.refs_4_.refs_0_), channel_id=1, source_target_pairs={{0,2},{1,3},{2,0},{3,1},{4,6},{5,7},{6,4},{7,5},{8,10},{9,11},{10,... | collective-permute-start | bytes 786440 | tf_op jit(solution)/shard_map/ppermute | solution.py:54
  199.9 1.6 collective-permute-done.25.refs_2_
  202.6 2.6 %out_product.4 = bf16[256,512]{1,0:T(8,128)(2,1)S(1)} custom-call(s32[2]{0:T(128)S(1)} %pad_add_fusion.1.s_ref, bf16[256,512]{1,0:T(8,128)(2,1)S(1)} %pad_maximum_fusion.3.refs_0_, bf16[256,512]{1,0:T(8,128)(2,1)S(1)} %collective-permute-done.24.refs_1_, bf16[256,512]{1,0:T(8,128)(2,1)S(1)} %collective-permute-done.25.refs_2_, ...), custom_call_target="tpu_custom_call" | custom-call | flops 536870912 | bytes 6291456 | tf_op jit(solution)/shard_map/out_product/pallas_call | solution.py:276
  205.3 2.8 %collective-permute-start.30 = (bf16[256,512]{1,0:T(8,128)(2,1)S(1)}, bf16[256,512]{1,0:T(8,128)(2,1)S(1)}, u32[]{:S(2)}, u32[]{:S(2)}) collective-permute-start(bf16[256,512]{1,0:T(8,128)(2,1)S(1)} %out_product.4), channel_id=1, source_target_pairs={{0,4},{1,5},{2,6},{3,7},{4,0},{5,1},{6,2},{7,3},{8,12},{9,13},{10,... | collective-permute-start | bytes 786440 | tf_op jit(solution)/shard_map/ppermute | solution.py:58
  208.1 2.6 %out_product.5 = bf16[256,512]{1,0:T(8,128)(2,1)S(1)} custom-call(s32[2]{0:T(128)S(1)} %pad_add_fusion.1.s_ref, bf16[256,512]{1,0:T(8,128)(2,1)S(1)} %pad_maximum_fusion.4.refs_4_.refs_0_, bf16[256,512]{1,0:T(8,128)(2,1)S(1)} %collective-permute-done.27.refs_5_.refs_1_, bf16[256,512]{1,0:T(8,128)(2,1)S(1)} %collective-permute-done.28.refs_6_.refs_2_, ...), custom_call_target="tpu_custom_call" | custom-call | flops 536870912 | bytes 6291456 | tf_op jit(solution)/shard_map/out_product/pallas_call | solution.py:276
  210.8 2.6 %collective-permute-start.31 = (bf16[256,512]{1,0:T(8,128)(2,1)S(1)}, bf16[256,512]{1,0:T(8,128)(2,1)S(1)}, u32[]{:S(2)}, u32[]{:S(2)}) collective-permute-start(bf16[256,512]{1,0:T(8,128)(2,1)S(1)} %out_product.5), channel_id=1, source_target_pairs={{0,4},{1,5},{2,6},{3,7},{4,0},{5,1},{6,2},{7,3},{8,12},{9,13},{10,... | collective-permute-start | bytes 786440 | tf_op jit(solution)/shard_map/ppermute | solution.py:58
  213.4 3.2 %out_product.3 = f32[512,512]{1,0:T(8,128)S(1)} custom-call(s32[2]{0:T(128)S(1)} %pad_add_fusion.s_ref, bf16[256,512]{1,0:T(8,128)(2,1)S(1)} %pad_maximum_fusion.3.refs_0_, bf16[256,512]{1,0:T(8,128)(2,1)S(1)} %collective-permute-done.24.refs_1_, bf16[256,512]{1,0:T(8,128)(2,1)S(1)} %collective-permute-done.25.refs_2_, ...), custom_call_target="tpu_custom_call" | custom-call | flops 1073741824 | bytes 6291456 | tf_op jit(solution)/shard_map/out_product/pallas_call | solution.py:276
  216.6 4.4 %collective-permute-done.31 = bf16[256,512]{1,0:T(8,128)(2,1)S(1)} collective-permute-done((bf16[256,512]{1,0:T(8,128)(2,1)S(1)}, bf16[256,512]{1,0:T(8,128)(2,1)S(1)}, u32[]{:S(2)}, u32[]{:S(2)}) %collective-permute-start.31) | collective-permute-done | bytes 262176 | tf_op jit(solution)/shard_map/ppermute | solution.py:58
  220.9 1.0 add_convert_fusion
  (126 shorter events, 16.1 us)
Async XLA Ops:
  7.2 167.7 %copy-start = (bf16[512,256]{1,0:T(8,128)(2,1)S(1)}, bf16[512,256]{1,0:T(8,128)(2,1)}, u32[]{:S(2)}) copy-start(bf16[512,256]{1,0:T(8,128)(2,1)} %param.34) | copy-start | bytes 786436
  9.1 14.6 %all-to-all-start = ((s32[16,1,64]{2,1,0:T(1,128)}), s32[16,1,64]{2,1,0:T(1,128)S(1)}, u32[]{:S(2)}, u32[]{:S(2)}) async-start(s32[16,1,64]{2,1,0:T(1,128)} %all_to_all.11), calls=%async_computation | async-start | bytes 16384 | tf_op jit(solution)/shard_map/all_to_all | solution.py:335
  15.5 103.1 %all-gather.4.cloned.1.call-start = ((), (), s32[]{:S(2)}) async-start(), calls=%async_computation.2 | async-start | bytes 8912896 | tf_op jit(solution)/shard_map/all_gather | solution.py:347
  15.6 1.2 copy-start.1
  16.8 1.2 copy-start.2
  18.0 1.2 copy-start.3
  19.3 1.0 copy-start.6
  20.3 15.4 %copy-start.13 = (f32[32,4096]{1,0:T(8,128)S(1)}, f32[32,4096]{1,0:T(8,128)}, u32[]{:S(2)}) copy-start(f32[32,4096]{1,0:T(8,128)} %param.23) | copy-start | bytes 1572868
  20.3 15.4 %copy-start.14 = (f32[32,4096]{1,0:T(8,128)S(1)}, f32[32,4096]{1,0:T(8,128)}, u32[]{:S(2)}) copy-start(f32[32,4096]{1,0:T(8,128)} %param.25) | copy-start | bytes 1572868
  20.3 15.4 %copy-start.15 = (f32[32,4096]{1,0:T(8,128)S(1)}, f32[32,4096]{1,0:T(8,128)}, u32[]{:S(2)}) copy-start(f32[32,4096]{1,0:T(8,128)} %param.24) | copy-start | bytes 1572868
  20.3 15.4 %copy-start.19 = (bf16[32,4096]{1,0:T(8,128)(2,1)S(1)}, bf16[32,4096]{1,0:T(8,128)(2,1)}, u32[]{:S(2)}) copy-start(bf16[32,4096]{1,0:T(8,128)(2,1)} %param.26) | copy-start | bytes 786436
  23.7 3.6 %collective-permute-start.8 = (bf16[2,32,1024]{2,1,0:T(8,128)(2,1)S(1)}, bf16[2,32,1024]{2,1,0:T(8,128)(2,1)S(1)}, u32[]{:S(2)}, u32[]{:S(2)}) collective-permute-start(bf16[2,32,1024]{2,1,0:T(8,128)(2,1)S(1)} %get-tuple-element.73), channel_id=1, source_target_pairs={{0,0},{1,1},{2,2},{3,3},{4,64},{5,65},{6,66},{7,67},{8,8},{9,9},{1... | collective-permute-start | bytes 393224 | tf_op jit(solution)/shard_map/ppermute | solution.py:345
  24.4 6.4 %collective-permute-start.9 = (bf16[2,32,1024]{2,1,0:T(8,128)(2,1)S(1)}, bf16[2,32,1024]{2,1,0:T(8,128)(2,1)S(1)}, u32[]{:S(2)}, u32[]{:S(2)}) collective-permute-start(bf16[2,32,1024]{2,1,0:T(8,128)(2,1)S(1)} %get-tuple-element.74), channel_id=1, source_target_pairs={{0,1},{1,2},{2,3},{3,0},{4,65},{5,66},{6,67},{7,64},{8,9},{9,10},{... | collective-permute-start | bytes 393224 | tf_op jit(solution)/shard_map/ppermute | solution.py:345
  24.9 7.8 %collective-permute-start.10 = (bf16[2,32,1024]{2,1,0:T(8,128)(2,1)S(1)}, bf16[2,32,1024]{2,1,0:T(8,128)(2,1)S(1)}, u32[]{:S(2)}, u32[]{:S(2)}) collective-permute-start(bf16[2,32,1024]{2,1,0:T(8,128)(2,1)S(1)} %get-tuple-element.75), channel_id=1, source_target_pairs={{0,2},{1,3},{2,0},{3,1},{4,66},{5,67},{6,64},{7,65},{8,10},{9,11},... | collective-permute-start | bytes 393224 | tf_op jit(solution)/shard_map/ppermute | solution.py:345
  27.3 7.4 %collective-permute-start.11 = (bf16[2,32,1024]{2,1,0:T(8,128)(2,1)S(1)}, bf16[2,32,1024]{2,1,0:T(8,128)(2,1)S(1)}, u32[]{:S(2)}, u32[]{:S(2)}) collective-permute-start(bf16[2,32,1024]{2,1,0:T(8,128)(2,1)S(1)} %get-tuple-element.76), channel_id=1, source_target_pairs={{0,3},{1,0},{2,1},{3,2},{4,67},{5,64},{6,65},{7,66},{8,11},{9,8},{... | collective-permute-start | bytes 393224 | tf_op jit(solution)/shard_map/ppermute | solution.py:345
  34.8 0.8 copy-start.12
  45.2 38.7 %all-to-all-start.1 = ((bf16[16,64,512]{2,1,0:T(8,128)(2,1)}), bf16[16,64,512]{2,1,0:T(8,128)(2,1)S(1)}, u32[]{:S(2)}, u32[]{:S(2)}) async-start(bf16[16,64,512]{2,1,0:T(8,128)(2,1)} %bitcast.19), calls=%async_computation.1 | async-start | bytes 2097152 | tf_op jit(solution)/shard_map/all_to_all | solution.py:351
  55.8 146.8 %all-gather.6.cloned.1.call-start = ((), (), s32[]{:S(2)}) async-start(), calls=%async_computation.3 | async-start | bytes 4456448 | tf_op jit(solution)/shard_map/all_gather | solution.py:401
  86.2 11.7 %collective-permute-start.6 = (bf16[256,512]{1,0:T(8,128)(2,1)S(1)}, bf16[256,512]{1,0:T(8,128)(2,1)S(1)}, u32[]{:S(2)}, u32[]{:S(2)}) collective-permute-start(bf16[256,512]{1,0:T(8,128)(2,1)S(1)} %gather_fusion.2), channel_id=1, source_target_pairs={{0,1},{1,2},{2,3},{3,0},{4,5},{5,6},{6,7},{7,4},{8,9},{9,10},{10,1... | collective-permute-start | bytes 786440 | tf_op jit(solution)/shard_map/ppermute | solution.py:54
  87.4 13.4 %collective-permute-start.5 = (bf16[256,512]{1,0:T(8,128)(2,1)S(1)}, bf16[256,512]{1,0:T(8,128)(2,1)S(1)}, u32[]{:S(2)}, u32[]{:S(2)}) collective-permute-start(bf16[256,512]{1,0:T(8,128)(2,1)S(1)} %gather_fusion.2), channel_id=1, source_target_pairs={{0,2},{1,3},{2,0},{3,1},{4,6},{5,7},{6,4},{7,5},{8,10},{9,11},{10,... | collective-permute-start | bytes 786440 | tf_op jit(solution)/shard_map/ppermute | solution.py:54
  89.2 12.9 %collective-permute-start.4 = (bf16[256,512]{1,0:T(8,128)(2,1)S(1)}, bf16[256,512]{1,0:T(8,128)(2,1)S(1)}, u32[]{:S(2)}, u32[]{:S(2)}) collective-permute-start(bf16[256,512]{1,0:T(8,128)(2,1)S(1)} %gather_fusion.2), channel_id=1, source_target_pairs={{0,3},{1,0},{2,1},{3,2},{4,7},{5,4},{6,5},{7,6},{8,11},{9,8},{10,9... | collective-permute-start | bytes 786440 | tf_op jit(solution)/shard_map/ppermute | solution.py:54
  89.4 20.0 %collective-permute-start = (bf16[256,512]{1,0:T(8,128)(2,1)S(1)}, bf16[256,512]{1,0:T(8,128)(2,1)S(1)}, u32[]{:S(2)}, u32[]{:S(2)}) collective-permute-start(bf16[256,512]{1,0:T(8,128)(2,1)S(1)} %gather_fusion.1), channel_id=1, source_target_pairs={{0,3},{1,0},{2,1},{3,2},{4,7},{5,4},{6,5},{7,6},{8,11},{9,8},{10,9... | collective-permute-start | bytes 786440 | tf_op jit(solution)/shard_map/ppermute | solution.py:54
  91.1 18.4 %collective-permute-start.2 = (bf16[256,512]{1,0:T(8,128)(2,1)S(1)}, bf16[256,512]{1,0:T(8,128)(2,1)S(1)}, u32[]{:S(2)}, u32[]{:S(2)}) collective-permute-start(bf16[256,512]{1,0:T(8,128)(2,1)S(1)} %gather_fusion.1), channel_id=1, source_target_pairs={{0,1},{1,2},{2,3},{3,0},{4,5},{5,6},{6,7},{7,4},{8,9},{9,10},{10,1... | collective-permute-start | bytes 786440 | tf_op jit(solution)/shard_map/ppermute | solution.py:54
  97.9 15.5 %collective-permute-start.1 = (bf16[256,512]{1,0:T(8,128)(2,1)S(1)}, bf16[256,512]{1,0:T(8,128)(2,1)S(1)}, u32[]{:S(2)}, u32[]{:S(2)}) collective-permute-start(bf16[256,512]{1,0:T(8,128)(2,1)S(1)} %gather_fusion.1), channel_id=1, source_target_pairs={{0,2},{1,3},{2,0},{3,1},{4,6},{5,7},{6,4},{7,5},{8,10},{9,11},{10,... | collective-permute-start | bytes 786440 | tf_op jit(solution)/shard_map/ppermute | solution.py:54
  102.3 12.5 %collective-permute-start.7 = (f32[2,128]{1,0:T(2,128)S(1)}, f32[2,128]{1,0:T(2,128)S(1)}, u32[]{:S(2)}, u32[]{:S(2)}) collective-permute-start(f32[2,128]{1,0:T(2,128)S(1)} %add_bitcast_fusion), channel_id=1, source_target_pairs={{0,4},{1,5},{2,6},{3,7},{4,0},{5,1},{6,2},{7,3},{8,12},{9,13},{10,... | collective-permute-start | bytes 3080 | tf_op jit(solution)/shard_map/ppermute | solution.py:58
  113.5 5.2 %collective-permute-start.3 = (f32[2,128]{1,0:T(2,128)S(1)}, f32[2,128]{1,0:T(2,128)S(1)}, u32[]{:S(2)}, u32[]{:S(2)}) collective-permute-start(f32[2,128]{1,0:T(2,128)S(1)} %add_bitcast_fusion.1), channel_id=1, source_target_pairs={{0,4},{1,5},{2,6},{3,7},{4,0},{5,1},{6,2},{7,3},{8,12},{9,13},{10,... | collective-permute-start | bytes 3080 | tf_op jit(solution)/shard_map/ppermute | solution.py:58
  121.2 24.3 %collective-permute-start.13 = (bf16[256,512]{1,0:T(8,128)(2,1)S(1)}, bf16[256,512]{1,0:T(8,128)(2,1)S(1)}, u32[]{:S(2)}, u32[]{:S(2)}) collective-permute-start(bf16[256,512]{1,0:T(8,128)(2,1)S(1)} %in_product.7), channel_id=1, source_target_pairs={{0,4},{1,5},{2,6},{3,7},{4,0},{5,1},{6,2},{7,3},{8,12},{9,13},{10,... | collective-permute-start | bytes 786440 | tf_op jit(solution)/shard_map/ppermute | solution.py:58
  125.1 20.5 %collective-permute-start.12 = (bf16[256,512]{1,0:T(8,128)(2,1)S(1)}, bf16[256,512]{1,0:T(8,128)(2,1)S(1)}, u32[]{:S(2)}, u32[]{:S(2)}) collective-permute-start(bf16[256,512]{1,0:T(8,128)(2,1)S(1)} %in_product.6), channel_id=1, source_target_pairs={{0,4},{1,5},{2,6},{3,7},{4,0},{5,1},{6,2},{7,3},{8,12},{9,13},{10,... | collective-permute-start | bytes 786440 | tf_op jit(solution)/shard_map/ppermute | solution.py:58
  130.5 16.7 %collective-permute-start.14 = (bf16[32,2048]{1,0:T(8,128)(2,1)}, bf16[32,2048]{1,0:T(8,128)(2,1)S(1)}, u32[]{:S(2)}, u32[]{:S(2)}) collective-permute-start(bf16[32,2048]{1,0:T(8,128)(2,1)} %get-tuple-element.90), channel_id=1, source_target_pairs={{0,0},{1,16},{2,32},{3,48},{4,4},{5,20},{6,36},{7,52},{8,8},{9,24}... | collective-permute-start | bytes 393224 | tf_op jit(solution)/shard_map/ppermute | solution.py:381
  132.5 14.8 %collective-permute-start.15 = (bf16[32,2048]{1,0:T(8,128)(2,1)}, bf16[32,2048]{1,0:T(8,128)(2,1)S(1)}, u32[]{:S(2)}, u32[]{:S(2)}) collective-permute-start(bf16[32,2048]{1,0:T(8,128)(2,1)} %get-tuple-element.91), channel_id=1, source_target_pairs={{0,4},{1,20},{2,36},{3,52},{4,0},{5,16},{6,32},{7,48},{8,12},{9,28... | collective-permute-start | bytes 393224 | tf_op jit(solution)/shard_map/ppermute | solution.py:381
  141.6 4.1 %copy-start.7 = (bf16[128,3,512]{2,0,1:T(8,128)(2,1)S(1)}, bf16[128,3,512]{2,0,1:T(8,128)(2,1)}, u32[]{:S(2)}) copy-start(bf16[128,3,512]{2,0,1:T(8,128)(2,1)} %param.29) | copy-start | bytes 1179652
  141.6 4.1 %copy-start.8 = (bf16[288,512]{1,0:T(8,128)(2,1)S(1)}, bf16[288,512]{1,0:T(8,128)(2,1)}, u32[]{:S(2)}) copy-start(bf16[288,512]{1,0:T(8,128)(2,1)} %refs_7_.1) | copy-start | bytes 884740
  141.6 4.1 %copy-start.9 = (f32[4,512]{1,0:T(4,128)S(1)}, f32[4,512]{1,0:T(4,128)}, u32[]{:S(2)}) copy-start(f32[4,512]{1,0:T(4,128)} %refs_5_.1) | copy-start | bytes 24580
  141.6 4.1 %copy-start.10 = (f32[512]{0:T(512)S(1)}, f32[512]{0:T(512)}, u32[]{:S(2)}) copy-start(f32[512]{0:T(512)} %param.32) | copy-start | bytes 6148
  144.7 0.8 copy-start.4
  145.5 23.4 %copy-start.5 = (bf16[512,512]{1,0:T(8,128)(2,1)S(1)}, bf16[512,512]{1,0:T(8,128)(2,1)}, u32[]{:S(2)}) copy-start(bf16[512,512]{1,0:T(8,128)(2,1)} %copy-done.4) | copy-start | bytes 1572868
  147.2 27.7 %copy-start.21 = (f32[512]{0:T(512)S(1)}, f32[512]{0:T(512)}, u32[]{:S(2)}) copy-start(f32[512]{0:T(512)} %param.35) | copy-start | bytes 6148
  147.3 6.9 %collective-permute-start.16 = (bf16[128,288]{1,0:T(8,128)(2,1)S(1)}, bf16[128,288]{1,0:T(8,128)(2,1)S(1)}, u32[]{:S(2)}, u32[]{:S(2)}) collective-permute-start(bf16[128,288]{1,0:T(8,128)(2,1)S(1)} %get-tuple-element.139), channel_id=1, source_target_pairs={{0,3},{1,0},{2,1},{3,2},{4,7},{5,4},{6,5},{7,6},{8,11},{9,8},{10,9... | collective-permute-start | bytes 221192 | tf_op jit(solution)/shard_map/ppermute | solution.py:54
  147.4 6.9 %collective-permute-start.17 = (bf16[128,288]{1,0:T(8,128)(2,1)S(1)}, bf16[128,288]{1,0:T(8,128)(2,1)S(1)}, u32[]{:S(2)}, u32[]{:S(2)}) collective-permute-start(bf16[128,288]{1,0:T(8,128)(2,1)S(1)} %get-tuple-element.141), channel_id=1, source_target_pairs={{0,2},{1,3},{2,0},{3,1},{4,6},{5,7},{6,4},{7,5},{8,10},{9,11},{10,... | collective-permute-start | bytes 221192 | tf_op jit(solution)/shard_map/ppermute | solution.py:54
  148.8 6.3 %collective-permute-start.18 = (bf16[128,288]{1,0:T(8,128)(2,1)S(1)}, bf16[128,288]{1,0:T(8,128)(2,1)S(1)}, u32[]{:S(2)}, u32[]{:S(2)}) collective-permute-start(bf16[128,288]{1,0:T(8,128)(2,1)S(1)} %get-tuple-element.140), channel_id=1, source_target_pairs={{0,1},{1,2},{2,3},{3,0},{4,5},{5,6},{6,7},{7,4},{8,9},{9,10},{10,1... | collective-permute-start | bytes 221192 | tf_op jit(solution)/shard_map/ppermute | solution.py:54
  154.2 0.9 copy-start.16
  154.2 1.6 copy-start.17
  155.1 0.7 copy-start.18
  155.8 6.4 %collective-permute-start.19 = (bf16[128,288]{1,0:T(8,128)(2,1)}, bf16[128,288]{1,0:T(8,128)(2,1)}, u32[]{:S(2)}, u32[]{:S(2)}) collective-permute-start(bf16[128,288]{1,0:T(8,128)(2,1)} %fusion.40), channel_id=1, source_target_pairs={{0,4},{1,5},{2,6},{3,7},{4,0},{5,1},{6,2},{7,3},{8,12},{9,13},{10,... | collective-permute-start | bytes 221192 | tf_op jit(solution)/shard_map/ppermute | solution.py:58
  164.9 6.4 %collective-permute-start.20 = (bf16[128,288]{1,0:T(8,128)(2,1)}, bf16[128,288]{1,0:T(8,128)(2,1)S(1)}, u32[]{:S(2)}, u32[]{:S(2)}) collective-permute-start(bf16[128,288]{1,0:T(8,128)(2,1)} %add_convert_fusion.1), channel_id=1, source_target_pairs={{0,3},{1,0},{2,1},{3,2},{4,7},{5,4},{6,5},{7,6},{8,11},{9,8},{10,9... | collective-permute-start | bytes 221192 | tf_op jit(solution)/shard_map/ppermute | solution.py:54
  165.9 6.7 %collective-permute-start.21 = (bf16[128,288]{1,0:T(8,128)(2,1)}, bf16[128,288]{1,0:T(8,128)(2,1)S(1)}, u32[]{:S(2)}, u32[]{:S(2)}) collective-permute-start(bf16[128,288]{1,0:T(8,128)(2,1)} %add_convert_fusion.1), channel_id=1, source_target_pairs={{0,2},{1,3},{2,0},{3,1},{4,6},{5,7},{6,4},{7,5},{8,10},{9,11},{10,... | collective-permute-start | bytes 221192 | tf_op jit(solution)/shard_map/ppermute | solution.py:54
  168.8 4.8 %collective-permute-start.22 = (bf16[128,288]{1,0:T(8,128)(2,1)}, bf16[128,288]{1,0:T(8,128)(2,1)S(1)}, u32[]{:S(2)}, u32[]{:S(2)}) collective-permute-start(bf16[128,288]{1,0:T(8,128)(2,1)} %add_convert_fusion.1), channel_id=1, source_target_pairs={{0,1},{1,2},{2,3},{3,0},{4,5},{5,6},{6,7},{7,4},{8,9},{9,10},{10,1... | collective-permute-start | bytes 221192 | tf_op jit(solution)/shard_map/ppermute | solution.py:54
  168.9 20.6 %collective-permute-start.23 = (bf16[512,512]{1,0:T(8,128)(2,1)S(1)}, bf16[512,512]{1,0:T(8,128)(2,1)S(1)}, u32[]{:S(2)}, u32[]{:S(2)}) collective-permute-start(bf16[512,512]{1,0:T(8,128)(2,1)S(1)} %copy-done.5), channel_id=1, source_target_pairs={{0,4},{1,5},{2,6},{3,7},{4,0},{5,1},{6,2},{7,3},{8,12},{9,13},{10,... | collective-permute-start | bytes 1572872 | tf_op jit(solution)/shard_map/ppermute | solution.py:58
  174.7 2.3 copy-start.11
  177.0 12.7 %copy-start.20 = (f32[512]{0:T(512)S(1)}, f32[512]{0:T(512)}, u32[]{:S(2)}) copy-start(f32[512]{0:T(512)} %param.37) | copy-start | bytes 6148
  190.1 9.1 %collective-permute-start.24 = (bf16[256,512]{1,0:T(8,128)(2,1)S(1)}, bf16[256,512]{1,0:T(8,128)(2,1)S(1)}, u32[]{:S(2)}, u32[]{:S(2)}) collective-permute-start(bf16[256,512]{1,0:T(8,128)(2,1)S(1)} %pad_maximum_fusion.3.refs_0_), channel_id=1, source_target_pairs={{0,3},{1,0},{2,1},{3,2},{4,7},{5,4},{6,5},{7,6},{8,11},{9,8},{10,9... | collective-permute-start | bytes 786440 | tf_op jit(solution)/shard_map/ppermute | solution.py:54
  193.6 7.9 %collective-permute-start.25 = (bf16[256,512]{1,0:T(8,128)(2,1)S(1)}, bf16[256,512]{1,0:T(8,128)(2,1)S(1)}, u32[]{:S(2)}, u32[]{:S(2)}) collective-permute-start(bf16[256,512]{1,0:T(8,128)(2,1)S(1)} %pad_maximum_fusion.3.refs_0_), channel_id=1, source_target_pairs={{0,2},{1,3},{2,0},{3,1},{4,6},{5,7},{6,4},{7,5},{8,10},{9,11},{10,... | collective-permute-start | bytes 786440 | tf_op jit(solution)/shard_map/ppermute | solution.py:54
  194.4 7.3 %collective-permute-start.26 = (bf16[256,512]{1,0:T(8,128)(2,1)S(1)}, bf16[256,512]{1,0:T(8,128)(2,1)S(1)}, u32[]{:S(2)}, u32[]{:S(2)}) collective-permute-start(bf16[256,512]{1,0:T(8,128)(2,1)S(1)} %pad_maximum_fusion.3.refs_0_), channel_id=1, source_target_pairs={{0,1},{1,2},{2,3},{3,0},{4,5},{5,6},{6,7},{7,4},{8,9},{9,10},{10,1... | collective-permute-start | bytes 786440 | tf_op jit(solution)/shard_map/ppermute | solution.py:54
  196.6 11.5 %collective-permute-start.27 = (bf16[256,512]{1,0:T(8,128)(2,1)S(1)}, bf16[256,512]{1,0:T(8,128)(2,1)S(1)}, u32[]{:S(2)}, u32[]{:S(2)}) collective-permute-start(bf16[256,512]{1,0:T(8,128)(2,1)S(1)} %pad_maximum_fusion.4.refs_4_.refs_0_), channel_id=1, source_target_pairs={{0,3},{1,0},{2,1},{3,2},{4,7},{5,4},{6,5},{7,6},{8,11},{9,8},{10,9... | collective-permute-start | bytes 786440 | tf_op jit(solution)/shard_map/ppermute | solution.py:54
  196.7 11.4 %collective-permute-start.28 = (bf16[256,512]{1,0:T(8,128)(2,1)S(1)}, bf16[256,512]{1,0:T(8,128)(2,1)S(1)}, u32[]{:S(2)}, u32[]{:S(2)}) collective-permute-start(bf16[256,512]{1,0:T(8,128)(2,1)S(1)} %pad_maximum_fusion.4.refs_4_.refs_0_), channel_id=1, source_target_pairs={{0,2},{1,3},{2,0},{3,1},{4,6},{5,7},{6,4},{7,5},{8,10},{9,11},{10,... | collective-permute-start | bytes 786440 | tf_op jit(solution)/shard_map/ppermute | solution.py:54
  199.3 8.8 %collective-permute-start.29 = (bf16[256,512]{1,0:T(8,128)(2,1)S(1)}, bf16[256,512]{1,0:T(8,128)(2,1)S(1)}, u32[]{:S(2)}, u32[]{:S(2)}) collective-permute-start(bf16[256,512]{1,0:T(8,128)(2,1)S(1)} %pad_maximum_fusion.4.refs_4_.refs_0_), channel_id=1, source_target_pairs={{0,1},{1,2},{2,3},{3,0},{4,5},{5,6},{6,7},{7,4},{8,9},{9,10},{10,1... | collective-permute-start | bytes 786440 | tf_op jit(solution)/shard_map/ppermute | solution.py:54
  205.3 11.3 %collective-permute-start.30 = (bf16[256,512]{1,0:T(8,128)(2,1)S(1)}, bf16[256,512]{1,0:T(8,128)(2,1)S(1)}, u32[]{:S(2)}, u32[]{:S(2)}) collective-permute-start(bf16[256,512]{1,0:T(8,128)(2,1)S(1)} %out_product.4), channel_id=1, source_target_pairs={{0,4},{1,5},{2,6},{3,7},{4,0},{5,1},{6,2},{7,3},{8,12},{9,13},{10,... | collective-permute-start | bytes 786440 | tf_op jit(solution)/shard_map/ppermute | solution.py:58
  210.8 10.2 %collective-permute-start.31 = (bf16[256,512]{1,0:T(8,128)(2,1)S(1)}, bf16[256,512]{1,0:T(8,128)(2,1)S(1)}, u32[]{:S(2)}, u32[]{:S(2)}) collective-permute-start(bf16[256,512]{1,0:T(8,128)(2,1)S(1)} %out_product.5), channel_id=1, source_target_pairs={{0,4},{1,5},{2,6},{3,7},{4,0},{5,1},{6,2},{7,3},{8,12},{9,13},{10,... | collective-permute-start | bytes 786440 | tf_op jit(solution)/shard_map/ppermute | solution.py:58
Sparse Core Ops, SparseCore 0:
  35.7 69.8 all-gather.3
  164.2 38.4 all-gather.5
